TPU v7x, 32 devices: a whole 2x2x4 slice. The times are simulated.
32 devices in a mesh: head: 4 (over x, core), ctx: 8 (over z, y).
Axes of the slice: x: 2, y: 2, z: 4, core: 2. Of those that a mesh axis runs over, the one named last changes fastest.
Arguments:
- query: bfloat16 [8, 512, 512], P('ctx', 'head'), may hold values from -36 to 36
- key: bfloat16 [8, 512, 512], P('ctx', 'head'), may hold values from -36 to 36
- value: bfloat16 [8, 512, 512], P('ctx', 'head'), may hold values from -6 to 6
- resid_in: bfloat16 [8, 512, 1024], P('ctx', 'head'), may hold values from -6 to 6
- out_grad: bfloat16 [8, 512, 1024], P('ctx', 'head'), may hold values from -6 to 6
- out_weight: bfloat16 [512, 1024], replicated, may hold values from -0.25 to 0.25
- conv_kernel: bfloat16 [31, 1024], replicated, may hold values from -1 to 1
- frame_lengths: int32 [8], replicated, may hold values from 256 to 512, as said below
Outputs:
- d_resid: bfloat16 [8, 512, 1024], P('ctx', None, 'head')
- d_query: bfloat16 [8, 512, 512], P('ctx', None, 'head')
- d_key: bfloat16 [8, 512, 512], P('ctx', None, 'head')
- d_value: bfloat16 [8, 512, 512], P('ctx', None, 'head')
Inputs may be any that keep to these rules, and one draw needn't show every extreme that they name: Block b holds audio in its first frame_lengths[b] frames; at least one block is full.
All inputs are finite; a program needn't handle non-finite values.
Results may differ from a plain program's by a relative error of at most 0.0086.
Values may be sent and summed in bfloat16 or wider, within the bound.
No kernel may reach another device: no remote copies, remote signals or barrier semaphores. Data moves between devices by JAX's collectives and lax.ppermute only.
A program may use at most 128 MiB of HBM per device.

v0:
```python
import jax
import jax.numpy as jnp
from jax import lax
from jax.sharding import PartitionSpec as P

HEAD_DIM = 64
KERNEL = 31
REACH = 2


def padded(cells, sides, width):
    for axis, dim in sides:
        count = lax.axis_size(axis)
        ends = count - 1
        head = lax.slice_in_dim(cells, 0, width, axis=dim)
        tail = lax.slice_in_dim(cells, cells.shape[dim] - width, cells.shape[dim], axis=dim)
        cells = jnp.concatenate(
            [
                lax.ppermute(tail, axis, [(i, (i + 1) % count) for i in range(ends)]),
                cells,
                lax.ppermute(head, axis, [((i + 1) % count, i) for i in range(ends)]),
            ],
            axis=dim,
        )
    return cells


def shifted(value, axis, steps):
    count = lax.axis_size(axis)
    first, last = (max(0, -steps), min(count, count - steps))
    return lax.ppermute(value, axis, [(source, source + steps) for source in range(first, last)])


def swish_slope(before):
    logistic = jax.nn.sigmoid(before)
    return logistic * (1.0 + before * (1.0 - logistic))


def conv_backward(resid_wide, grad_wide, weights_here, frames_here):
    margin = (KERNEL - 1) // 2
    channels = resid_wide.shape[1]
    extent = frames_here + 2 * margin
    conv_pre = jnp.zeros((extent, channels), jnp.float32)
    for offset in range(KERNEL):
        conv_pre = conv_pre + weights_here[offset] * resid_wide[offset : offset + extent]
    conv_grad = grad_wide[margin : margin + extent] * swish_slope(conv_pre)
    total = grad_wide[2 * margin : 2 * margin + frames_here]
    for offset in range(KERNEL):
        start_at = 2 * margin - offset
        total = total + weights_here[offset] * conv_grad[start_at : start_at + frames_here]
    return total.astype(jnp.bfloat16)


def on_device(query, key, value, resid_in, out_grad, out_weight, conv_kernel, frame_lengths):
    margin = (KERNEL - 1) // 2
    reach_rows = 2 * margin
    head_place = lax.axis_index("head")
    moved = (
        lax.all_to_all(query, "head", split_axis=2, concat_axis=1, tiled=True),
        lax.all_to_all(key, "head", split_axis=2, concat_axis=1, tiled=True),
        lax.all_to_all(value, "head", split_axis=2, concat_axis=1, tiled=True),
        lax.all_to_all(resid_in, "head", split_axis=2, concat_axis=1, tiled=True),
        lax.all_to_all(out_grad, "head", split_axis=2, concat_axis=1, tiled=True),
    )
    query_rows = moved[0][0]
    key_rows = moved[1][0]
    value_rows = moved[2][0]
    resid_rows = moved[3][0]
    grad_rows = moved[4][0]
    block_frames = resid_rows.shape[0]
    channels = resid_rows.shape[1]
    weights_here = lax.dynamic_slice_in_dim(conv_kernel, head_place * channels, channels, 1).astype(
        jnp.float32
    )
    resid_ext, grad_ext = (
        padded(resid_rows, (("ctx", 0),), reach_rows),
        padded(grad_rows, (("ctx", 0),), reach_rows),
    )
    d_resid = conv_backward(
        resid_ext.astype(jnp.float32), grad_ext.astype(jnp.float32), weights_here, block_frames
    )
    width_cols = query_rows.shape[1]
    weight_rows = lax.dynamic_slice_in_dim(out_weight, head_place * width_cols, width_cols, 0)
    head_sum = lax.dot_general(
        lax.all_gather(d_resid, "head", axis=1, tiled=True),
        weight_rows,
        (((1,), (1,)), ((), ())),
        preferred_element_type=jnp.float32,
    )
    head_grad = head_sum.astype(jnp.bfloat16)
    d_resid_out = d_resid[None]
    frames_here = query_rows.shape[0]
    width_here = query_rows.shape[1]
    heads_here = width_here // HEAD_DIM
    scale = HEAD_DIM ** (-0.5)
    query_heads = query_rows.reshape(frames_here, heads_here, HEAD_DIM)
    grad_heads = head_grad.reshape(frames_here, heads_here, HEAD_DIM)
    block_place = lax.axis_index("ctx")
    block_count = frame_lengths.shape[0]
    window = REACH * frames_here
    local_rows = jnp.arange(frames_here, dtype=jnp.int32)
    query_place = block_place * frames_here + local_rows

    def live_mask(offset):
        neighbour = block_place + offset
        key_place = neighbour * frames_here + local_rows
        limit = frame_lengths[jnp.clip(neighbour, 0, block_count - 1)]
        inside = (neighbour >= 0) & (neighbour < block_count)
        near = jnp.abs(query_place[:, None] - key_place[None, :]) <= window
        return near & (local_rows[None, :] < limit) & inside

    fetched = {0: (key_rows, value_rows)}
    for direction in (1, -1):
        last_key, last_value = (key_rows, value_rows)
        for distance in range(1, REACH + 1):
            send_key = last_key
            send_value = last_value
            last_key, last_value = shifted((send_key, send_value), "ctx", direction)
            fetched[-direction * distance] = (last_key, last_value)
    order = [0] + [offset for offset in range(-REACH, REACH + 1) if offset != 0]

    def block_logits(offset):
        keys_now = fetched[offset][0].reshape(frames_here, heads_here, HEAD_DIM)
        raw = (
            jnp.einsum("qhd,khd->hqk", query_heads, keys_now, preferred_element_type=jnp.float32)
            * scale
        )
        return jnp.where(live_mask(offset)[None], raw, -jnp.inf)

    def block_slopes(offset):
        values_now = fetched[offset][1].reshape(frames_here, heads_here, HEAD_DIM)
        return jnp.einsum(
            "qhd,khd->hqk", grad_heads, values_now, preferred_element_type=jnp.float32
        )

    for offset in order:
        logits = block_logits(offset)
        slopes = block_slopes(offset)
        if offset == 0:
            highest = jnp.max(logits, axis=2)
            scaled = jnp.exp(logits - highest[:, :, None])
            mass = jnp.sum(scaled, axis=2)
            weighted = jnp.sum(scaled * slopes, axis=2)
        else:
            fresh = jnp.maximum(highest, jnp.max(logits, axis=2))
            factor = jnp.exp(highest - fresh)
            scaled = jnp.exp(logits - fresh[:, :, None])
            mass = mass * factor + jnp.sum(scaled, axis=2)
            weighted = weighted * factor + jnp.sum(scaled * slopes, axis=2)
            highest = fresh
    log_total = highest + jnp.log(mass)
    delta = weighted / mass
    query_grad = jnp.zeros((frames_here, heads_here, HEAD_DIM), jnp.float32)
    for offset in order:
        keys_now = fetched[offset][0].reshape(frames_here, heads_here, HEAD_DIM)
        logits = block_logits(offset)
        probs = jnp.exp(logits - log_total[:, :, None])
        slopes = block_slopes(offset)
        dlogits = (probs * (slopes - delta[:, :, None])).astype(jnp.bfloat16)
        probs_low = probs.astype(jnp.bfloat16)
        query_grad = (
            query_grad
            + jnp.einsum("hqk,khd->qhd", dlogits, keys_now, preferred_element_type=jnp.float32)
            * scale
        )
        key_part = (
            (
                jnp.einsum("hqk,qhd->khd", dlogits, query_heads, preferred_element_type=jnp.float32)
                * scale
            )
            .astype(jnp.bfloat16)
            .reshape(frames_here, width_here)
        )
        value_part = (
            jnp.einsum("hqk,qhd->khd", probs_low, grad_heads, preferred_element_type=jnp.float32)
            .astype(jnp.bfloat16)
            .reshape(frames_here, width_here)
        )
        if offset == 0:
            key_total = key_part.astype(jnp.float32)
            value_total = value_part.astype(jnp.float32)
        else:
            back_key, back_value = shifted((key_part, value_part), "ctx", offset)
            key_total = key_total + back_key.astype(jnp.float32)
            value_total = value_total + back_value.astype(jnp.float32)
    return (
        d_resid_out,
        query_grad.reshape(frames_here, width_here).astype(jnp.bfloat16)[None],
        key_total.astype(jnp.bfloat16)[None],
        value_total.astype(jnp.bfloat16)[None],
    )


def solution(mesh):
    in_specs = (
        P("ctx", "head", None),
        P("ctx", "head", None),
        P("ctx", "head", None),
        P("ctx", "head", None),
        P("ctx", "head", None),
        P(),
        P(),
        P(),
    )
    out_specs = (
        P("ctx", None, "head"),
        P("ctx", None, "head"),
        P("ctx", None, "head"),
        P("ctx", None, "head"),
    )
    return jax.shard_map(
        on_device, mesh=mesh, in_specs=in_specs, out_specs=out_specs, check_vma=False
    )
```

profile of v0, /device:TPU:0, one launch (start us, length us, event | category | flops | bytes accessed | tf_op | source)
XLA Modules:
  0.0 203.7 jit_solution(15611372679468310429)
XLA Ops:
  7.2 1.2 copy.117
  8.9 1.4 reduce.3
  11.0 4.2 %all-to-all-start.2 = ((bf16[4,2,8192]{2,1,0:T(2,128)(2,1)}), bf16[4,2,8192]{2,1,0:T(2,128)(2,1)S(1)}, u32[]{:S(2)}, u32[]{:S(2)}) async-start(bf16[4,2,8192]{2,1,0:T(2,128)(2,1)} %reshape.507), calls=%async_computation.2 | async-start | bytes 262144 | tf_op jit(solution)/shard_map/all_to_all | solution.py:59
  15.2 1.5 fusion.111
  17.4 1.3 iota_compare_fusion.2
  18.7 1.3 iota_compare_fusion
  20.0 3.0 %fusion.33 = (pred[512,512]{0,1:T(8,128)(4,1)}, pred[512,512]{0,1:T(8,128)(4,1)}, pred[512,512]{0,1:T(8,128)(4,1)}, pred[512,512]{0,1:T(8,128)(4,1)}, pred[512,512]{0,1:T(8,128)(4,1)}) fusion(s32[512]{0:T(512)S(1)} %get-tuple-element.108, s32[512]{0:T(512)S(1)} %iota_add_fusion.4, pred[512]{0:T(512)(128)(4,1)S(1)} %get-tuple-element.106, pred[]{:T(512)S(6)} %and.169, ...), kind=kLoop, calls=%fused_computation.72 | loop fusion | flops 6553600 | bytes 1323525 | tf_op jit(solution)/shard_map/and | solution.py:110
  23.1 1.4 reduce.2
  25.4 1.4 reduce.4
  27.5 3.4 %all-to-all-start.3 = ((bf16[4,2,8192]{2,1,0:T(2,128)(2,1)}), bf16[4,2,8192]{2,1,0:T(2,128)(2,1)S(1)}, u32[]{:S(2)}, u32[]{:S(2)}) async-start(bf16[4,2,8192]{2,1,0:T(2,128)(2,1)} %reshape.503), calls=%async_computation.3 | async-start | bytes 262144 | tf_op jit(solution)/shard_map/all_to_all | solution.py:60
  31.6 3.9 %all-to-all-done.3 = bf16[4,2,8192]{2,1,0:T(2,128)(2,1)S(1)} async-done(((bf16[4,2,8192]{2,1,0:T(2,128)(2,1)}), bf16[4,2,8192]{2,1,0:T(2,128)(2,1)S(1)}, u32[]{:S(2)}, u32[]{:S(2)}) %all-to-all-start.3) | async-done | bytes 131104 | tf_op jit(solution)/shard_map/all_to_all | solution.py:60
  35.5 3.3 %all-to-all-start.4 = ((bf16[4,2,8192]{2,1,0:T(2,128)(2,1)}), bf16[4,2,8192]{2,1,0:T(2,128)(2,1)S(1)}, u32[]{:S(2)}, u32[]{:S(2)}) async-start(bf16[4,2,8192]{2,1,0:T(2,128)(2,1)} %reshape.505), calls=%async_computation.4 | async-start | bytes 262144 | tf_op jit(solution)/shard_map/all_to_all | solution.py:61
  39.3 2.2 %reduce.1 = bf16[1024,128]{1,0:T(8,128)(2,1)S(1)} reduce(bf16[1024,1,128]{2,1,0:T(2,128)(2,1)S(1)} %bitcast.177, bf16[]{:T(256)} %broadcast.279), dimensions={1}, to_apply=%bitcast.110.reduce_sub_computation | reduce | bytes 524290
  42.7 2.2 %reduce = bf16[1024,128]{1,0:T(8,128)(2,1)S(1)} reduce(bf16[1024,1,128]{2,1,0:T(2,128)(2,1)S(1)} %bitcast.176, bf16[]{:T(256)} %broadcast.279), dimensions={1}, to_apply=%bitcast.108.reduce_sub_computation | reduce | bytes 524290
  45.7 3.4 %all-to-all-start.1 = ((bf16[4,2,16384]{2,1,0:T(2,128)(2,1)}), bf16[4,2,16384]{2,1,0:T(2,128)(2,1)S(1)}, u32[]{:S(2)}, u32[]{:S(2)}) async-start(bf16[4,2,16384]{2,1,0:T(2,128)(2,1)} %reshape.501), calls=%async_computation.1 | async-start | bytes 524288 | tf_op jit(solution)/shard_map/all_to_all | solution.py:62
  50.2 1.3 collective-permute-start.6
  51.5 5.3 %collective-permute-start.4 = (bf16[512,128]{1,0:T(8,128)(2,1)}, bf16[512,128]{1,0:T(8,128)(2,1)}, u32[]{:S(2)}, u32[]{:S(2)}) collective-permute-start(bf16[512,128]{1,0:T(8,128)(2,1)} %bitcast.40), channel_id=1, source_target_pairs={{0,1},{1,2},{2,3},{3,4},{4,5},{5,6},{6,7},{8,9},{9,10},{10,11},{11... | collective-permute-start | bytes 393224 | tf_op jit(solution)/shard_map/ppermute | solution.py:31
  58.1 1.3 collective-permute-start.10
  59.4 3.4 %all-to-all-start = ((bf16[4,2,16384]{2,1,0:T(2,128)(2,1)}), bf16[4,2,16384]{2,1,0:T(2,128)(2,1)S(1)}, u32[]{:S(2)}, u32[]{:S(2)}) async-start(bf16[4,2,16384]{2,1,0:T(2,128)(2,1)} %reshape.499), calls=%async_computation | async-start | bytes 524288 | tf_op jit(solution)/shard_map/all_to_all | solution.py:63
  63.3 4.8 %collective-permute-start.2 = (bf16[30,256]{1,0:T(8,128)(2,1)S(1)}, bf16[30,256]{1,0:T(8,128)(2,1)S(1)}, u32[]{:S(2)}, u32[]{:S(2)}) collective-permute-start(bf16[30,256]{1,0:T(8,128)(2,1)S(1)} %get-tuple-element.36), channel_id=1, source_target_pairs={{0,1},{1,2},{2,3},{3,4},{4,5},{5,6},{6,7},{8,9},{9,10},{10,11},{11... | collective-permute-start | bytes 46088 | tf_op jit(solution)/shard_map/ppermute | solution.py:19
  68.1 1.3 collective-permute-start.3
  70.0 5.4 %collective-permute-start = (bf16[30,256]{1,0:T(8,128)(2,1)S(1)}, bf16[30,256]{1,0:T(8,128)(2,1)S(1)}, u32[]{:S(2)}, u32[]{:S(2)}) collective-permute-start(bf16[30,256]{1,0:T(8,128)(2,1)S(1)} %get-tuple-element.38), channel_id=1, source_target_pairs={{0,1},{1,2},{2,3},{3,4},{4,5},{5,6},{6,7},{8,9},{9,10},{10,11},{11... | collective-permute-start | bytes 46088 | tf_op jit(solution)/shard_map/ppermute | solution.py:19
  75.4 1.3 collective-permute-start.1
  76.8 6.1 %collective-permute-start.8 = (bf16[512,128]{1,0:T(8,128)(2,1)}, bf16[512,128]{1,0:T(8,128)(2,1)}, u32[]{:S(2)}, u32[]{:S(2)}) collective-permute-start(bf16[512,128]{1,0:T(8,128)(2,1)} %bitcast.50), channel_id=1, source_target_pairs={{0,1},{1,2},{2,3},{3,4},{4,5},{5,6},{6,7},{8,9},{9,10},{10,11},{11... | collective-permute-start | bytes 393224 | tf_op jit(solution)/shard_map/ppermute | solution.py:31
  83.0 2.4 %slice_multiply_fusion.31 = f32[542,256]{1,0:T(8,128)S(1)} fusion(f32[572,256]{1,0:T(8,128)S(1)} %maximum_convert_fusion, f32[572,256]{1,0:T(8,128)S(1)} %maximum_convert_fusion.1, f32[256]{0:T(256)S(1)} %bitcast.221, f32[256]{0:T(256)S(1)} %bitcast.223, f32[256]{0:T(256)S(1)} %bitcast.225, f32[256]{0:T(256)S(1)} %bitcast.227, f32[256]{0:T(256)S(1)} %bitcast.229, ...), kind=kLoop, calls=%fused_computation.140 | loop fusion | flops 9573888 | bytes 18347008 | tf_op jit(solution)/shard_map/mul | solution.py:46
  85.4 2.8 %fusion.71 = bf16[512,256]{1,0:T(8,128)(2,1)} fusion(f32[542,256]{1,0:T(8,128)S(1)} %slice_multiply_fusion.31, f32[572,256]{1,0:T(8,128)S(1)} %maximum_convert_fusion, f32[256]{0:T(256)S(1)} %bitcast.222, f32[256]{0:T(256)S(1)} %bitcast.224, f32[256]{0:T(256)S(1)} %bitcast.226, f32[256]{0:T(256)S(1)} %bitcast.228, f32[256]{0:T(256)S(1)} %bitcast.230, ...), kind=kLoop, calls=%fused_computation.143 | loop fusion | flops 8257536 | bytes 17071104 | tf_op jit(solution)/shard_map/convert_element_type | solution.py:51
  88.2 1.6 fusion.115
  91.0 1.3 collective-permute-start.7
  92.3 1.7 copy.123
  94.0 5.8 %collective-permute-start.5 = (bf16[512,128]{1,0:T(8,128)(2,1)}, bf16[512,128]{1,0:T(8,128)(2,1)}, u32[]{:S(2)}, u32[]{:S(2)}) collective-permute-start(bf16[512,128]{1,0:T(8,128)(2,1)} %collective-permute-done.4), channel_id=1, source_target_pairs={{0,1},{1,2},{2,3},{3,4},{4,5},{5,6},{6,7},{8,9},{9,10},{10,11},{11... | collective-permute-start | bytes 393224 | tf_op jit(solution)/shard_map/ppermute | solution.py:31
  99.8 1.3 collective-permute-start.11
  101.1 5.5 %collective-permute-start.9 = (bf16[512,128]{1,0:T(8,128)(2,1)}, bf16[512,128]{1,0:T(8,128)(2,1)}, u32[]{:S(2)}, u32[]{:S(2)}) collective-permute-start(bf16[512,128]{1,0:T(8,128)(2,1)} %collective-permute-done.8), channel_id=1, source_target_pairs={{0,1},{1,2},{2,3},{3,4},{4,5},{5,6},{6,7},{8,9},{9,10},{10,11},{11... | collective-permute-start | bytes 393224 | tf_op jit(solution)/shard_map/ppermute | solution.py:31
  106.6 3.5 %fusion.113 = (f32[2,512]{1,0:T(2,128)}, f32[2,512,512]{1,2,0:T(8,128)}) fusion(bf16[512,2,64]{0,2,1:T(8,128)(2,1)S(1)} %reshape_squeeze.12, bf16[512,2,64]{0,2,1:T(8,128)(2,1)S(1)} %bitcast.213, pred[512,512]{0,1:T(8,128)(4,1)} %get-tuple-element.78), kind=kOutput, calls=%fused_computation.237 | convolution fusion | flops 68680704 | bytes 2625536 | tf_op jit(solution)/shard_map/qhd,khd->hqk/dot_general | solution.py:125
  110.1 2.5 %fusion.114 = (f32[2,512]{1,0:T(2,128)}, f32[2,512,512]{1,2,0:T(8,128)}) fusion(bf16[512,2,64]{0,2,1:T(8,128)(2,1)S(1)} %reshape_squeeze.12, bf16[512,2,64]{0,2,1:T(8,128)(2,1)S(1)} %bitcast.217, pred[512,512]{0,1:T(8,128)(4,1)S(1)} %copy-done.27), kind=kOutput, calls=%fused_computation.238 | convolution fusion | flops 68680704 | bytes 2625536 | tf_op jit(solution)/shard_map/qhd,khd->hqk/dot_general | solution.py:125
  112.6 1.7 copy.131
  114.2 1.7 copy.130
  116.9 1.7 copy.122
  118.7 1.7 copy.132
  120.3 1.7 copy.129
  122.0 3.0 %fusion.116 = (f32[2,512]{1,0:T(2,128)S(1)}, f32[2,512,512]{1,2,0:T(8,128)}) fusion(bf16[512,2,64]{0,2,1:T(8,128)(2,1)S(1)} %reshape_squeeze.12, bf16[512,2,64]{0,2,1:T(8,128)(2,1)} %bitcast.215, pred[512,512]{0,1:T(8,128)(4,1)} %get-tuple-element.76), kind=kOutput, calls=%fused_computation.240 | convolution fusion | flops 68680704 | bytes 2625536 | tf_op jit(solution)/shard_map/qhd,khd->hqk/dot_general | solution.py:125
  125.0 2.0 fusion.112
  127.1 1.7 convolution_convert_fusion.5
  136.3 1.1 convolution_convert_fusion.2
  138.6 1.1 convolution_convert_fusion
  139.7 1.2 fusion.12
  140.9 4.3 %multiply_convert_fusion = (bf16[2,512,512]{1,2,0:T(8,128)(2,1)}, bf16[2,512,512]{1,2,0:T(8,128)(2,1)}, bf16[2,512,512]{1,2,0:T(8,128)(2,1)}, bf16[2,512,512]{1,2,0:T(8,128)(2,1)S(1)}, bf16[2,512,512]{1,2,0:T(8,128)(2,1)}) fusion(f32[2,512,512]{1,2,0:T(8,128)S(1)} %get-tuple-element.96, f32[2,512,512]{1,2,0:T(8,128)S(1)} %copy-done.4, ...), kind=kLoop, calls=%fused_computation | loop fusion | flops 10485760 | bytes 26222592 | tf_op jit(solution)/shard_map/convert_element_type | solution.py:159
  151.7 1.7 copy.147
  153.4 2.3 %fusion.15 = bf16[2,512,64]{1,2,0:T(8,128)(2,1)} fusion(bf16[2,512,512]{1,2,0:T(8,128)(2,1)} %get-tuple-element.72, bf16[512,2,64]{0,2,1:T(8,128)(2,1)S(1)} %reshape_squeeze.12), kind=kOutput, calls=%fused_computation.54 | convolution fusion | flops 67239936 | bytes 1310720 | tf_op jit(solution)/shard_map/hqk,qhd->khd/dot_general | solution.py:168
  155.7 1.7 copy.140
  157.4 2.3 %fusion.16 = bf16[2,512,64]{1,2,0:T(8,128)(2,1)} fusion(bf16[2,512,512]{1,2,0:T(8,128)(2,1)} %get-tuple-element.73, bf16[512,2,64]{0,2,1:T(8,128)(2,1)S(1)} %reshape_squeeze.12), kind=kOutput, calls=%fused_computation.55 | convolution fusion | flops 67239936 | bytes 1310720 | tf_op jit(solution)/shard_map/hqk,qhd->khd/dot_general | solution.py:168
  159.7 1.6 copy.143
  161.3 1.7 copy.145
  163.0 1.3 fusion.117
  164.3 1.6 convolution_add_fusion.2
  167.3 1.7 copy.158
  168.9 4.2 %collective-permute-start.14 = (bf16[512,128]{1,0:T(8,128)(2,1)}, bf16[512,128]{1,0:T(8,128)(2,1)S(1)}, u32[]{:S(2)}, u32[]{:S(2)}) collective-permute-start(bf16[512,128]{1,0:T(8,128)(2,1)} %copy.145), channel_id=1, source_target_pairs={{0,1},{1,2},{2,3},{3,4},{4,5},{5,6},{6,7},{8,9},{9,10},{10,11},{11... | collective-permute-start | bytes 393224 | tf_op jit(solution)/shard_map/ppermute | solution.py:31
  173.1 1.3 collective-permute-start.13
  174.4 1.3 collective-permute-start.12
  175.7 4.7 %collective-permute-start.15 = (bf16[512,128]{1,0:T(8,128)(2,1)}, bf16[512,128]{1,0:T(8,128)(2,1)S(1)}, u32[]{:S(2)}, u32[]{:S(2)}) collective-permute-start(bf16[512,128]{1,0:T(8,128)(2,1)} %copy.147), channel_id=1, source_target_pairs={{0,2},{1,3},{2,4},{3,5},{4,6},{5,7},{8,10},{9,11},{10,12},{11,13},... | collective-permute-start | bytes 393224 | tf_op jit(solution)/shard_map/ppermute | solution.py:31
  181.1 1.3 collective-permute-start.16
  182.4 1.3 collective-permute-start.17
  183.7 5.0 %collective-permute-start.18 = (bf16[512,128]{1,0:T(8,128)(2,1)}, bf16[512,128]{1,0:T(8,128)(2,1)S(1)}, u32[]{:S(2)}, u32[]{:S(2)}) collective-permute-start(bf16[512,128]{1,0:T(8,128)(2,1)} %copy.155), channel_id=1, source_target_pairs={{0,1},{1,2},{2,3},{3,4},{4,5},{5,6},{6,7},{8,9},{9,10},{10,11},{11... | collective-permute-start | bytes 393224 | tf_op jit(solution)/shard_map/ppermute | solution.py:31
  188.7 4.5 %collective-permute-start.19 = (bf16[512,128]{1,0:T(8,128)(2,1)}, bf16[512,128]{1,0:T(8,128)(2,1)S(1)}, u32[]{:S(2)}, u32[]{:S(2)}) collective-permute-start(bf16[512,128]{1,0:T(8,128)(2,1)} %copy.157), channel_id=1, source_target_pairs={{0,2},{1,3},{2,4},{3,5},{4,6},{5,7},{8,10},{9,11},{10,12},{11,13},... | collective-permute-start | bytes 393224 | tf_op jit(solution)/shard_map/ppermute | solution.py:31
  194.0 2.1 %collective-permute-done.19 = bf16[512,128]{1,0:T(8,128)(2,1)S(1)} collective-permute-done((bf16[512,128]{1,0:T(8,128)(2,1)}, bf16[512,128]{1,0:T(8,128)(2,1)S(1)}, u32[]{:S(2)}, u32[]{:S(2)}) %collective-permute-start.19) | collective-permute-done | bytes 131104 | tf_op jit(solution)/shard_map/ppermute | solution.py:31
  (161 shorter events, 30.7 us)
Async XLA Ops:
  7.2 119.9 %copy-start = (bf16[512,1024]{1,0:T(8,128)(2,1)S(1)}, bf16[512,1024]{1,0:T(8,128)(2,1)}, u32[]{:S(2)}) copy-start(bf16[512,1024]{1,0:T(8,128)(2,1)} %param.13) | copy-start | bytes 3145732
  7.2 15.8 %copy-start.28 = (bf16[1,128,512]{2,1,0:T(8,128)(2,1)S(1)}, bf16[1,128,512]{2,1,0:T(8,128)(2,1)}, u32[]{:S(2)}) copy-start(bf16[1,128,512]{2,1,0:T(8,128)(2,1)} %param.9) | copy-start | bytes 393220
  7.2 18.1 %copy-start.29 = (bf16[1,128,512]{2,1,0:T(8,128)(2,1)S(1)}, bf16[1,128,512]{2,1,0:T(8,128)(2,1)}, u32[]{:S(2)}) copy-start(bf16[1,128,512]{2,1,0:T(8,128)(2,1)} %param.10) | copy-start | bytes 393220
  11.0 16.5 %all-to-all-start.2 = ((bf16[4,2,8192]{2,1,0:T(2,128)(2,1)}), bf16[4,2,8192]{2,1,0:T(2,128)(2,1)S(1)}, u32[]{:S(2)}, u32[]{:S(2)}) async-start(bf16[4,2,8192]{2,1,0:T(2,128)(2,1)} %reshape.507), calls=%async_computation.2 | async-start | bytes 262144 | tf_op jit(solution)/shard_map/all_to_all | solution.py:59
  15.2 23.7 %copy-start.24 = (bf16[1,128,1024]{2,1,0:T(8,128)(2,1)S(1)}, bf16[1,128,1024]{2,1,0:T(8,128)(2,1)}, u32[]{:S(2)}) copy-start(bf16[1,128,1024]{2,1,0:T(8,128)(2,1)} %param.11) | copy-start | bytes 786436
  24.5 17.8 %copy-start.25 = (bf16[1,128,1024]{2,1,0:T(8,128)(2,1)S(1)}, bf16[1,128,1024]{2,1,0:T(8,128)(2,1)}, u32[]{:S(2)}) copy-start(bf16[1,128,1024]{2,1,0:T(8,128)(2,1)} %param.12) | copy-start | bytes 786436
  27.5 8.0 %all-to-all-start.3 = ((bf16[4,2,8192]{2,1,0:T(2,128)(2,1)}), bf16[4,2,8192]{2,1,0:T(2,128)(2,1)S(1)}, u32[]{:S(2)}, u32[]{:S(2)}) async-start(bf16[4,2,8192]{2,1,0:T(2,128)(2,1)} %reshape.503), calls=%async_computation.3 | async-start | bytes 262144 | tf_op jit(solution)/shard_map/all_to_all | solution.py:60
  35.5 10.2 %all-to-all-start.4 = ((bf16[4,2,8192]{2,1,0:T(2,128)(2,1)}), bf16[4,2,8192]{2,1,0:T(2,128)(2,1)S(1)}, u32[]{:S(2)}, u32[]{:S(2)}) async-start(bf16[4,2,8192]{2,1,0:T(2,128)(2,1)} %reshape.505), calls=%async_computation.4 | async-start | bytes 262144 | tf_op jit(solution)/shard_map/all_to_all | solution.py:61
  45.7 13.7 %all-to-all-start.1 = ((bf16[4,2,16384]{2,1,0:T(2,128)(2,1)}), bf16[4,2,16384]{2,1,0:T(2,128)(2,1)S(1)}, u32[]{:S(2)}, u32[]{:S(2)}) async-start(bf16[4,2,16384]{2,1,0:T(2,128)(2,1)} %reshape.501), calls=%async_computation.1 | async-start | bytes 524288 | tf_op jit(solution)/shard_map/all_to_all | solution.py:62
  50.2 39.8 %collective-permute-start.6 = (bf16[512,128]{1,0:T(8,128)(2,1)}, bf16[512,128]{1,0:T(8,128)(2,1)}, u32[]{:S(2)}, u32[]{:S(2)}) collective-permute-start(bf16[512,128]{1,0:T(8,128)(2,1)} %bitcast.40), channel_id=1, source_target_pairs={{1,0},{2,1},{3,2},{4,3},{5,4},{6,5},{7,6},{9,8},{10,9},{11,10},{12... | collective-permute-start | bytes 393224 | tf_op jit(solution)/shard_map/ppermute | solution.py:31
  51.5 40.9 %collective-permute-start.4 = (bf16[512,128]{1,0:T(8,128)(2,1)}, bf16[512,128]{1,0:T(8,128)(2,1)}, u32[]{:S(2)}, u32[]{:S(2)}) collective-permute-start(bf16[512,128]{1,0:T(8,128)(2,1)} %bitcast.40), channel_id=1, source_target_pairs={{0,1},{1,2},{2,3},{3,4},{4,5},{5,6},{6,7},{8,9},{9,10},{10,11},{11... | collective-permute-start | bytes 393224 | tf_op jit(solution)/shard_map/ppermute | solution.py:31
  57.1 31.1 %copy-start.19 = (bf16[512,2,64]{0,2,1:T(8,128)(2,1)}, bf16[512,2,64]{0,2,1:T(8,128)(2,1)S(1)}, u32[]{:S(2)}) copy-start(bf16[512,2,64]{0,2,1:T(8,128)(2,1)S(1)} %reshape_squeeze.13) | copy-start | bytes 393220
  58.1 41.7 %collective-permute-start.10 = (bf16[512,128]{1,0:T(8,128)(2,1)}, bf16[512,128]{1,0:T(8,128)(2,1)}, u32[]{:S(2)}, u32[]{:S(2)}) collective-permute-start(bf16[512,128]{1,0:T(8,128)(2,1)} %bitcast.50), channel_id=1, source_target_pairs={{1,0},{2,1},{3,2},{4,3},{5,4},{6,5},{7,6},{9,8},{10,9},{11,10},{12... | collective-permute-start | bytes 393224 | tf_op jit(solution)/shard_map/ppermute | solution.py:31
  59.4 10.1 %all-to-all-start = ((bf16[4,2,16384]{2,1,0:T(2,128)(2,1)}), bf16[4,2,16384]{2,1,0:T(2,128)(2,1)S(1)}, u32[]{:S(2)}, u32[]{:S(2)}) async-start(bf16[4,2,16384]{2,1,0:T(2,128)(2,1)} %reshape.499), calls=%async_computation | async-start | bytes 524288 | tf_op jit(solution)/shard_map/all_to_all | solution.py:63
  62.8 64.3 %all-gather.2.cloned.1.call-start = ((), (), s32[]{:S(2)}) async-start(), calls=%async_computation.5 | async-start | bytes 1310720 | tf_op jit(solution)/shard_map/all_gather | solution.py:85
  63.3 6.6 %collective-permute-start.2 = (bf16[30,256]{1,0:T(8,128)(2,1)S(1)}, bf16[30,256]{1,0:T(8,128)(2,1)S(1)}, u32[]{:S(2)}, u32[]{:S(2)}) collective-permute-start(bf16[30,256]{1,0:T(8,128)(2,1)S(1)} %get-tuple-element.36), channel_id=1, source_target_pairs={{0,1},{1,2},{2,3},{3,4},{4,5},{5,6},{6,7},{8,9},{9,10},{10,11},{11... | collective-permute-start | bytes 46088 | tf_op jit(solution)/shard_map/ppermute | solution.py:19
  68.1 7.3 %collective-permute-start.3 = (bf16[30,256]{1,0:T(8,128)(2,1)S(1)}, bf16[30,256]{1,0:T(8,128)(2,1)S(1)}, u32[]{:S(2)}, u32[]{:S(2)}) collective-permute-start(bf16[30,256]{1,0:T(8,128)(2,1)S(1)} %get-tuple-element.37), channel_id=1, source_target_pairs={{1,0},{2,1},{3,2},{4,3},{5,4},{6,5},{7,6},{9,8},{10,9},{11,10},{12... | collective-permute-start | bytes 46088 | tf_op jit(solution)/shard_map/ppermute | solution.py:21
  70.0 6.9 %collective-permute-start = (bf16[30,256]{1,0:T(8,128)(2,1)S(1)}, bf16[30,256]{1,0:T(8,128)(2,1)S(1)}, u32[]{:S(2)}, u32[]{:S(2)}) collective-permute-start(bf16[30,256]{1,0:T(8,128)(2,1)S(1)} %get-tuple-element.38), channel_id=1, source_target_pairs={{0,1},{1,2},{2,3},{3,4},{4,5},{5,6},{6,7},{8,9},{9,10},{10,11},{11... | collective-permute-start | bytes 46088 | tf_op jit(solution)/shard_map/ppermute | solution.py:19
  75.4 7.5 %collective-permute-start.1 = (bf16[30,256]{1,0:T(8,128)(2,1)S(1)}, bf16[30,256]{1,0:T(8,128)(2,1)S(1)}, u32[]{:S(2)}, u32[]{:S(2)}) collective-permute-start(bf16[30,256]{1,0:T(8,128)(2,1)S(1)} %get-tuple-element.39), channel_id=1, source_target_pairs={{1,0},{2,1},{3,2},{4,3},{5,4},{6,5},{7,6},{9,8},{10,9},{11,10},{12... | collective-permute-start | bytes 46088 | tf_op jit(solution)/shard_map/ppermute | solution.py:21
  76.8 24.2 %collective-permute-start.8 = (bf16[512,128]{1,0:T(8,128)(2,1)}, bf16[512,128]{1,0:T(8,128)(2,1)}, u32[]{:S(2)}, u32[]{:S(2)}) collective-permute-start(bf16[512,128]{1,0:T(8,128)(2,1)} %bitcast.50), channel_id=1, source_target_pairs={{0,1},{1,2},{2,3},{3,4},{4,5},{5,6},{6,7},{8,9},{9,10},{10,11},{11... | collective-permute-start | bytes 393224 | tf_op jit(solution)/shard_map/ppermute | solution.py:31
  91.0 21.6 %copy-start.20 = (bf16[512,128]{0,1:T(8,128)(2,1)}, bf16[512,128]{0,1:T(8,128)(2,1)S(1)}, u32[]{:S(2)}) copy-start(bf16[512,128]{0,1:T(8,128)(2,1)S(1)} %copy.124) | copy-start | bytes 393220
  91.0 24.9 %collective-permute-start.7 = (bf16[512,128]{1,0:T(8,128)(2,1)}, bf16[512,128]{1,0:T(8,128)(2,1)}, u32[]{:S(2)}, u32[]{:S(2)}) collective-permute-start(bf16[512,128]{1,0:T(8,128)(2,1)} %collective-permute-done.6), channel_id=1, source_target_pairs={{1,0},{2,1},{3,2},{4,3},{5,4},{6,5},{7,6},{9,8},{10,9},{11,10},{12... | collective-permute-start | bytes 393224 | tf_op jit(solution)/shard_map/ppermute | solution.py:31
  94.0 16.1 %copy-start.22 = (bf16[512,128]{0,1:T(8,128)(2,1)S(1)}, bf16[512,128]{0,1:T(8,128)(2,1)}, u32[]{:S(2)}) copy-start(bf16[512,128]{0,1:T(8,128)(2,1)} %copy.123) | copy-start | bytes 393220
  94.0 16.1 %copy-start.27 = (pred[512,512]{0,1:T(8,128)(4,1)S(1)}, pred[512,512]{0,1:T(8,128)(4,1)}, u32[]{:S(2)}) copy-start(pred[512,512]{0,1:T(8,128)(4,1)} %get-tuple-element.77) | copy-start | bytes 786436
  94.0 22.9 %collective-permute-start.5 = (bf16[512,128]{1,0:T(8,128)(2,1)}, bf16[512,128]{1,0:T(8,128)(2,1)}, u32[]{:S(2)}, u32[]{:S(2)}) collective-permute-start(bf16[512,128]{1,0:T(8,128)(2,1)} %collective-permute-done.4), channel_id=1, source_target_pairs={{0,1},{1,2},{2,3},{3,4},{4,5},{5,6},{6,7},{8,9},{9,10},{10,11},{11... | collective-permute-start | bytes 393224 | tf_op jit(solution)/shard_map/ppermute | solution.py:31
  99.8 18.9 %collective-permute-start.11 = (bf16[512,128]{1,0:T(8,128)(2,1)}, bf16[512,128]{1,0:T(8,128)(2,1)}, u32[]{:S(2)}, u32[]{:S(2)}) collective-permute-start(bf16[512,128]{1,0:T(8,128)(2,1)} %collective-permute-done.10), channel_id=1, source_target_pairs={{1,0},{2,1},{3,2},{4,3},{5,4},{6,5},{7,6},{9,8},{10,9},{11,10},{12... | collective-permute-start | bytes 393224 | tf_op jit(solution)/shard_map/ppermute | solution.py:31
  101.1 19.2 %collective-permute-start.9 = (bf16[512,128]{1,0:T(8,128)(2,1)}, bf16[512,128]{1,0:T(8,128)(2,1)}, u32[]{:S(2)}, u32[]{:S(2)}) collective-permute-start(bf16[512,128]{1,0:T(8,128)(2,1)} %collective-permute-done.8), channel_id=1, source_target_pairs={{0,1},{1,2},{2,3},{3,4},{4,5},{5,6},{6,7},{8,9},{9,10},{10,11},{11... | collective-permute-start | bytes 393224 | tf_op jit(solution)/shard_map/ppermute | solution.py:31
  116.9 10.1 %copy-start.10 = (bf16[512,128]{0,1:T(8,128)(2,1)}, bf16[512,128]{0,1:T(8,128)(2,1)S(1)}, u32[]{:S(2)}) copy-start(bf16[512,128]{0,1:T(8,128)(2,1)S(1)} %copy.125) | copy-start | bytes 393220
  122.0 3.0 %copy-start.26 = (pred[512,512]{0,1:T(8,128)(4,1)S(1)}, pred[512,512]{0,1:T(8,128)(4,1)}, u32[]{:S(2)}) copy-start(pred[512,512]{0,1:T(8,128)(4,1)} %get-tuple-element.79) | copy-start | bytes 786436
  122.0 5.1 %copy-start.32 = (f32[2,512]{1,0:T(2,128)S(1)}, f32[2,512]{1,0:T(2,128)}, u32[]{:S(2)}) copy-start(f32[2,512]{1,0:T(2,128)} %get-tuple-element.88) | copy-start | bytes 12292
  122.0 5.1 %copy-start.33 = (f32[2,512]{1,0:T(2,128)S(1)}, f32[2,512]{1,0:T(2,128)}, u32[]{:S(2)}) copy-start(f32[2,512]{1,0:T(2,128)} %get-tuple-element.90) | copy-start | bytes 12292
  127.1 8.8 %copy-start.30 = (f32[2,512]{1,0:T(2,128)}, f32[2,512]{1,0:T(2,128)S(1)}, u32[]{:S(2)}) copy-start(f32[2,512]{1,0:T(2,128)S(1)} %get-tuple-element.35) | copy-start | bytes 12292
  128.8 1.6 copy-start.4
  128.8 1.6 copy-start.18
  130.4 1.6 copy-start.1
  130.4 1.6 copy-start.13
  132.0 1.6 copy-start.2
  132.0 1.6 copy-start.12
  133.6 1.6 copy-start.3
  133.6 1.6 copy-start.14
  138.6 2.3 %copy-start.31 = (f32[2,512]{1,0:T(2,128)S(1)}, f32[2,512]{1,0:T(2,128)}, u32[]{:S(2)}) copy-start(f32[2,512]{1,0:T(2,128)} %copy-done.30) | copy-start | bytes 12292
  140.9 5.4 %copy-start.21 = (bf16[512,128]{0,1:T(8,128)(2,1)S(1)}, bf16[512,128]{0,1:T(8,128)(2,1)}, u32[]{:S(2)}) copy-start(bf16[512,128]{0,1:T(8,128)(2,1)} %copy-done.20) | copy-start | bytes 393220
  145.2 2.2 %copy-start.8 = (f32[2,64,512]{2,1,0:T(8,128)S(1)}, f32[2,64,512]{2,1,0:T(8,128)}, u32[]{:S(2)}) copy-start(f32[2,64,512]{2,1,0:T(8,128)} %fusion.12) | copy-start | bytes 786436
  145.2 2.3 %copy-start.17 = (bf16[2,64,512]{2,1,0:T(8,128)(2,1)S(1)}, bf16[2,64,512]{2,1,0:T(8,128)(2,1)}, u32[]{:S(2)}) copy-start(bf16[2,64,512]{2,1,0:T(8,128)(2,1)} %convolution_convert_fusion) | copy-start | bytes 393220
  145.2 3.1 %copy-start.16 = (bf16[2,64,512]{2,1,0:T(8,128)(2,1)S(1)}, bf16[2,64,512]{2,1,0:T(8,128)(2,1)}, u32[]{:S(2)}) copy-start(bf16[2,64,512]{2,1,0:T(8,128)(2,1)} %convolution_convert_fusion.1) | copy-start | bytes 393220
  145.2 3.8 %copy-start.15 = (bf16[2,64,512]{2,1,0:T(8,128)(2,1)S(1)}, bf16[2,64,512]{2,1,0:T(8,128)(2,1)}, u32[]{:S(2)}) copy-start(bf16[2,64,512]{2,1,0:T(8,128)(2,1)} %convolution_convert_fusion.2) | copy-start | bytes 393220
  145.2 5.4 %copy-start.6 = (bf16[2,512,512]{1,2,0:T(8,128)(2,1)S(1)}, bf16[2,512,512]{1,2,0:T(8,128)(2,1)}, u32[]{:S(2)}) copy-start(bf16[2,512,512]{1,2,0:T(8,128)(2,1)} %get-tuple-element.71) | copy-start | bytes 3145732
  151.7 11.4 %copy-start.5 = (bf16[2,512,512]{1,2,0:T(8,128)(2,1)S(1)}, bf16[2,512,512]{1,2,0:T(8,128)(2,1)}, u32[]{:S(2)}) copy-start(bf16[2,512,512]{1,2,0:T(8,128)(2,1)} %get-tuple-element.75) | copy-start | bytes 3145732
  163.0 3.0 %copy-start.7 = (bf16[2,512,512]{1,2,0:T(8,128)(2,1)S(1)}, bf16[2,512,512]{1,2,0:T(8,128)(2,1)}, u32[]{:S(2)}) copy-start(bf16[2,512,512]{1,2,0:T(8,128)(2,1)} %get-tuple-element.73) | copy-start | bytes 3145732
  163.0 3.0 %copy-start.9 = (f32[2,512,64]{1,2,0:T(8,128)S(1)}, f32[2,512,64]{1,2,0:T(8,128)}, u32[]{:S(2)}) copy-start(f32[2,512,64]{1,2,0:T(8,128)} %fusion.118) | copy-start | bytes 786436
  163.0 3.0 %copy-start.23 = (bf16[512,128]{0,1:T(8,128)(2,1)S(1)}, bf16[512,128]{0,1:T(8,128)(2,1)}, u32[]{:S(2)}) copy-start(bf16[512,128]{0,1:T(8,128)(2,1)} %copy.123) | copy-start | bytes 393220
  164.3 2.0 copy-start.11
  168.9 13.4 %collective-permute-start.14 = (bf16[512,128]{1,0:T(8,128)(2,1)}, bf16[512,128]{1,0:T(8,128)(2,1)S(1)}, u32[]{:S(2)}, u32[]{:S(2)}) collective-permute-start(bf16[512,128]{1,0:T(8,128)(2,1)} %copy.145), channel_id=1, source_target_pairs={{0,1},{1,2},{2,3},{3,4},{4,5},{5,6},{6,7},{8,9},{9,10},{10,11},{11... | collective-permute-start | bytes 393224 | tf_op jit(solution)/shard_map/ppermute | solution.py:31
  173.1 10.5 %collective-permute-start.13 = (bf16[512,128]{1,0:T(8,128)(2,1)}, bf16[512,128]{1,0:T(8,128)(2,1)S(1)}, u32[]{:S(2)}, u32[]{:S(2)}) collective-permute-start(bf16[512,128]{1,0:T(8,128)(2,1)} %copy.143), channel_id=1, source_target_pairs={{1,0},{2,1},{3,2},{4,3},{5,4},{6,5},{7,6},{9,8},{10,9},{11,10},{12... | collective-permute-start | bytes 393224 | tf_op jit(solution)/shard_map/ppermute | solution.py:31
  174.4 14.2 %collective-permute-start.12 = (bf16[512,128]{1,0:T(8,128)(2,1)}, bf16[512,128]{1,0:T(8,128)(2,1)S(1)}, u32[]{:S(2)}, u32[]{:S(2)}) collective-permute-start(bf16[512,128]{1,0:T(8,128)(2,1)} %copy.140), channel_id=1, source_target_pairs={{2,0},{3,1},{4,2},{5,3},{6,4},{7,5},{10,8},{11,9},{12,10},{13,11},... | collective-permute-start | bytes 393224 | tf_op jit(solution)/shard_map/ppermute | solution.py:31
  175.7 17.5 %collective-permute-start.15 = (bf16[512,128]{1,0:T(8,128)(2,1)}, bf16[512,128]{1,0:T(8,128)(2,1)S(1)}, u32[]{:S(2)}, u32[]{:S(2)}) collective-permute-start(bf16[512,128]{1,0:T(8,128)(2,1)} %copy.147), channel_id=1, source_target_pairs={{0,2},{1,3},{2,4},{3,5},{4,6},{5,7},{8,10},{9,11},{10,12},{11,13},... | collective-permute-start | bytes 393224 | tf_op jit(solution)/shard_map/ppermute | solution.py:31
  181.1 12.9 %collective-permute-start.16 = (bf16[512,128]{1,0:T(8,128)(2,1)}, bf16[512,128]{1,0:T(8,128)(2,1)S(1)}, u32[]{:S(2)}, u32[]{:S(2)}) collective-permute-start(bf16[512,128]{1,0:T(8,128)(2,1)} %copy.150), channel_id=1, source_target_pairs={{2,0},{3,1},{4,2},{5,3},{6,4},{7,5},{10,8},{11,9},{12,10},{13,11},... | collective-permute-start | bytes 393224 | tf_op jit(solution)/shard_map/ppermute | solution.py:31
  182.4 11.6 %collective-permute-start.17 = (bf16[512,128]{1,0:T(8,128)(2,1)}, bf16[512,128]{1,0:T(8,128)(2,1)S(1)}, u32[]{:S(2)}, u32[]{:S(2)}) collective-permute-start(bf16[512,128]{1,0:T(8,128)(2,1)} %copy.153), channel_id=1, source_target_pairs={{1,0},{2,1},{3,2},{4,3},{5,4},{6,5},{7,6},{9,8},{10,9},{11,10},{12... | collective-permute-start | bytes 393224 | tf_op jit(solution)/shard_map/ppermute | solution.py:31
  183.7 10.3 %collective-permute-start.18 = (bf16[512,128]{1,0:T(8,128)(2,1)}, bf16[512,128]{1,0:T(8,128)(2,1)S(1)}, u32[]{:S(2)}, u32[]{:S(2)}) collective-permute-start(bf16[512,128]{1,0:T(8,128)(2,1)} %copy.155), channel_id=1, source_target_pairs={{0,1},{1,2},{2,3},{3,4},{4,5},{5,6},{6,7},{8,9},{9,10},{10,11},{11... | collective-permute-start | bytes 393224 | tf_op jit(solution)/shard_map/ppermute | solution.py:31
  188.7 7.4 %collective-permute-start.19 = (bf16[512,128]{1,0:T(8,128)(2,1)}, bf16[512,128]{1,0:T(8,128)(2,1)S(1)}, u32[]{:S(2)}, u32[]{:S(2)}) collective-permute-start(bf16[512,128]{1,0:T(8,128)(2,1)} %copy.157), channel_id=1, source_target_pairs={{0,2},{1,3},{2,4},{3,5},{4,6},{5,7},{8,10},{9,11},{10,12},{11,13},... | collective-permute-start | bytes 393224 | tf_op jit(solution)/shard_map/ppermute | solution.py:31
Sparse Core Ops, SparseCore 0:
  88.4 18.4 all-gather.1
where the time goes:
time: 207 us; the launch traced here: 204 us
  starting transfers between devices  82 us (40%)
  local copies, waits for them, and re-layouts  39.1 us (19%)
  matrix products  34.8 us (17%)
  other arithmetic  26.7 us (13%)
  between operations  14.9 us (7%)
  waiting for transfers between devices  6.1 us (3%)
    ppermute x16, starting transfers between devices, shifted(): lax.ppermute(value, axis, [(source, source + steps) for source in range(f...  51.4 us
    unnamed x90, local copies, waits for them, and re-layouts  13.2 us
    dot_general x5, matrix products, block_logits(): jnp.einsum('qhd,khd->hqk', query_heads, keys_now, preferred_element_type=...  12.6 us
    ppermute x8, local copies, waits for them, and re-layouts, shifted(): lax.ppermute(value, axis, [(source, source + steps) for source in range(f...  12 us
    ppermute x2, starting transfers between devices, padded(): lax.ppermute(tail, axis, [(i, (i + 1) % count) for i in range(ends)])  10.2 us
    unnamed x5, other arithmetic  8.65 us
    dot_general x5, matrix products, on_device(): jnp.einsum('hqk,qhd->khd', dlogits, query_heads, preferred_element_type=j...  7.3 us
    reshape x4, local copies, waits for them, and re-layouts, on_device(): key_part = (jnp.einsum('hqk,qhd->khd', dlogits, query_heads, preferred_el...  6.71 us
  transfers between devices with their start and end apart: 26, of which 2 were waited for; matrix products, arithmetic and copies ran while one was open for 27% of the time, Pallas kernels for 0%

commit v1 on v0

v1 whole, which is shorter than its diff:
```python
import jax
import jax.numpy as jnp
from jax import lax
from jax.experimental import pallas as pl
from jax.experimental.pallas import tpu as pltpu
from jax.sharding import Mesh
from jax.sharding import PartitionSpec as P

HEAD_DIM = 64
KERNEL = 31
REACH = 2
LANES = 128
QT = 256
HALO = 32
HALF = 16
NEG = -1e30
F32 = jnp.float32
BF16 = jnp.bfloat16
NT_DIMS = (((1,), (1,)), ((), ()))
NN_DIMS = (((1,), (0,)), ((), ()))
VMEM_LIMIT = 56 * 1024 * 1024


def dot(a, b, dims):
    return lax.dot_general(a, b, dims, preferred_element_type=F32)


def call(body, outs, n_in, smem=(), scratch=(), name=None):
    vm = pl.BlockSpec(memory_space=pltpu.VMEM)
    sm = pl.BlockSpec(memory_space=pltpu.SMEM)
    return pl.pallas_call(
        body,
        out_shape=outs,
        in_specs=[sm if i in smem else vm for i in range(n_in)],
        out_specs=jax.tree.map(lambda _: vm, outs),
        scratch_shapes=list(scratch),
        compiler_params=pltpu.CompilerParams(vmem_limit_bytes=VMEM_LIMIT),
        name=name,
    )


def arr(shape, dtype=BF16):
    return jax.ShapeDtypeStruct(shape, dtype)


def swap_pairs(count, distance, phase):
    pairs = []
    for i in range(count - distance):
        if (i // distance) % 2 == phase:
            pairs += [(i, i + distance), (i + distance, i)]
    return pairs


def on_device(sizes, query, key, value, resid_in, out_grad, out_weight, conv_kernel, frame_lengths):
    heads_axis, z_count, group = sizes
    ctx_count = z_count * group
    rows = query.shape[1]
    width = query.shape[2]
    channels = resid_in.shape[2]
    block = rows * heads_axis
    supers = group * block
    members = group * heads_axis
    half = rows // 2
    near = -(-REACH // group)
    window = REACH * block
    tiles = 2 * window // QT + 1
    per_block = block // QT
    lead = near * supers - window
    ext = (2 * near + 1) * supers
    out_cols = channels // heads_axis
    scale = HEAD_DIM ** (-0.5)
    chain = heads_axis * ctx_count

    def head_of(member):
        return group * (member % heads_axis) + member // heads_axis

    def cols(head):
        return slice(head * HEAD_DIM, (head + 1) * HEAD_DIM)

    def edge_body(resid_ref, grad_ref, first_ref, second_ref):
        odd = (lax.axis_index("head") % 2) == 1
        bottom = rows - HALO
        for out_ref, low in ((first_ref, odd), (second_ref, jnp.logical_not(odd))):
            out_ref[0:HALO, :] = jnp.where(low, resid_ref[0, 0:HALO, :], resid_ref[0, bottom:rows, :])
            out_ref[HALO : HALO + HALF, :] = jnp.where(
                low, grad_ref[0, 0:HALF, :], grad_ref[0, rows - HALF : rows, :]
            )

    edges = call(edge_body, [arr((HALO + HALF, channels))] * 2, 2, name="edges")(resid_in, out_grad)

    def place(i):
        return (i % heads_axis) * ctx_count + i // heads_axis

    halos = [
        lax.ppermute(
            edges[phase],
            ("head", "z", "y"),
            [(place(a), place(b)) for a, b in swap_pairs(chain, 1, phase)],
        )
        for phase in (0, 1)
    ]

    def pack_body(q_ref, k_ref, v_ref, out_ref):
        for member in range(members):
            c = cols(head_of(member))
            out_ref[member, 0:rows, 0:HEAD_DIM] = k_ref[0, :, c]
            out_ref[member, 0:rows, HEAD_DIM:LANES] = v_ref[0, :, c]
            out_ref[member, rows : rows + half, 0:HEAD_DIM] = q_ref[0, 0:half, c]
            out_ref[member, rows : rows + half, HEAD_DIM:LANES] = q_ref[0, half:rows, c]

    packed = call(pack_body, arr((members, rows + half, LANES)), 3, name="pack")(query, key, value)
    mine = lax.all_to_all(packed, ("y", "head"), 0, 0, tiled=True)

    span = rows + 2 * HALF

    def conv_body(resid_ref, grad_ref, first_ref, second_ref, taps_ref, weight_ref, dres_ref, hg_ref, low_ref):
        odd = (lax.axis_index("head") % 2) == 1

        def taps_sum(x, tap_of, length):
            total = None
            for b in range(8):
                part = None
                for a in range(4):
                    offset = 8 * a + b
                    if offset < 1 or offset > KERNEL:
                        continue
                    term = tap_of(offset - 1) * x[8 * a : 8 * a + length + 8]
                    part = term if part is None else part + term
                if b:
                    part = pltpu.roll(part, length + 8 - b, 0)
                part = part[0:length]
                total = part if total is None else total + part
            return total

        def chunk(c, carry):
            at = pl.multiple_of(c * LANES, LANES)
            lane = pl.ds(at, LANES)
            first = first_ref[:, lane].astype(F32)
            second = second_ref[:, lane].astype(F32)
            before = jnp.where(odd, first, second)
            after = jnp.where(odd, second, first)
            taps = taps_ref[:, lane].astype(F32)
            x = jnp.concatenate([before[0:HALO], resid_ref[0, :, lane].astype(F32), after[0:HALO]], axis=0)
            middle = grad_ref[0, :, lane].astype(F32)
            g = jnp.concatenate([before[HALO:], middle, after[HALO:]], axis=0)
            pre = taps_sum(x, lambda k: taps[k : k + 1], span)
            s = 1.0 / (1.0 + jnp.exp(-pre))
            cg = g * (s * (1.0 + pre * (1.0 - s)))
            out = middle + taps_sum(cg, lambda k: taps[KERNEL - 1 - k : KERNEL - k], rows)
            low_ref[:, lane] = out.astype(BF16)
            return carry

        lax.fori_loop(0, channels // LANES, chunk, 0)
        for h in range(heads_axis):
            dres_ref[h] = low_ref[:, h * out_cols : (h + 1) * out_cols]
        hg = dot(low_ref[...], weight_ref[...], NT_DIMS).astype(BF16)
        for member in range(members):
            c = cols(head_of(member))
            hg_ref[member, :, 0:HEAD_DIM] = hg[0:half, c]
            hg_ref[member, :, HEAD_DIM:LANES] = hg[half:rows, c]

    dres, hg = call(
        conv_body,
        [arr((heads_axis, rows, out_cols)), arr((members, half, LANES))],
        6,
        scratch=[pltpu.VMEM((rows, channels), BF16)],
        name="conv",
    )(resid_in, out_grad, halos[0], halos[1], conv_kernel, out_weight)
    grads = lax.all_to_all(hg, ("y", "head"), 0, 0, tiled=True)

    both = mine[:, 0:rows, :].reshape(supers, LANES)

    def spread(parts):
        return [
            lax.ppermute(parts[2 * d - 2 + phase], "z", swap_pairs(z_count, d, phase))
            for d in range(1, near + 1)
            for phase in (0, 1)
        ]

    around = spread([both] * (2 * near))
    d_resid = lax.all_to_all(dres, "head", 0, 0, tiled=True).reshape(1, block, out_cols)

    def attn_body(*refs):
        len_ref, mine_ref, hg_ref = refs[:3]
        around_refs = refs[3 : 3 + 2 * near]
        dq_ref, own_ref = refs[3 + 2 * near : 5 + 2 * near]
        back_refs = refs[5 + 2 * near : 5 + 4 * near]
        kv, kt, qz, hz, s_sc, d_sc, acc, dq_sc = refs[5 + 4 * near :]
        z = lax.axis_index("z")
        low = lax.broadcasted_iota(jnp.int32, (half, LANES), 1) < HEAD_DIM
        zero = jnp.zeros((half, LANES), BF16)
        for member in range(members):
            at = member * rows
            kv[near * supers + at : near * supers + at + rows, :] = mine_ref[member, 0:rows, :]
            q = mine_ref[member, rows : rows + half, :].astype(F32) * scale
            qz[at : at + half, :] = jnp.where(low, q, 0.0).astype(BF16)
            qz[at + half : at + rows, :] = jnp.where(low, pltpu.roll(q, HEAD_DIM, 1), 0.0).astype(BF16)
            g = hg_ref[member].astype(F32)
            hz[at : at + half, :] = jnp.where(low, 0.0, pltpu.roll(g, HEAD_DIM, 1)).astype(BF16)
            hz[at + half : at + rows, :] = jnp.where(low, 0.0, g).astype(BF16)
        for d in range(1, near + 1):
            left, right = (near - d) * supers, (near + d) * supers
            odd = ((z // d) % 2) == 1

            @pl.when(odd)
            def _():
                kv[left : left + supers, :] = around_refs[2 * d - 2][...]
                kv[right : right + supers, :] = around_refs[2 * d - 1][...]

            @pl.when(jnp.logical_not(odd))
            def _():
                kv[left : left + supers, :] = around_refs[2 * d - 1][...]
                kv[right : right + supers, :] = around_refs[2 * d - 2][...]

        def turn(t, carry):
            at = pl.multiple_of(t * QT, QT)
            kt[t] = jnp.transpose(kv[pl.ds(at, QT), :].astype(F32))[0:HEAD_DIM].astype(BF16)
            return carry

        lax.fori_loop(0, ext // QT, turn, 0)
        acc[...] = jnp.zeros_like(acc)
        key_at = lax.broadcasted_iota(jnp.int32, (QT, QT), 0)
        query_at = lax.broadcasted_iota(jnp.int32, (QT, QT), 1)

        def fold(x, op):
            return op(x.reshape(QT // 8, 8, QT), axis=0)

        def limit(t):
            index = (z - near) * group + t // per_block
            inside = jnp.logical_and(index >= 0, index < ctx_count)
            length = len_ref[jnp.clip(index, 0, ctx_count - 1)]
            return jnp.where(inside, length, 0) - (t % per_block) * QT

        def query_tile(a, carry):
            q_rows = pl.ds(pl.multiple_of(a * QT, QT), QT)
            q = qz[q_rows, :]
            g = hz[q_rows, :]

            def keys(j):
                return pl.ds(pl.multiple_of((a + j) * QT + lead, QT), QT)

            top = jnp.full((8, QT), NEG, F32)
            for j in range(tiles):
                s = dot(kv[keys(j), :], q, NT_DIMS)
                live = key_at < limit(a + j + lead // QT)
                if j == 0:
                    live = jnp.logical_and(live, key_at >= query_at)
                if j == tiles - 1:
                    live = jnp.logical_and(live, key_at <= query_at)
                s = jnp.where(live, s, NEG)
                s_sc[j] = s
                top = jnp.maximum(top, fold(s, jnp.max))
            top = jnp.max(top, axis=0, keepdims=True)
            mass = jnp.zeros((8, QT), F32)
            weighted = jnp.zeros((8, QT), F32)
            for j in range(tiles):
                e = jnp.exp(s_sc[j] - top)
                slopes = dot(kv[keys(j), :], g, NT_DIMS)
                s_sc[j] = e
                d_sc[j] = slopes
                mass = mass + fold(e, jnp.sum)
                weighted = weighted + fold(e * slopes, jnp.sum)
            inverse = 1.0 / jnp.sum(mass, axis=0, keepdims=True)
            delta = jnp.sum(weighted, axis=0, keepdims=True) * inverse
            dq = jnp.zeros((HEAD_DIM, QT), F32)
            for j in range(tiles):
                p = s_sc[j] * inverse
                ds = (p * (d_sc[j] - delta)).astype(BF16)
                acc[keys(j), :] += dot(ds, q, NN_DIMS) + dot(p.astype(BF16), g, NN_DIMS)
                dq = dq + dot(kt[a + j + lead // QT], ds, NN_DIMS)
            dq_sc[q_rows, :] = jnp.transpose(dq * scale).astype(BF16)
            return carry

        lax.fori_loop(0, supers // QT, query_tile, 0)
        own_ref[...] = acc[near * supers : (near + 1) * supers, :]
        for d in range(1, near + 1):
            left, right = (near - d) * supers, (near + d) * supers
            odd = ((z // d) % 2) == 1

            @pl.when(odd)
            def _():
                back_refs[2 * d - 2][...] = acc[left : left + supers, :].astype(BF16)
                back_refs[2 * d - 1][...] = acc[right : right + supers, :].astype(BF16)

            @pl.when(jnp.logical_not(odd))
            def _():
                back_refs[2 * d - 1][...] = acc[left : left + supers, :].astype(BF16)
                back_refs[2 * d - 2][...] = acc[right : right + supers, :].astype(BF16)

        if group == 1:
            dq_ref[0] = dq_sc[...]
        else:
            for b in range(group):
                at = b * block
                mid = at + block // 2
                dq_ref[b, :, 0:HEAD_DIM] = dq_sc[at:mid, :]
                dq_ref[b, :, HEAD_DIM:LANES] = dq_sc[mid : at + block, :]

    dq_shape = (1, supers, HEAD_DIM) if group == 1 else (group, block // 2, LANES)
    outs = call(
        attn_body,
        [arr(dq_shape), arr((supers, LANES), F32)] + [arr((supers, LANES))] * (2 * near),
        3 + 2 * near,
        smem=(0,),
        scratch=[
            pltpu.VMEM((ext, LANES), BF16),
            pltpu.VMEM((ext // QT, HEAD_DIM, QT), BF16),
            pltpu.VMEM((supers, LANES), BF16),
            pltpu.VMEM((supers, LANES), BF16),
            pltpu.VMEM((tiles, QT, QT), F32),
            pltpu.VMEM((tiles, QT, QT), F32),
            pltpu.VMEM((ext, LANES), F32),
            pltpu.VMEM((supers, HEAD_DIM), BF16),
        ],
        name="attn",
    )(frame_lengths, mine, grads, *around)
    dq, own = outs[:2]
    back = spread(outs[2:])

    if group == 1:

        def last_body(*refs):
            total = refs[0][...]
            for ref in refs[1 : 1 + 2 * near]:
                total = total + ref[...].astype(F32)
            total = total.astype(BF16)
            refs[-2][0] = total[:, 0:HEAD_DIM]
            refs[-1][0] = total[:, HEAD_DIM:LANES]

        d_key, d_value = call(last_body, [arr((1, block, HEAD_DIM))] * 2, 1 + 2 * near, name="last")(own, *back)
        return d_resid, dq, d_key, d_value

    hb = block // 2

    def sum_body(*refs):
        dq_ref, own_ref = refs[:2]
        part_refs = refs[2 : 2 + 2 * near]
        keep_ref, send_ref = refs[2 + 2 * near :]
        y = lax.axis_index("y")
        for slot, out_ref in ((y, keep_ref), (1 - y, send_ref)):
            take = pl.ds(pl.multiple_of(slot * block, block), block)
            total = own_ref[take, :]
            for ref in part_refs:
                total = total + ref[take, :].astype(F32)
            out_ref[0:block, :] = total.astype(BF16)
            out_ref[block : block + hb, :] = dq_ref[slot]

    keep, send = call(sum_body, [arr((block + hb, LANES))] * 2, 2 + 2 * near, name="sum")(dq, own, *back)
    other = lax.ppermute(send, "y", [(0, 1), (1, 0)])

    def last_body(keep_ref, other_ref, dq_ref, dk_ref, dv_ref):
        y = lax.axis_index("y")

        def put(lo_ref, up_ref):
            lo, up = lo_ref[0:block, :], up_ref[0:block, :]
            dk_ref[0, :, 0:HEAD_DIM] = lo[:, 0:HEAD_DIM]
            dk_ref[0, :, HEAD_DIM:LANES] = up[:, 0:HEAD_DIM]
            dv_ref[0, :, 0:HEAD_DIM] = lo[:, HEAD_DIM:LANES]
            dv_ref[0, :, HEAD_DIM:LANES] = up[:, HEAD_DIM:LANES]
            for ref, at in ((lo_ref, 0), (up_ref, HEAD_DIM)):
                dq_ref[0, 0:hb, at : at + HEAD_DIM] = ref[block : block + hb, 0:HEAD_DIM]
                dq_ref[0, hb:block, at : at + HEAD_DIM] = ref[block : block + hb, HEAD_DIM:LANES]

        @pl.when(y == 0)
        def _():
            put(keep_ref, other_ref)

        @pl.when(y == 1)
        def _():
            put(other_ref, keep_ref)

    d_query, d_key, d_value = call(last_body, [arr((1, block, LANES))] * 3, 2, name="last")(keep, other)
    return d_resid, d_query, d_key, d_value


def solution(mesh):
    heads_axis = mesh.shape["head"]
    ctx_count = mesh.shape["ctx"]

    def run(query, *rest):
        group = query.shape[2] // HEAD_DIM // heads_axis
        z_count = ctx_count // group
        fine = Mesh(mesh.devices.reshape(heads_axis, z_count, group), ("head", "z", "y"))
        rows_spec = P(("z", "y"), "head", None)
        cols_spec = P(("z", "y"), None, "head")
        sizes = (heads_axis, z_count, group)
        return jax.shard_map(
            lambda *args: on_device(sizes, *args),
            mesh=fine,
            in_specs=(rows_spec,) * 5 + (P(),) * 3,
            out_specs=(cols_spec,) * 4,
            check_vma=False,
        )(query, *rest)

    return run
```

time: 207 us -> 82.2 us (0.40)
  starting transfers between devices: 82 us -> 12.4 us
  matrix products: 34.8 us -> 0 us
  local copies, waits for them, and re-layouts: 39.1 us -> 4.85 us
  Pallas kernels: 0 us -> 27.3 us
  blocking collectives: 0 us -> 26.9 us
  other arithmetic: 26.7 us -> 0 us
  between operations: 14.9 us -> 0.69 us
  waiting for transfers between devices: 6.1 us -> 8.5 us
    ppermute x20 -> x7, starting transfers between devices: 64.2 us -> 8.95 us  [the longest x4 7.74 us: spread(): lax.ppermute(parts[2 * d - 2 + phase], 'z', swap_pairs(z_count, d, phase))]
    dot_general x26 -> x0, matrix products: 34.8 us -> none  [the longest x5 12.6 us: block_logits(): jnp.einsum('qhd,khd->hqk', query_heads, keys_now, preferred_element_type=...]
    pallas_call x0 -> x6, Pallas kernels: none -> 27.3 us  [the longest x1 12.9 us: on_device(): call(attn_body, [arr(dq_shape), arr((supers, LANES), F32)] + [arr((supers...]
    all_to_all x0 -> x2, blocking collectives: none -> 26.9 us  [the longest x1 13.5 us: on_device(): mine = lax.all_to_all(packed, ('y', 'head'), 0, 0, tiled=True)]
    all_to_all x5 -> x1, starting transfers between devices: 17.7 us -> 3.42 us  [on_device(): lax.all_to_all(dres, 'head', 0, 0, tiled=True).reshape(1, block, out_cols)]
    ppermute x8 -> x0, local copies, waits for them, and re-layouts: 12 us -> none  [shifted(): lax.ppermute(value, axis, [(source, source + steps) for source in range(f...]
    reshape x8 -> x0, local copies, waits for them, and re-layouts: 9.77 us -> none  [the longest x4 6.71 us: on_device(): key_part = (jnp.einsum('hqk,qhd->khd', dlogits, query_heads, preferred_el...]
    unnamed x5 -> x0, other arithmetic: 8.65 us -> none
  transfers between devices with their start and end apart: 26 -> 8, of which waited for: 2 -> 4; matrix products, arithmetic and copies ran while one was open for 27% -> 0% of each run, Pallas kernels for 0% -> 13%
where the time goes in v1:
time: 82.2 us; the launch traced here: 80.6 us
  Pallas kernels  27.3 us (33%)
  blocking collectives  26.9 us (33%)
  starting transfers between devices  12.4 us (15%)
  waiting for transfers between devices  8.5 us (10%)
  local copies, waits for them, and re-layouts  4.85 us (6%)
    all_to_all x1, blocking collectives, on_device(): mine = lax.all_to_all(packed, ('y', 'head'), 0, 0, tiled=True)  13.5 us
    all_to_all x1, blocking collectives, on_device(): grads = lax.all_to_all(hg, ('y', 'head'), 0, 0, tiled=True)  13.4 us
    pallas_call x1, Pallas kernels, on_device(): call(attn_body, [arr(dq_shape), arr((supers, LANES), F32)] + [arr((supers...  12.9 us
    ppermute x4, starting transfers between devices, spread(): lax.ppermute(parts[2 * d - 2 + phase], 'z', swap_pairs(z_count, d, phase))  7.74 us
    pallas_call x1, Pallas kernels, on_device(): call(conv_body, [arr((heads_axis, rows, out_cols)), arr((members, half, L...  6.57 us
    ppermute x1, waiting for transfers between devices, on_device(): other = lax.ppermute(send, 'y', [(0, 1), (1, 0)])  5.02 us
    unnamed x17, local copies, waits for them, and re-layouts  4.84 us
    all_to_all x1, starting transfers between devices, on_device(): lax.all_to_all(dres, 'head', 0, 0, tiled=True).reshape(1, block, out_cols)  3.42 us
  transfers between devices with their start and end apart: 8, of which 4 were waited for; matrix products, arithmetic and copies ran while one was open for 0% of the time, Pallas kernels for 13%

profile of v1, /device:TPU:0, one launch (start us, length us, event | category | flops | bytes accessed | tf_op | source)
XLA Modules:
  0.0 80.6 jit_solution(5983077245273831506)
XLA Ops:
  0.6 2.1 %pack.1 = bf16[8,192,128]{2,1,0:T(8,128)(2,1)} custom-call(bf16[1,128,512]{2,1,0:T(8,128)(2,1)} %q_ref.1, bf16[1,128,512]{2,1,0:T(8,128)(2,1)} %k_ref.1, bf16[1,128,512]{2,1,0:T(8,128)(2,1)} %v_ref.1), custom_call_target="tpu_custom_call" | custom-call | tf_op jit(solution)/shard_map/pack/pallas_call | solution.py:111
  2.7 13.5 %all_to_all.15.refs_1_ = bf16[8,192,128]{2,1,0:T(8,128)(2,1)S(1)} all-to-all(bf16[8,192,128]{2,1,0:T(8,128)(2,1)} %pack.1), channel_id=1, replica_groups=mesh['head'=4,'z'=4,'y'=2] {'y','head'}, dimensions={0} | all-to-all | bytes 786432 | tf_op jit(solution)/shard_map/all_to_all | solution.py:112
  16.2 0.0 copy-start
  16.2 0.7 collective-permute-start.3
  16.9 4.4 %collective-permute-start.2 = (bf16[1024,128]{1,0:T(8,128)(2,1)S(1)}, bf16[1024,128]{1,0:T(8,128)(2,1)S(1)}, u32[]{:S(2)}, u32[]{:S(2)}) collective-permute-start(bf16[1024,128]{1,0:T(8,128)(2,1)S(1)} %bitcast.4), channel_id=1, source_target_pairs={{0,2},{2,0},{4,6},{6,4},{1,3},{3,1},{5,7},{7,5},{8,10},{10,8},{12,... | collective-permute-start | bytes 786440 | tf_op jit(solution)/shard_map/ppermute | solution.py:175
  21.3 1.7 %edges.1 = (bf16[48,1024]{1,0:T(8,128)(2,1)}, bf16[48,1024]{1,0:T(8,128)(2,1)}) custom-call(bf16[1,128,1024]{2,1,0:T(8,128)(2,1)} %resid_ref.3, bf16[1,128,1024]{2,1,0:T(8,128)(2,1)} %grad_ref.3), custom_call_target="tpu_custom_call" | custom-call | tf_op jit(solution)/shard_map/edges/pallas_call | solution.py:89
  23.1 0.0 copy-done
  23.1 0.0 collective-permute-start
  23.1 0.7 collective-permute-start.1
  23.7 0.8 %collective-permute-done.first_ref = bf16[48,1024]{1,0:T(8,128)(2,1)S(1)} collective-permute-done((bf16[48,1024]{1,0:T(8,128)(2,1)}, bf16[48,1024]{1,0:T(8,128)(2,1)S(1)}, u32[]{:S(2)}, u32[]{:S(2)}) %collective-permute-start) | collective-permute-done | bytes 98336 | tf_op jit(solution)/shard_map/ppermute | solution.py:95
  24.6 0.0 copy-start.6
  24.6 0.0 collective-permute-done.1.second_ref
  24.6 0.6 copy-done.6
  25.2 0.0 copy-start.7
  25.2 0.6 copy-done.7
  25.9 6.6 %conv.1 = (bf16[4,128,256]{2,1,0:T(8,128)(2,1)}, bf16[8,64,128]{2,1,0:T(8,128)(2,1)}) custom-call(bf16[1,128,1024]{2,1,0:T(8,128)(2,1)} %resid_ref.3, bf16[1,128,1024]{2,1,0:T(8,128)(2,1)} %grad_ref.3, bf16[48,1024]{1,0:T(8,128)(2,1)} %copy-done.6, bf16[48,1024]{1,0:T(8,128)(2,1)} %copy-done.7, bf16[31,1024]{1,0:T(8,128)(2,1)} %taps_ref.1, ...), custom_call_target="tpu_custom_call" | custom-call | tf_op jit(solution)/shard_map/conv/pallas_call | solution.py:162
  32.4 13.4 %all_to_all.16.refs_2_ = bf16[8,64,128]{2,1,0:T(8,128)(2,1)} all-to-all(bf16[8,64,128]{2,1,0:T(8,128)(2,1)} %get-tuple-element.20), channel_id=1, replica_groups=mesh['head'=4,'z'=4,'y'=2] {'y','head'}, dimensions={0} | all-to-all | bytes 262144 | tf_op jit(solution)/shard_map/all_to_all | solution.py:169
  45.8 0.0 collective-permute-done.3.refs_4_
  45.8 0.0 copy-start.1
  45.8 0.0 collective-permute-done.2.refs_3_
  45.8 0.7 copy-done.1
  46.5 0.0 copy-start.2
  46.5 0.7 copy-done.2
  47.2 12.9 %attn.1 = (bf16[2,256,128]{2,1,0:T(8,128)(2,1)}, f32[1024,128]{1,0:T(8,128)}, bf16[1024,128]{1,0:T(8,128)(2,1)}, bf16[1024,128]{1,0:T(8,128)(2,1)}) custom-call(s32[8]{0:T(128)} %refs_0_.1, bf16[8,192,128]{2,1,0:T(8,128)(2,1)} %copy-done, bf16[8,64,128]{2,1,0:T(8,128)(2,1)} %all_to_all.16.refs_2_, bf16[1024,128]{1,0:T(8,128)(2,1)} %copy-done.2, ...), custom_call_target="tpu_custom_call" | custom-call | tf_op jit(solution)/shard_map/attn/pallas_call | solution.py:300
  60.1 1.9 %collective-permute-start.4 = (bf16[1024,128]{1,0:T(8,128)(2,1)}, bf16[1024,128]{1,0:T(8,128)(2,1)S(1)}, u32[]{:S(2)}, u32[]{:S(2)}) collective-permute-start(bf16[1024,128]{1,0:T(8,128)(2,1)} %get-tuple-element.23), channel_id=1, source_target_pairs={{0,2},{2,0},{4,6},{6,4},{1,3},{3,1},{5,7},{7,5},{8,10},{10,8},{12,... | collective-permute-start | bytes 786440 | tf_op jit(solution)/shard_map/ppermute | solution.py:175
  62.0 0.7 collective-permute-start.5
  62.7 3.4 %all-to-all-start = ((bf16[4,128,256]{2,1,0:T(8,128)(2,1)}), bf16[4,128,256]{2,1,0:T(8,128)(2,1)S(1)}, u32[]{:S(2)}, u32[]{:S(2)}) async-start(bf16[4,128,256]{2,1,0:T(8,128)(2,1)} %get-tuple-element.19), calls=%async_computation | async-start | bytes 524288 | tf_op jit(solution)/shard_map/all_to_all | solution.py:181
  66.1 2.2 %collective-permute-done.4.refs_2_ = bf16[1024,128]{1,0:T(8,128)(2,1)S(1)} collective-permute-done((bf16[1024,128]{1,0:T(8,128)(2,1)}, bf16[1024,128]{1,0:T(8,128)(2,1)S(1)}, u32[]{:S(2)}, u32[]{:S(2)}) %collective-permute-start.4) | collective-permute-done | bytes 262176 | tf_op jit(solution)/shard_map/ppermute | solution.py:175
  68.4 0.0 copy-start.3
  68.4 0.0 collective-permute-done.5.refs_3_
  68.4 0.0 copy-start.4
  68.4 0.7 copy-done.3
  69.1 0.1 copy-done.4
  69.1 2.0 %sum.1 = (bf16[768,128]{1,0:T(8,128)(2,1)}, bf16[768,128]{1,0:T(8,128)(2,1)}) custom-call(bf16[2,256,128]{2,1,0:T(8,128)(2,1)} %get-tuple-element.21.refs_0_, f32[1024,128]{1,0:T(8,128)} %get-tuple-element.22.refs_1_, bf16[1024,128]{1,0:T(8,128)(2,1)} %copy-done.3, bf16[1024,128]{1,0:T(8,128)(2,1)} %copy-done.4), custom_call_target="tpu_custom_call" | custom-call | tf_op jit(solution)/shard_map/sum/pallas_call | solution.py:348
  71.2 0.6 collective-permute-start.6
  71.7 0.4 all-to-all-done
  72.1 5.0 %collective-permute-done.6.other_ref = bf16[768,128]{1,0:T(8,128)(2,1)S(1)} collective-permute-done((bf16[768,128]{1,0:T(8,128)(2,1)}, bf16[768,128]{1,0:T(8,128)(2,1)S(1)}, u32[]{:S(2)}, u32[]{:S(2)}) %collective-permute-start.6) | collective-permute-done | bytes 196640 | tf_op jit(solution)/shard_map/ppermute | solution.py:349
  77.2 0.0 copy-start.5
  77.2 0.7 copy-done.5
  77.8 2.0 %last.1 = (bf16[1,512,128]{2,1,0:T(8,128)(2,1)}, bf16[1,512,128]{2,1,0:T(8,128)(2,1)}, bf16[1,512,128]{2,1,0:T(8,128)(2,1)}) custom-call(bf16[768,128]{1,0:T(8,128)(2,1)} %get-tuple-element.25.keep_ref, bf16[768,128]{1,0:T(8,128)(2,1)} %copy-done.5), custom_call_target="tpu_custom_call" | custom-call | tf_op jit(solution)/shard_map/last/pallas_call | solution.py:372
  79.9 0.7 copy.13
  (1 shorter events, 0.0 us)
Async XLA Ops:
  16.2 6.9 %copy-start = (bf16[8,192,128]{2,1,0:T(8,128)(2,1)}, bf16[8,192,128]{2,1,0:T(8,128)(2,1)S(1)}, u32[]{:S(2)}) copy-start(bf16[8,192,128]{2,1,0:T(8,128)(2,1)S(1)} %all_to_all.15.refs_1_) | copy-start | bytes 1179652
  16.2 29.6 %collective-permute-start.3 = (bf16[1024,128]{1,0:T(8,128)(2,1)S(1)}, bf16[1024,128]{1,0:T(8,128)(2,1)S(1)}, u32[]{:S(2)}, u32[]{:S(2)}) collective-permute-start(bf16[1024,128]{1,0:T(8,128)(2,1)S(1)} %bitcast.3), channel_id=1, source_target_pairs={{2,4},{4,2},{3,5},{5,3},{10,12},{12,10},{11,13},{13,11},{18,20},{2... | collective-permute-start | bytes 786440 | tf_op jit(solution)/shard_map/ppermute | solution.py:175
  16.9 28.9 %collective-permute-start.2 = (bf16[1024,128]{1,0:T(8,128)(2,1)S(1)}, bf16[1024,128]{1,0:T(8,128)(2,1)S(1)}, u32[]{:S(2)}, u32[]{:S(2)}) collective-permute-start(bf16[1024,128]{1,0:T(8,128)(2,1)S(1)} %bitcast.4), channel_id=1, source_target_pairs={{0,2},{2,0},{4,6},{6,4},{1,3},{3,1},{5,7},{7,5},{8,10},{10,8},{12,... | collective-permute-start | bytes 786440 | tf_op jit(solution)/shard_map/ppermute | solution.py:175
  23.1 1.5 %collective-permute-start = (bf16[48,1024]{1,0:T(8,128)(2,1)}, bf16[48,1024]{1,0:T(8,128)(2,1)S(1)}, u32[]{:S(2)}, u32[]{:S(2)}) collective-permute-start(bf16[48,1024]{1,0:T(8,128)(2,1)} %get-tuple-element.17), channel_id=1, source_target_pairs={{0,8},{8,0},{16,24},{24,16},{1,9},{9,1},{17,25},{25,17},{2,10},{10... | collective-permute-start | bytes 294920 | tf_op jit(solution)/shard_map/ppermute | solution.py:95
  23.1 1.5 %collective-permute-start.1 = (bf16[48,1024]{1,0:T(8,128)(2,1)}, bf16[48,1024]{1,0:T(8,128)(2,1)S(1)}, u32[]{:S(2)}, u32[]{:S(2)}) collective-permute-start(bf16[48,1024]{1,0:T(8,128)(2,1)} %get-tuple-element.18), channel_id=1, source_target_pairs={{8,16},{16,8},{24,1},{1,24},{9,17},{17,9},{25,2},{2,25},{10,18},{1... | collective-permute-start | bytes 294920 | tf_op jit(solution)/shard_map/ppermute | solution.py:95
  24.6 0.6 copy-start.6
  25.2 0.6 copy-start.7
  45.8 0.7 copy-start.1
  46.5 0.7 copy-start.2
  60.1 8.3 %collective-permute-start.4 = (bf16[1024,128]{1,0:T(8,128)(2,1)}, bf16[1024,128]{1,0:T(8,128)(2,1)S(1)}, u32[]{:S(2)}, u32[]{:S(2)}) collective-permute-start(bf16[1024,128]{1,0:T(8,128)(2,1)} %get-tuple-element.23), channel_id=1, source_target_pairs={{0,2},{2,0},{4,6},{6,4},{1,3},{3,1},{5,7},{7,5},{8,10},{10,8},{12,... | collective-permute-start | bytes 786440 | tf_op jit(solution)/shard_map/ppermute | solution.py:175
  62.0 6.3 %collective-permute-start.5 = (bf16[1024,128]{1,0:T(8,128)(2,1)}, bf16[1024,128]{1,0:T(8,128)(2,1)S(1)}, u32[]{:S(2)}, u32[]{:S(2)}) collective-permute-start(bf16[1024,128]{1,0:T(8,128)(2,1)} %get-tuple-element.24), channel_id=1, source_target_pairs={{2,4},{4,2},{3,5},{5,3},{10,12},{12,10},{11,13},{13,11},{18,20},{2... | collective-permute-start | bytes 786440 | tf_op jit(solution)/shard_map/ppermute | solution.py:175
  62.7 9.4 %all-to-all-start = ((bf16[4,128,256]{2,1,0:T(8,128)(2,1)}), bf16[4,128,256]{2,1,0:T(8,128)(2,1)S(1)}, u32[]{:S(2)}, u32[]{:S(2)}) async-start(bf16[4,128,256]{2,1,0:T(8,128)(2,1)} %get-tuple-element.19), calls=%async_computation | async-start | bytes 524288 | tf_op jit(solution)/shard_map/all_to_all | solution.py:181
  68.4 0.7 copy-start.3
  68.4 0.8 copy-start.4
  71.2 6.0 %collective-permute-start.6 = (bf16[768,128]{1,0:T(8,128)(2,1)}, bf16[768,128]{1,0:T(8,128)(2,1)S(1)}, u32[]{:S(2)}, u32[]{:S(2)}) collective-permute-start(bf16[768,128]{1,0:T(8,128)(2,1)} %get-tuple-element.26), channel_id=1, source_target_pairs={{0,1},{1,0},{2,3},{3,2},{4,5},{5,4},{6,7},{7,6},{8,9},{9,8},{10,11... | collective-permute-start | bytes 589832 | tf_op jit(solution)/shard_map/ppermute | solution.py:349
  77.2 0.7 copy-start.5

commit v2 on v1

v2 whole, which is shorter than its diff:
```python
import jax
import jax.numpy as jnp
from jax import lax
from jax.experimental import pallas as pl
from jax.experimental.pallas import tpu as pltpu
from jax.sharding import Mesh
from jax.sharding import PartitionSpec as P

HEAD_DIM = 64
KERNEL = 31
REACH = 2
LANES = 128
QT = 256
HALO = 32
HALF = 16
NEG = -1e30
F32 = jnp.float32
BF16 = jnp.bfloat16
NT_DIMS = (((1,), (1,)), ((), ()))
NN_DIMS = (((1,), (0,)), ((), ()))
VMEM_LIMIT = 12 * 1024 * 1024
CONV_COST = (6_000_000_000, 0, 0)
SCORES_COST = (9_000_000_000, 0, 0)
FAR_COST = (4_000_000_000, 0, 0)
NEAR_COST = (4_000_000_000, 0, 0)


def dot(a, b, dims):
    return lax.dot_general(a, b, dims, preferred_element_type=F32)


def call(body, outs, smem=(), scratch=(), name=None, cost=None):
    on_vmem = pl.BlockSpec(memory_space=pltpu.VMEM)
    on_smem = pl.BlockSpec(memory_space=pltpu.SMEM)

    def run(*args):
        return pl.pallas_call(
            body,
            out_shape=outs,
            in_specs=[on_smem if i in smem else on_vmem for i in range(len(args))],
            out_specs=[on_vmem] * len(outs),
            scratch_shapes=list(scratch),
            compiler_params=pltpu.CompilerParams(vmem_limit_bytes=VMEM_LIMIT),
            cost_estimate=None if cost is None else pl.CostEstimate(*cost),
            name=name,
        )(*args)

    return run


def arr(shape, dtype=BF16):
    return jax.ShapeDtypeStruct(shape, dtype)


def vmem(shape, dtype=BF16):
    return pltpu.VMEM(shape, dtype)


def on_chip(*arrays):
    return [pltpu.with_memory_space_constraint(x, pltpu.VMEM) for x in arrays]


def in_hbm(*arrays):
    return [pltpu.with_memory_space_constraint(x, pltpu.HBM) for x in arrays]


def swap_pairs(count, distance, phase):
    pairs = []
    for i in range(count - distance):
        if (i // distance) % 2 == phase:
            pairs += [(i, i + distance), (i + distance, i)]
    return pairs


def on_device(sizes, query, key, value, resid_in, out_grad, out_weight, conv_kernel, frame_lengths):
    heads_axis, z_count, group = sizes
    ctx_count = z_count * group
    rows = query.shape[1]
    width = query.shape[2]
    channels = resid_in.shape[2]
    block = rows * heads_axis
    supers = group * block
    members = group * heads_axis
    chips = members // 2
    half = rows // 2
    near = -(-REACH // group)
    window = REACH * block
    tiles = 2 * window // QT + 1
    per_block = block // QT
    lead = near * supers - window
    ext = (2 * near + 1) * supers
    out_cols = channels // heads_axis
    scale = HEAD_DIM ** (-0.5)
    chain = heads_axis * ctx_count

    def head_of(member):
        return group * (member % heads_axis) + member // heads_axis

    def cols(head):
        return slice(head * HEAD_DIM, (head + 1) * HEAD_DIM)

    def sides(core, slots):
        first, second = slots
        return jnp.where(core == 0, first, second), jnp.where(core == 0, second, first)

    def member_of(chip, core):
        return chip * 2 + core

    def my_chip():
        return lax.axis_index("y") * (heads_axis // 2) + lax.axis_index("head") // 2

    def my_core():
        return lax.axis_index("head") % 2

    def pack_body(
        q_ref, k_ref, v_ref, resid_ref, grad_ref, taps_ref, weight_ref,
        keep_ref, send_ref, first_ref, second_ref, resid_out, grad_out, taps_out, weight_out, sems,
    ):
        copies = [
            pltpu.make_async_copy(source, target, sems.at[i])
            for i, (source, target) in enumerate(
                ((resid_ref, resid_out), (grad_ref, grad_out), (taps_ref, taps_out), (weight_ref, weight_out))
            )
        ]
        for copy in copies:
            copy.start()
        core = my_core()
        for chip in range(chips):
            heads = [cols(head_of(member_of(chip, c))) for c in (0, 1)]
            for at, width, c_ref, low, high in (
                (0, 0, k_ref, 0, rows),
                (0, HEAD_DIM, v_ref, 0, rows),
                (rows, 0, q_ref, 0, half),
                (rows, HEAD_DIM, q_ref, half, rows),
            ):
                stay, leave = sides(core, [c_ref[0, low:high, c] for c in heads])
                keep_ref[chip, at : at + high - low, width : width + HEAD_DIM] = stay
                send_ref[chip, at : at + high - low, width : width + HEAD_DIM] = leave
        copies[0].wait()
        copies[1].wait()
        odd = core == 1
        for side_ref, low in ((first_ref, odd), (second_ref, jnp.logical_not(odd))):
            side_ref[0:HALO, :] = jnp.where(low, resid_out[0, 0:HALO, :], resid_out[0, rows - HALO : rows, :])
            side_ref[HALO : HALO + HALF, :] = jnp.where(
                low, grad_out[0, 0:HALF, :], grad_out[0, rows - HALF : rows, :]
            )
        copies[2].wait()
        copies[3].wait()

    slot = rows + half
    raw = pl.BlockSpec(memory_space=pltpu.HBM)
    on_vmem = pl.BlockSpec(memory_space=pltpu.VMEM)
    pack_outs = [
        vmem((chips, slot, LANES)), vmem((chips, slot, LANES)),
        vmem((HALO + HALF, channels)), vmem((HALO + HALF, channels)),
        vmem((1, rows, channels)), vmem((1, rows, channels)),
        vmem(conv_kernel.shape), vmem(out_weight.shape),
    ]
    keep, send, first, second, resid, upstream, taps_in, weight_in = pl.pallas_call(
        pack_body,
        out_shape=pack_outs,
        in_specs=[on_vmem] * 3 + [raw] * 4,
        out_specs=[on_vmem] * 8,
        scratch_shapes=[pltpu.SemaphoreType.DMA((4,))],
        compiler_params=pltpu.CompilerParams(vmem_limit_bytes=VMEM_LIMIT),
        name="pack",
    )(*in_hbm(query, key, value, resid_in, out_grad, conv_kernel, out_weight))

    mesh_axes = ("head", "z", "y")

    def place(head, z, y):
        return head * ctx_count + z * group + y

    def everyone(target):
        return [
            (place(h, z, y), place(*target(h, z, y)))
            for h in range(heads_axis)
            for z in range(z_count)
            for y in range(group)
        ]

    def core_swap(x):
        return lax.ppermute(x, mesh_axes, everyone(lambda h, z, y: (h ^ 1, z, y)))

    def exchange(keep, got, count, index, name):
        def body(keep_ref, got_ref, *out_refs):
            me = index()
            for m, out_ref in enumerate(out_refs, 1):
                out_ref[0] = keep_ref[me ^ m]
                out_ref[1] = got_ref[me ^ m]

        per_row = heads_axis // 2

        def target(m):
            def f(h, z, y):
                chip = (y * per_row + h // 2) ^ m
                return (chip % per_row) * 2 + h % 2, z, chip // per_row

            return f

        parts = call(body, [vmem((2,) + keep.shape[1:])] * (count - 1), name=name)(*on_chip(keep, got))
        return [lax.ppermute(part, mesh_axes, everyone(target(m))) for m, part in enumerate(parts, 1)]

    def arrivals(me, core, keep_ref, got_ref, part_refs):
        out = [(member_of(me, core), lambda: keep_ref[me]), (member_of(me, 1 - core), lambda: got_ref[me])]
        for m, ref in enumerate(part_refs, 1):
            out.append((member_of(me ^ m, core), lambda ref=ref: ref[0]))
            out.append((member_of(me ^ m, 1 - core), lambda ref=ref: ref[1]))
        return out

    got = core_swap(send)

    def chain_place(i):
        return place(i % heads_axis, i // heads_axis // group, i // heads_axis % group)

    halos = [
        lax.ppermute(side, mesh_axes, [(chain_place(a), chain_place(b)) for a, b in swap_pairs(chain, 1, phase)])
        for phase, side in enumerate((first, second))
    ]
    mine = [keep, got] + exchange(keep, got, chips, my_chip, "regroup")

    def keys_body(keep_ref, got_ref, *refs):
        out_ref = refs[-1]
        for member, take in arrivals(my_chip(), my_core(), keep_ref, got_ref, refs[:-1]):
            out_ref[pl.ds(pl.multiple_of(member * rows, rows), rows), :] = take()[0:rows]

    (both,) = call(keys_body, [vmem((supers, LANES))], name="keys")(*on_chip(*mine))

    steps = [(d, phase) for d in range(1, near + 1) for phase in (0, 1)]
    around = [lax.ppermute(both, "z", swap_pairs(z_count, d, phase)) for d, phase in steps]

    span = rows + 2 * HALF

    def conv_body(
        resid_ref, grad_ref, first_ref, second_ref, taps_ref, weight_ref,
        hg_keep, hg_send, dres_keep, dres_send, low_ref,
    ):
        odd = (lax.axis_index("head") % 2) == 1

        def taps_sum(x, tap_of, length):
            total = None
            for b in range(8):
                part = None
                for a in range(4):
                    offset = 8 * a + b
                    if offset < 1 or offset > KERNEL:
                        continue
                    term = tap_of(offset - 1) * x[8 * a : 8 * a + length + 8]
                    part = term if part is None else part + term
                if b:
                    part = pltpu.roll(part, length + 8 - b, 0)
                part = part[0:length]
                total = part if total is None else total + part
            return total

        def chunk(c, carry):
            at = pl.multiple_of(c * LANES, LANES)
            lane = pl.ds(at, LANES)
            first = first_ref[:, lane].astype(F32)
            second = second_ref[:, lane].astype(F32)
            before = jnp.where(odd, first, second)
            after = jnp.where(odd, second, first)
            taps = taps_ref[:, lane].astype(F32)
            x = jnp.concatenate([before[0:HALO], resid_ref[0, :, lane].astype(F32), after[0:HALO]], axis=0)
            middle = grad_ref[0, :, lane].astype(F32)
            g = jnp.concatenate([before[HALO:], middle, after[HALO:]], axis=0)
            pre = taps_sum(x, lambda k: taps[k : k + 1], span)
            s = 1.0 / (1.0 + jnp.exp(-pre))
            cg = g * (s * (1.0 + pre * (1.0 - s)))
            out = middle + taps_sum(cg, lambda k: taps[KERNEL - 1 - k : KERNEL - k], rows)
            low_ref[:, lane] = out.astype(BF16)
            return carry

        lax.fori_loop(0, channels // LANES, chunk, 0)
        core = my_core()
        for x in range(heads_axis // 2):
            dres_keep[x], dres_send[x] = sides(
                core, [low_ref[:, h * out_cols : (h + 1) * out_cols] for h in (2 * x, 2 * x + 1)]
            )
        hg = dot(low_ref[...], weight_ref[...], NT_DIMS).astype(BF16)
        for chip in range(chips):
            heads = [cols(head_of(member_of(chip, c))) for c in (0, 1)]
            for at, part in ((0, slice(0, half)), (HEAD_DIM, slice(half, rows))):
                stay, leave = sides(core, [hg[part, c] for c in heads])
                hg_keep[chip, :, at : at + HEAD_DIM] = stay
                hg_send[chip, :, at : at + HEAD_DIM] = leave

    hg_keep, hg_send, dres_keep, dres_send = call(
        conv_body,
        [vmem((chips, half, LANES))] * 2 + [vmem((heads_axis // 2, rows, out_cols))] * 2,
        scratch=[pltpu.VMEM((rows, channels), BF16)],
        name="conv",
        cost=CONV_COST,
    )(*on_chip(resid, upstream, *halos, taps_in, weight_in))
    hg_got = core_swap(hg_send)
    grads = [hg_keep, hg_got] + exchange(hg_keep, hg_got, chips, my_chip, "regroup_grads")
    dres_got = core_swap(dres_send)
    dres = [dres_keep, dres_got] + exchange(
        dres_keep, dres_got, heads_axis // 2, lambda: lax.axis_index("head") // 2, "regroup_resid"
    )
    n_dres = len(dres)
    dres_shape = arr((1, block, out_cols))

    def resid_out(refs, out_ref):
        for member, take in arrivals(lax.axis_index("head") // 2, my_core(), refs[0], refs[1], refs[2:]):
            out_ref[0, pl.ds(pl.multiple_of(member * rows, rows), rows), :] = take()

    q_tiles = supers // QT
    k_tiles = ext // QT
    first_tile = lead // QT
    own_tiles = range(near * q_tiles, (near + 1) * q_tiles)

    def seen(a):
        return range(a + first_tile, a + first_tile + tiles)

    def at_tile(t):
        return slice(t * QT, (t + 1) * QT)

    def score_body(*refs):
        len_ref, both_ref = refs[:2]
        mine_refs = refs[2 : 3 + chips]
        around_refs = refs[3 + chips : 3 + chips + 2 * near]
        e_ref, inv_ref, out_ref, kv, kvt, qz, kb, qs = refs[3 + chips + 2 * near :]
        z = lax.axis_index("z")
        low = lax.broadcasted_iota(jnp.int32, (half, LANES), 1) < HEAD_DIM
        lane = lax.broadcasted_iota(jnp.int32, (half, LANES), 1)
        kv[near * supers : (near + 1) * supers, :] = both_ref[...]
        for member, take in arrivals(my_chip(), my_core(), mine_refs[0], mine_refs[1], mine_refs[2:]):
            q = take()[rows:slot].astype(F32) * scale
            for i, part in enumerate((q, pltpu.roll(q, HEAD_DIM, 1))):
                at = pl.ds(pl.multiple_of(member * rows + i * half, half), half)
                part = jnp.where(low, part, 0.0)
                qz[at, :] = part.astype(BF16)
                qs[at, :] = jnp.where(lane == HEAD_DIM, 1.0, part).astype(BF16)
        for d in range(1, near + 1):
            left, right = (near - d) * supers, (near + d) * supers
            odd = ((z // d) % 2) == 1

            @pl.when(odd)
            def _():
                kv[left : left + supers, :] = around_refs[2 * d - 2][...]
                kv[right : right + supers, :] = around_refs[2 * d - 1][...]

            @pl.when(jnp.logical_not(odd))
            def _():
                kv[left : left + supers, :] = around_refs[2 * d - 1][...]
                kv[right : right + supers, :] = around_refs[2 * d - 2][...]

        def limit(t):
            index = (z - near) * group + t // per_block
            inside = jnp.logical_and(index >= 0, index < ctx_count)
            length = len_ref[jnp.clip(index, 0, ctx_count - 1)]
            return jnp.where(inside, length, 0) - (t % per_block) * QT

        tile_lane = lax.broadcasted_iota(jnp.int32, (QT, LANES), 1)
        tile_row = lax.broadcasted_iota(jnp.int32, (QT, LANES), 0)

        def turn(t, carry):
            at = pl.ds(pl.multiple_of(t * QT, QT), QT)
            tile = kv[at, :].astype(F32)
            kvt[t] = jnp.transpose(tile).astype(BF16)
            dead = jnp.logical_and(tile_lane == HEAD_DIM, tile_row >= limit(t))
            kb[at, :] = jnp.where(tile_lane < HEAD_DIM, tile, jnp.where(dead, NEG, 0.0)).astype(BF16)
            return carry

        lax.fori_loop(0, k_tiles, turn, 0)
        key_at = lax.broadcasted_iota(jnp.int32, (QT, QT), 0)
        query_at = lax.broadcasted_iota(jnp.int32, (QT, QT), 1)

        def fold(x, op):
            return op(x.reshape(QT // 8, 8, QT), axis=0)

        def query_tile(a, carry):
            q = qs[pl.ds(pl.multiple_of(a * QT, QT), QT), :]
            e_at = a * tiles
            top = jnp.full((8, QT), NEG, F32)
            for j in range(tiles):
                t = a + j + first_tile
                s = dot(kb[pl.ds(pl.multiple_of(t * QT, QT), QT), :], q, NT_DIMS)
                if j == 0:
                    s = jnp.where(key_at >= query_at, s, NEG)
                if j == tiles - 1:
                    s = jnp.where(key_at <= query_at, s, NEG)
                e_ref[e_at + j] = s
                top = jnp.maximum(top, fold(s, jnp.max))
            top = jnp.max(top, axis=0, keepdims=True)
            mass = jnp.zeros((8, QT), F32)
            out = jnp.zeros((HEAD_DIM, QT), F32)
            for j in range(tiles):
                e = jnp.exp(e_ref[e_at + j] - top)
                e_ref[e_at + j] = e
                mass = mass + fold(e, jnp.sum)
                out = out + dot(kvt[a + j + first_tile, HEAD_DIM:LANES, :], e.astype(BF16), NN_DIMS)
            inverse = 1.0 / jnp.sum(mass, axis=0, keepdims=True)
            inv_ref[a] = inverse
            out_ref[a] = out * inverse
            return carry

        lax.fori_loop(0, q_tiles, query_tile, 0)

    exps, inverse, outs, kv, kvt, qz = call(
        score_body,
        [
            vmem((q_tiles * tiles, QT, QT), F32),
            vmem((q_tiles, 1, QT), F32),
            vmem((q_tiles, HEAD_DIM, QT), F32),
            vmem((ext, LANES)),
            vmem((k_tiles, LANES, QT)),
            vmem((supers, LANES)),
        ],
        smem=(0,),
        scratch=[pltpu.VMEM((ext, LANES), BF16), pltpu.VMEM((supers, LANES), BF16)],
        name="scores",
        cost=SCORES_COST,
    )(frame_lengths, *on_chip(both, *mine, *around))

    def key_tile(t, e_ref, inv_ref, delta_ref, kv, kvt, qz, hz, dq):
        total = None
        for a in range(q_tiles):
            if t not in seen(a):
                continue
            q = qz[at_tile(a), :]
            g = hz[at_tile(a), :]
            p = e_ref[a * tiles + t - a - first_tile] * inv_ref[a]
            slopes = dot(kv[at_tile(t), :], g, NT_DIMS)
            ds = (p * (slopes - delta_ref[a])).astype(BF16)
            part = dot(ds, q, NN_DIMS) + dot(p.astype(BF16), g, NN_DIMS)
            total = part if total is None else total + part
            dq[a] += dot(kvt[t, 0:HEAD_DIM, :], ds, NN_DIMS)
        return jnp.zeros((QT, LANES), F32) if total is None else total

    n_back = 2 * near * group

    def far_body(*refs):
        grad_refs = refs[: 1 + chips]
        e_ref, inv_ref, out_ref, kv, kvt, qz, hz, delta_ref, dq = refs[1 + chips : 10 + chips]
        back_refs = refs[10 + chips : -1]
        acc = refs[-1]
        z, y = lax.axis_index("z"), lax.axis_index("y")
        low = lax.broadcasted_iota(jnp.int32, (half, LANES), 1) < HEAD_DIM
        for member, take in arrivals(my_chip(), my_core(), grad_refs[0], grad_refs[1], grad_refs[2:]):
            g = take().astype(F32)
            for i, part in enumerate((pltpu.roll(g, HEAD_DIM, 1), g)):
                at = pl.ds(pl.multiple_of(member * rows + i * half, half), half)
                hz[at, :] = jnp.where(low, 0.0, part).astype(BF16)
        for a in range(q_tiles):
            g = jnp.transpose(hz[at_tile(a), :].astype(F32))[HEAD_DIM:LANES]
            delta_ref[a] = jnp.sum(g * out_ref[a], axis=0, keepdims=True)
        dq[...] = jnp.zeros_like(dq)
        for t in range(k_tiles):
            if t not in own_tiles:
                acc[at_tile(t), :] = key_tile(t, e_ref, inv_ref, delta_ref, kv, kvt, qz, hz, dq)
        for i, (d, phase) in enumerate(steps):
            odd = ((z // d) % 2) == 1
            right = odd if phase else jnp.logical_not(odd)
            side = jnp.where(right, near + d, near - d) * supers
            for cross in range(group):
                slot = jnp.where(cross == 1, 1 - y, y)
                take = pl.ds(pl.multiple_of(side + slot * block, block), block)
                back_refs[i * group + cross][...] = acc[take, :].astype(BF16)

    far = call(
        far_body,
        [vmem((supers, LANES)), vmem((q_tiles, 1, QT), F32), vmem((q_tiles, HEAD_DIM, QT), F32)]
        + [vmem((block, LANES))] * n_back,
        scratch=[pltpu.VMEM((ext, LANES), F32)],
        name="far",
        cost=FAR_COST,
    )(*on_chip(*grads, exps, inverse, outs, kv, kvt, qz))
    hz, delta, dq_far = far[:3]

    def across(d, phase, cross):
        return [
            (a * group + i, b * group + (i ^ cross))
            for a, b in swap_pairs(z_count, d, phase)
            for i in range(group)
        ]

    back = [
        lax.ppermute(far[3 + i * group + cross], ("z", "y"), across(d, phase, cross))
        for i, (d, phase) in enumerate(steps)
        for cross in range(group)
    ]

    hb = block // 2
    sent = (group - 1) * (block + hb)

    def near_body(*refs):
        e_ref, inv_ref, delta_ref, kv, kvt, qz, hz, far_ref = refs[:8]
        keep_ref, dq_ref = refs[8:10]
        acc, dq, dq_sc = refs[-3:]
        y = lax.axis_index("y")
        dq[...] = far_ref[...]
        for t in own_tiles:
            acc[at_tile(t - near * q_tiles), :] = key_tile(t, e_ref, inv_ref, delta_ref, kv, kvt, qz, hz, dq)
        for a in range(q_tiles):
            dq_sc[at_tile(a), 0:HEAD_DIM] = jnp.transpose(dq[a] * scale)
        if group == 1:
            keep_ref[...] = acc[...]
            dq_ref[0] = dq_sc[:, 0:HEAD_DIM].astype(BF16)
            return
        send_ref = refs[10]
        keep_at = pl.multiple_of(y * block, block)
        send_at = pl.multiple_of((1 - y) * block, block)
        keep_ref[...] = acc[pl.ds(keep_at, block), :]
        send_ref[0:block, :] = acc[pl.ds(send_at, block), :].astype(BF16)
        for ref, at, base in ((dq_ref, keep_at, 0), (send_ref, send_at, block)):
            upper = dq_sc[pl.ds(at, hb), 0:HEAD_DIM]
            lower = dq_sc[pl.ds(pl.multiple_of(at + hb, hb), hb), 0:HEAD_DIM]
            ref[base : base + hb, :] = jnp.concatenate([upper, lower], axis=1).astype(BF16)

    results = call(
        near_body,
        [vmem((block, LANES), F32)]
        + ([arr((1, block, HEAD_DIM))] if group == 1 else [vmem((hb, LANES)), vmem((sent, LANES))]),
        scratch=[
            pltpu.VMEM((supers, LANES), F32),
            pltpu.VMEM((q_tiles, HEAD_DIM, QT), F32),
            pltpu.VMEM((supers, LANES), F32),
        ],
        name="near",
        cost=NEAR_COST,
    )(*on_chip(exps, inverse, delta, kv, kvt, qz, hz, dq_far))
    keep, dq = results[:2]

    if group == 1:

        def last_body(*refs):
            total = refs[0][...]
            for ref in refs[1 : 1 + n_back]:
                total = total + ref[...].astype(F32)
            total = total.astype(BF16)
            refs[-2][0] = total[:, 0:HEAD_DIM]
            refs[-1][0] = total[:, HEAD_DIM:LANES]
            resid_out(refs[1 + n_back : 1 + n_back + n_dres], refs[-3])

        d_resid, d_key, d_value = call(last_body, [dres_shape] + [arr((1, block, HEAD_DIM))] * 2, name="last")(
            *on_chip(keep, *back, *dres)
        )
        return d_resid, dq, d_key, d_value

    other = lax.ppermute(results[2], "y", [(0, 1), (1, 0)])

    def last_body(*refs):
        keep_ref, dq_keep_ref, other_ref = refs[:3]
        back_refs = refs[3 : 3 + n_back]
        dres_refs = refs[3 + n_back : 3 + n_back + n_dres]
        dres_ref, dq_ref, dk_ref, dv_ref = refs[3 + n_back + n_dres :]
        resid_out(dres_refs, dres_ref)
        y = lax.axis_index("y")
        own = keep_ref[...]
        peer = other_ref[0:block, :].astype(F32)
        for i in range(2 * near):
            own = own + back_refs[2 * i][...].astype(F32)
            peer = peer + back_refs[2 * i + 1][...].astype(F32)
        first = y == 0
        lo = jnp.where(first, own, peer)
        up = jnp.where(first, peer, own)
        low = lax.broadcasted_iota(jnp.int32, (block, LANES), 1) < HEAD_DIM
        dk_ref[0] = jnp.where(low, lo, pltpu.roll(up, HEAD_DIM, 1)).astype(BF16)
        dv_ref[0] = jnp.where(low, pltpu.roll(lo, HEAD_DIM, 1), up).astype(BF16)
        own = dq_keep_ref[...].astype(F32)
        peer = other_ref[block : block + hb, :].astype(F32)
        lo = jnp.where(first, own, peer)
        up = jnp.where(first, peer, own)
        low = low[0:hb]
        dq_ref[0, 0:hb, :] = jnp.where(low, lo, pltpu.roll(up, HEAD_DIM, 1)).astype(BF16)
        dq_ref[0, hb:block, :] = jnp.where(low, pltpu.roll(lo, HEAD_DIM, 1), up).astype(BF16)

    d_resid, d_query, d_key, d_value = call(
        last_body, [dres_shape] + [arr((1, block, LANES))] * 3, name="last"
    )(*on_chip(keep, dq, other, *back, *dres))
    return d_resid, d_query, d_key, d_value


def solution(mesh):
    heads_axis = mesh.shape["head"]
    ctx_count = mesh.shape["ctx"]

    def run(query, *rest):
        group = query.shape[2] // HEAD_DIM // heads_axis
        z_count = ctx_count // group
        fine = Mesh(mesh.devices.reshape(heads_axis, z_count, group), ("head", "z", "y"))
        rows_spec = P(("z", "y"), "head", None)
        cols_spec = P(("z", "y"), None, "head")
        sizes = (heads_axis, z_count, group)
        return jax.shard_map(
            lambda *args: on_device(sizes, *args),
            mesh=fine,
            in_specs=(rows_spec,) * 5 + (P(),) * 3,
            out_specs=(cols_spec,) * 4,
            check_vma=False,
        )(query, *rest)

    return run
```

time: 82.2 us -> 58.6 us (0.71)
  the two profiles are of different devices: /device:TPU:0 before, /device:TPU:12 now
where the time goes in v2:
time: 58.6 us; the launch traced here: 58.4 us
  starting transfers between devices  25.3 us (43%)
  Pallas kernels  23 us (39%)
  waiting for transfers between devices  9.24 us (16%)
  between operations  0.82 us (1%)
    pallas_call x9, Pallas kernels, run(): pl.pallas_call(body, out_shape=outs, in_specs=[on_smem if i in smem else...  20.5 us
    ppermute x7, starting transfers between devices, exchange(): lax.ppermute(part, mesh_axes, everyone(target(m)))  8.78 us
    ppermute x4, starting transfers between devices, on_device(): lax.ppermute(far[3 + i * group + cross], ('z', 'y'), across(d, phase, cro...  8.77 us
    ppermute x4, waiting for transfers between devices, on_device(): lax.ppermute(far[3 + i * group + cross], ('z', 'y'), across(d, phase, cro...  5.57 us
    ppermute x2, starting transfers between devices, on_device(): lax.ppermute(both, 'z', swap_pairs(z_count, d, phase))  3.56 us
    ppermute x2, starting transfers between devices, on_device(): lax.ppermute(side, mesh_axes, [(chain_place(a), chain_place(b)) for a, b...  3.45 us
    pallas_call x1, Pallas kernels, on_device(): pl.pallas_call(pack_body, out_shape=pack_outs, in_specs=[on_vmem] * 3 + [...  2.49 us
    ppermute x3, waiting for transfers between devices, core_swap(): return lax.ppermute(x, mesh_axes, everyone(lambda h, z, y: (h ^ 1, z, y)))  2.36 us
  transfers between devices with their start and end apart: 19, of which 5 were waited for; matrix products, arithmetic and copies ran while one was open for 0% of the time, Pallas kernels for 33%

profile of v2, /device:TPU:12, one launch (start us, length us, event | category | flops | bytes accessed | tf_op | source)
XLA Modules:
  0.0 58.4 jit_solution(8405375289884557173)
XLA Ops:
  0.6 2.5 %pack.1 = (bf16[4,192,128]{2,1,0:T(8,128)(2,1)S(1)}, bf16[4,192,128]{2,1,0:T(8,128)(2,1)S(1)}, bf16[48,1024]{1,0:T(8,128)(2,1)S(1)}, bf16[48,1024]{1,0:T(8,128)(...) custom-call(bf16[1,128,512]{2,1,0:T(8,128)(2,1)} %q_ref.1, ...), custom_call_target="tpu_custom_call" | custom-call | tf_op jit(solution)/shard_map/pack/pallas_call | solution.py:159
  3.1 0.1 collective-permute-start
  3.2 1.4 %collective-permute-done.got_ref.refs_3_ = bf16[4,192,128]{2,1,0:T(8,128)(2,1)S(1)} collective-permute-done((bf16[4,192,128]{2,1,0:T(8,128)(2,1)S(1)}, bf16[4,192,128]{2,1,0:T(8,128)(2,1)S(1)}, u32[]{:S(2)}, u32[]{:S(2)}) %collective-permute-start) | collective-permute-done | bytes 196640 | tf_op jit(solution)/shard_map/ppermute | solution.py:183
  4.7 1.6 %collective-permute-start.1 = (bf16[2,192,128]{2,1,0:T(8,128)(2,1)S(1)}, bf16[2,192,128]{2,1,0:T(8,128)(2,1)S(1)}, u32[]{:S(2)}, u32[]{:S(2)}) collective-permute-start(bf16[2,192,128]{2,1,0:T(8,128)(2,1)S(1)} %get-tuple-element.40), channel_id=1, source_target_pairs={{0,16},{1,17},{2,18},{3,19},{4,20},{5,21},{6,22},{7,23},{8,24},{9,... | collective-permute-start | bytes 294920 | tf_op jit(solution)/shard_map/ppermute | solution.py:202
  6.2 0.5 collective-permute-start.2
  6.7 1.5 %collective-permute-start.3 = (bf16[2,192,128]{2,1,0:T(8,128)(2,1)S(1)}, bf16[2,192,128]{2,1,0:T(8,128)(2,1)S(1)}, u32[]{:S(2)}, u32[]{:S(2)}) collective-permute-start(bf16[2,192,128]{2,1,0:T(8,128)(2,1)S(1)} %get-tuple-element.42), channel_id=1, source_target_pairs={{0,17},{1,16},{2,19},{3,18},{4,21},{5,20},{6,23},{7,22},{8,25},{9,... | collective-permute-start | bytes 294920 | tf_op jit(solution)/shard_map/ppermute | solution.py:202
  8.2 0.0 collective-permute-start.6
  8.2 3.4 %collective-permute-start.7 = (bf16[48,1024]{1,0:T(8,128)(2,1)S(1)}, bf16[48,1024]{1,0:T(8,128)(2,1)S(1)}, u32[]{:S(2)}, u32[]{:S(2)}) collective-permute-start(bf16[48,1024]{1,0:T(8,128)(2,1)S(1)} %get-tuple-element.48), channel_id=1, source_target_pairs={{8,16},{16,8},{24,1},{1,24},{9,17},{17,9},{25,2},{2,25},{10,18},{1... | collective-permute-start | bytes 294920 | tf_op jit(solution)/shard_map/ppermute | solution.py:217
  11.7 0.0 collective-permute-done.1.refs_0_.refs_4_
  11.7 1.3 %collective-permute-done.2.refs_1_.refs_5_ = bf16[2,192,128]{2,1,0:T(8,128)(2,1)S(1)} collective-permute-done((bf16[2,192,128]{2,1,0:T(8,128)(2,1)S(1)}, bf16[2,192,128]{2,1,0:T(8,128)(2,1)S(1)}, u32[]{:S(2)}, u32[]{:S(2)}) %collective-permute-start.2) | collective-permute-done | bytes 98336 | tf_op jit(solution)/shard_map/ppermute | solution.py:202
  12.9 0.0 collective-permute-done.3.refs_2_.refs_6_
  13.0 3.5 %collective-permute-start.5 = (bf16[1024,128]{1,0:T(8,128)(2,1)S(1)}, bf16[1024,128]{1,0:T(8,128)(2,1)S(1)}, u32[]{:S(2)}, u32[]{:S(2)}) collective-permute-start(bf16[1024,128]{1,0:T(8,128)(2,1)S(1)} %keys.1.refs_1_), channel_id=1, source_target_pairs={{2,4},{4,2},{3,5},{5,3},{10,12},{12,10},{11,13},{13,11},{18,20},{2... | collective-permute-start | bytes 786440 | tf_op jit(solution)/shard_map/ppermute | solution.py:230
  16.5 0.1 collective-permute-start.4
  16.6 0.0 collective-permute-done.6.first_ref
  16.6 0.0 collective-permute-done.7.second_ref
  16.6 0.0 copy-start
  16.6 4.4 %conv.1 = (bf16[4,64,128]{2,1,0:T(8,128)(2,1)S(1)}, bf16[4,64,128]{2,1,0:T(8,128)(2,1)S(1)}, bf16[2,128,256]{2,1,0:T(8,128)(2,1)S(1)}, bf16[2,128,256]{2,1,0:T(8,128)(2,1)S(1)}) custom-call(bf16[1,128,1024]{2,1,0:T(8,128)(2,1)S(1)} %get-tuple-element.45.resid_ref, bf16[1,128,1024]{2,1,0:T(8,128)(2,1)S(1)} %get-tuple-element.46.grad_ref, ...), custom_call_target="tpu_custom_call" | custom-call | flops 6000000000 | tf_op jit(solution)/shard_map/conv/pallas_call | solution.py:37
  21.0 0.1 collective-permute-start.17
  21.1 0.5 collective-permute-start.8
  21.6 0.9 %collective-permute-done.8.got_ref.refs_1_ = bf16[4,64,128]{2,1,0:T(8,128)(2,1)S(1)} collective-permute-done((bf16[4,64,128]{2,1,0:T(8,128)(2,1)S(1)}, bf16[4,64,128]{2,1,0:T(8,128)(2,1)S(1)}, u32[]{:S(2)}, u32[]{:S(2)}) %collective-permute-start.8) | collective-permute-done | bytes 65568 | tf_op jit(solution)/shard_map/ppermute | solution.py:183
  22.5 1.7 %collective-permute-start.9 = (bf16[2,64,128]{2,1,0:T(8,128)(2,1)S(1)}, bf16[2,64,128]{2,1,0:T(8,128)(2,1)S(1)}, u32[]{:S(2)}, u32[]{:S(2)}) collective-permute-start(bf16[2,64,128]{2,1,0:T(8,128)(2,1)S(1)} %get-tuple-element.53), channel_id=1, source_target_pairs={{0,16},{1,17},{2,18},{3,19},{4,20},{5,21},{6,22},{7,23},{8,24},{9,... | collective-permute-start | bytes 98312 | tf_op jit(solution)/shard_map/ppermute | solution.py:202
  24.2 0.1 collective-permute-start.10
  24.3 0.0 collective-permute-done.17.got_ref.refs_8_
  24.3 1.8 %collective-permute-start.11 = (bf16[2,64,128]{2,1,0:T(8,128)(2,1)S(1)}, bf16[2,64,128]{2,1,0:T(8,128)(2,1)S(1)}, u32[]{:S(2)}, u32[]{:S(2)}) collective-permute-start(bf16[2,64,128]{2,1,0:T(8,128)(2,1)S(1)} %get-tuple-element.55), channel_id=1, source_target_pairs={{0,17},{1,16},{2,19},{3,18},{4,21},{5,20},{6,23},{7,22},{8,25},{9,... | collective-permute-start | bytes 98312 | tf_op jit(solution)/shard_map/ppermute | solution.py:202
  26.1 0.0 collective-permute-done.5.refs_8_
  26.1 1.7 %collective-permute-start.18 = (bf16[2,128,256]{2,1,0:T(8,128)(2,1)S(1)}, bf16[2,128,256]{2,1,0:T(8,128)(2,1)S(1)}, u32[]{:S(2)}, u32[]{:S(2)}) collective-permute-start(bf16[2,128,256]{2,1,0:T(8,128)(2,1)S(1)} %regroup_resid.1), channel_id=1, source_target_pairs={{0,16},{1,17},{2,18},{3,19},{4,20},{5,21},{6,22},{7,23},{8,24},{9,... | collective-permute-start | bytes 393224 | tf_op jit(solution)/shard_map/ppermute | solution.py:202
  27.8 0.0 collective-permute-done.4.refs_7_
  27.8 0.0 copy-done
  27.8 7.4 %scores.1 = (f32[36,256,256]{2,1,0:T(8,128)S(1)}, f32[4,1,256]{2,1,0:T(1,128)S(1)}, f32[4,64,256]{2,1,0:T(8,128)S(1)}, bf16[3072,128]{1,0:T(8,128)(2,1)S(1)}, bf...) custom-call(s32[8]{0:T(128)S(1)} %copy-done, bf16[1024,128]{1,0:T(8,128)(2,1)S(1)} %keys.1.refs_1_, ...), custom_call_target="tpu_custom_call" | custom-call | flops 8999999488 | tf_op jit(solution)/shard_map/scores/pallas_call | solution.py:37
  35.2 0.0 collective-permute-done.9.refs_2_
  35.2 0.0 collective-permute-done.10.refs_3_
  35.2 0.0 collective-permute-done.11.refs_4_
  35.2 3.7 %far.1 = (bf16[1024,128]{1,0:T(8,128)(2,1)S(1)}, f32[4,1,256]{2,1,0:T(1,128)S(1)}, f32[4,64,256]{2,1,0:T(8,128)S(1)}, bf16[512,128]{1,0:T(8,128)(2,1)S(1)}, bf16...) custom-call(bf16[4,64,128]{2,1,0:T(8,128)(2,1)S(1)} %get-tuple-element.51.keep_ref.refs_0_, ...), custom_call_target="tpu_custom_call" | custom-call | flops 4000000000 | tf_op jit(solution)/shard_map/far/pallas_call | solution.py:37
  38.9 3.9 %near.1 = (f32[512,128]{1,0:T(8,128)S(1)}, bf16[256,128]{1,0:T(8,128)(2,1)S(1)}, bf16[768,128]{1,0:T(8,128)(2,1)S(1)}) custom-call(f32[36,256,256]{2,1,0:T(8,128)S(1)} %get-tuple-element.43.refs_5_.refs_0_, f32[4,1,256]{2,1,0:T(1,128)S(1)} %get-tuple-element.44.refs_6_.refs_1_, f32[4,1,256]{2,1,0:T(1,128)S(1)} %get-tuple-element.60.refs_2_, ...), custom_call_target="tpu_custom_call" | custom-call | flops 4000000000 | tf_op jit(solution)/shard_map/near/pallas_call | solution.py:37
  42.9 0.1 collective-permute-start.12
  43.0 2.0 %collective-permute-start.13 = (bf16[512,128]{1,0:T(8,128)(2,1)S(1)}, bf16[512,128]{1,0:T(8,128)(2,1)S(1)}, u32[]{:S(2)}, u32[]{:S(2)}) collective-permute-start(bf16[512,128]{1,0:T(8,128)(2,1)S(1)} %get-tuple-element.66), channel_id=1, source_target_pairs={{0,2},{1,3},{2,0},{3,1},{4,6},{5,7},{6,4},{7,5},{8,10},{9,11},{10,... | collective-permute-start | bytes 393224 | tf_op jit(solution)/shard_map/ppermute | solution.py:480
  45.0 1.4 %collective-permute-start.14 = (bf16[512,128]{1,0:T(8,128)(2,1)S(1)}, bf16[512,128]{1,0:T(8,128)(2,1)S(1)}, u32[]{:S(2)}, u32[]{:S(2)}) collective-permute-start(bf16[512,128]{1,0:T(8,128)(2,1)S(1)} %get-tuple-element.67), channel_id=1, source_target_pairs={{0,3},{1,2},{2,1},{3,0},{4,7},{5,6},{6,5},{7,4},{8,11},{9,10},{10,... | collective-permute-start | bytes 393224 | tf_op jit(solution)/shard_map/ppermute | solution.py:480
  46.4 3.2 %collective-permute-start.15 = (bf16[512,128]{1,0:T(8,128)(2,1)S(1)}, bf16[512,128]{1,0:T(8,128)(2,1)S(1)}, u32[]{:S(2)}, u32[]{:S(2)}) collective-permute-start(bf16[512,128]{1,0:T(8,128)(2,1)S(1)} %get-tuple-element.68), channel_id=1, source_target_pairs={{2,4},{3,5},{4,2},{5,3},{10,12},{11,13},{12,10},{13,11},{18,20},{1... | collective-permute-start | bytes 393224 | tf_op jit(solution)/shard_map/ppermute | solution.py:480
  49.6 0.0 collective-permute-done.18.refs_9_
  49.6 2.2 %collective-permute-start.16 = (bf16[512,128]{1,0:T(8,128)(2,1)S(1)}, bf16[512,128]{1,0:T(8,128)(2,1)S(1)}, u32[]{:S(2)}, u32[]{:S(2)}) collective-permute-start(bf16[512,128]{1,0:T(8,128)(2,1)S(1)} %get-tuple-element.69), channel_id=1, source_target_pairs={{2,5},{3,4},{4,3},{5,2},{10,13},{11,12},{12,11},{13,10},{18,21},{1... | collective-permute-start | bytes 393224 | tf_op jit(solution)/shard_map/ppermute | solution.py:480
  51.8 0.0 collective-permute-done.13.refs_3_
  51.8 0.0 collective-permute-done.14.refs_4_
  51.8 2.8 %collective-permute-done.15.refs_5_ = bf16[512,128]{1,0:T(8,128)(2,1)S(1)} collective-permute-done((bf16[512,128]{1,0:T(8,128)(2,1)S(1)}, bf16[512,128]{1,0:T(8,128)(2,1)S(1)}, u32[]{:S(2)}, u32[]{:S(2)}) %collective-permute-start.15) | collective-permute-done | bytes 131104 | tf_op jit(solution)/shard_map/ppermute | solution.py:480
  54.7 2.7 %collective-permute-done.16.refs_6_ = bf16[512,128]{1,0:T(8,128)(2,1)S(1)} collective-permute-done((bf16[512,128]{1,0:T(8,128)(2,1)S(1)}, bf16[512,128]{1,0:T(8,128)(2,1)S(1)}, u32[]{:S(2)}, u32[]{:S(2)}) %collective-permute-start.16) | collective-permute-done | bytes 131104 | tf_op jit(solution)/shard_map/ppermute | solution.py:480
  57.4 0.0 collective-permute-done.12.refs_2_
  57.4 1.0 %last.1 = (bf16[1,512,256]{2,1,0:T(8,128)(2,1)}, bf16[1,512,128]{2,1,0:T(8,128)(2,1)}, bf16[1,512,128]{2,1,0:T(8,128)(2,1)}, bf16[1,512,128]{2,1,0:T(8,128)(2,1)}) custom-call(f32[512,128]{1,0:T(8,128)S(1)} %get-tuple-element.63.refs_0_, bf16[256,128]{1,0:T(8,128)(2,1)S(1)} %get-tuple-element.64.refs_1_, ...), custom_call_target="tpu_custom_call" | custom-call | tf_op jit(solution)/shard_map/last/pallas_call | solution.py:37
  (4 shorter events, 0.1 us)
Async XLA Ops:
  3.1 1.5 %collective-permute-start = (bf16[4,192,128]{2,1,0:T(8,128)(2,1)S(1)}, bf16[4,192,128]{2,1,0:T(8,128)(2,1)S(1)}, u32[]{:S(2)}, u32[]{:S(2)}) collective-permute-start(bf16[4,192,128]{2,1,0:T(8,128)(2,1)S(1)} %get-tuple-element.39), channel_id=1, source_target_pairs={{0,8},{1,9},{2,10},{3,11},{4,12},{5,13},{6,14},{7,15},{8,0},{9,1},... | collective-permute-start | bytes 589832 | tf_op jit(solution)/shard_map/ppermute | solution.py:183
  4.7 7.0 %collective-permute-start.1 = (bf16[2,192,128]{2,1,0:T(8,128)(2,1)S(1)}, bf16[2,192,128]{2,1,0:T(8,128)(2,1)S(1)}, u32[]{:S(2)}, u32[]{:S(2)}) collective-permute-start(bf16[2,192,128]{2,1,0:T(8,128)(2,1)S(1)} %get-tuple-element.40), channel_id=1, source_target_pairs={{0,16},{1,17},{2,18},{3,19},{4,20},{5,21},{6,22},{7,23},{8,24},{9,... | collective-permute-start | bytes 294920 | tf_op jit(solution)/shard_map/ppermute | solution.py:202
  6.2 6.7 %collective-permute-start.2 = (bf16[2,192,128]{2,1,0:T(8,128)(2,1)S(1)}, bf16[2,192,128]{2,1,0:T(8,128)(2,1)S(1)}, u32[]{:S(2)}, u32[]{:S(2)}) collective-permute-start(bf16[2,192,128]{2,1,0:T(8,128)(2,1)S(1)} %get-tuple-element.41), channel_id=1, source_target_pairs={{0,1},{1,0},{2,3},{3,2},{4,5},{5,4},{6,7},{7,6},{8,9},{9,8},{10,11... | collective-permute-start | bytes 294920 | tf_op jit(solution)/shard_map/ppermute | solution.py:202
  6.7 6.2 %collective-permute-start.3 = (bf16[2,192,128]{2,1,0:T(8,128)(2,1)S(1)}, bf16[2,192,128]{2,1,0:T(8,128)(2,1)S(1)}, u32[]{:S(2)}, u32[]{:S(2)}) collective-permute-start(bf16[2,192,128]{2,1,0:T(8,128)(2,1)S(1)} %get-tuple-element.42), channel_id=1, source_target_pairs={{0,17},{1,16},{2,19},{3,18},{4,21},{5,20},{6,23},{7,22},{8,25},{9,... | collective-permute-start | bytes 294920 | tf_op jit(solution)/shard_map/ppermute | solution.py:202
  8.2 8.3 %collective-permute-start.6 = (bf16[48,1024]{1,0:T(8,128)(2,1)S(1)}, bf16[48,1024]{1,0:T(8,128)(2,1)S(1)}, u32[]{:S(2)}, u32[]{:S(2)}) collective-permute-start(bf16[48,1024]{1,0:T(8,128)(2,1)S(1)} %get-tuple-element.47), channel_id=1, source_target_pairs={{0,8},{8,0},{16,24},{24,16},{1,9},{9,1},{17,25},{25,17},{2,10},{10... | collective-permute-start | bytes 294920 | tf_op jit(solution)/shard_map/ppermute | solution.py:217
  8.2 8.4 %collective-permute-start.7 = (bf16[48,1024]{1,0:T(8,128)(2,1)S(1)}, bf16[48,1024]{1,0:T(8,128)(2,1)S(1)}, u32[]{:S(2)}, u32[]{:S(2)}) collective-permute-start(bf16[48,1024]{1,0:T(8,128)(2,1)S(1)} %get-tuple-element.48), channel_id=1, source_target_pairs={{8,16},{16,8},{24,1},{1,24},{9,17},{17,9},{25,2},{2,25},{10,18},{1... | collective-permute-start | bytes 294920 | tf_op jit(solution)/shard_map/ppermute | solution.py:217
  13.0 13.1 %collective-permute-start.5 = (bf16[1024,128]{1,0:T(8,128)(2,1)S(1)}, bf16[1024,128]{1,0:T(8,128)(2,1)S(1)}, u32[]{:S(2)}, u32[]{:S(2)}) collective-permute-start(bf16[1024,128]{1,0:T(8,128)(2,1)S(1)} %keys.1.refs_1_), channel_id=1, source_target_pairs={{2,4},{4,2},{3,5},{5,3},{10,12},{12,10},{11,13},{13,11},{18,20},{2... | collective-permute-start | bytes 786440 | tf_op jit(solution)/shard_map/ppermute | solution.py:230
  16.5 11.3 %collective-permute-start.4 = (bf16[1024,128]{1,0:T(8,128)(2,1)S(1)}, bf16[1024,128]{1,0:T(8,128)(2,1)S(1)}, u32[]{:S(2)}, u32[]{:S(2)}) collective-permute-start(bf16[1024,128]{1,0:T(8,128)(2,1)S(1)} %keys.1.refs_1_), channel_id=1, source_target_pairs={{0,2},{2,0},{4,6},{6,4},{1,3},{3,1},{5,7},{7,5},{8,10},{10,8},{12,... | collective-permute-start | bytes 786440 | tf_op jit(solution)/shard_map/ppermute | solution.py:230
  16.6 11.2 %copy-start = (s32[8]{0:T(128)S(1)}, s32[8]{0:T(128)}, u32[]{:S(2)}) copy-start(s32[8]{0:T(128)} %refs_0_.1) | copy-start | bytes 100
  21.0 3.3 %collective-permute-start.17 = (bf16[2,128,256]{2,1,0:T(8,128)(2,1)S(1)}, bf16[2,128,256]{2,1,0:T(8,128)(2,1)S(1)}, u32[]{:S(2)}, u32[]{:S(2)}) collective-permute-start(bf16[2,128,256]{2,1,0:T(8,128)(2,1)S(1)} %get-tuple-element.71), channel_id=1, source_target_pairs={{0,8},{1,9},{2,10},{3,11},{4,12},{5,13},{6,14},{7,15},{8,0},{9,1},... | collective-permute-start | bytes 393224 | tf_op jit(solution)/shard_map/ppermute | solution.py:183
  21.1 1.4 %collective-permute-start.8 = (bf16[4,64,128]{2,1,0:T(8,128)(2,1)S(1)}, bf16[4,64,128]{2,1,0:T(8,128)(2,1)S(1)}, u32[]{:S(2)}, u32[]{:S(2)}) collective-permute-start(bf16[4,64,128]{2,1,0:T(8,128)(2,1)S(1)} %get-tuple-element.52), channel_id=1, source_target_pairs={{0,8},{1,9},{2,10},{3,11},{4,12},{5,13},{6,14},{7,15},{8,0},{9,1},... | collective-permute-start | bytes 196616 | tf_op jit(solution)/shard_map/ppermute | solution.py:183
  22.5 12.7 %collective-permute-start.9 = (bf16[2,64,128]{2,1,0:T(8,128)(2,1)S(1)}, bf16[2,64,128]{2,1,0:T(8,128)(2,1)S(1)}, u32[]{:S(2)}, u32[]{:S(2)}) collective-permute-start(bf16[2,64,128]{2,1,0:T(8,128)(2,1)S(1)} %get-tuple-element.53), channel_id=1, source_target_pairs={{0,16},{1,17},{2,18},{3,19},{4,20},{5,21},{6,22},{7,23},{8,24},{9,... | collective-permute-start | bytes 98312 | tf_op jit(solution)/shard_map/ppermute | solution.py:202
  24.2 11.0 %collective-permute-start.10 = (bf16[2,64,128]{2,1,0:T(8,128)(2,1)S(1)}, bf16[2,64,128]{2,1,0:T(8,128)(2,1)S(1)}, u32[]{:S(2)}, u32[]{:S(2)}) collective-permute-start(bf16[2,64,128]{2,1,0:T(8,128)(2,1)S(1)} %get-tuple-element.54), channel_id=1, source_target_pairs={{0,1},{1,0},{2,3},{3,2},{4,5},{5,4},{6,7},{7,6},{8,9},{9,8},{10,11... | collective-permute-start | bytes 98312 | tf_op jit(solution)/shard_map/ppermute | solution.py:202
  24.3 10.9 %collective-permute-start.11 = (bf16[2,64,128]{2,1,0:T(8,128)(2,1)S(1)}, bf16[2,64,128]{2,1,0:T(8,128)(2,1)S(1)}, u32[]{:S(2)}, u32[]{:S(2)}) collective-permute-start(bf16[2,64,128]{2,1,0:T(8,128)(2,1)S(1)} %get-tuple-element.55), channel_id=1, source_target_pairs={{0,17},{1,16},{2,19},{3,18},{4,21},{5,20},{6,23},{7,22},{8,25},{9,... | collective-permute-start | bytes 98312 | tf_op jit(solution)/shard_map/ppermute | solution.py:202
  26.1 23.5 %collective-permute-start.18 = (bf16[2,128,256]{2,1,0:T(8,128)(2,1)S(1)}, bf16[2,128,256]{2,1,0:T(8,128)(2,1)S(1)}, u32[]{:S(2)}, u32[]{:S(2)}) collective-permute-start(bf16[2,128,256]{2,1,0:T(8,128)(2,1)S(1)} %regroup_resid.1), channel_id=1, source_target_pairs={{0,16},{1,17},{2,18},{3,19},{4,20},{5,21},{6,22},{7,23},{8,24},{9,... | collective-permute-start | bytes 393224 | tf_op jit(solution)/shard_map/ppermute | solution.py:202
  42.9 14.5 %collective-permute-start.12 = (bf16[768,128]{1,0:T(8,128)(2,1)S(1)}, bf16[768,128]{1,0:T(8,128)(2,1)S(1)}, u32[]{:S(2)}, u32[]{:S(2)}) collective-permute-start(bf16[768,128]{1,0:T(8,128)(2,1)S(1)} %get-tuple-element.65), channel_id=1, source_target_pairs={{0,1},{1,0},{2,3},{3,2},{4,5},{5,4},{6,7},{7,6},{8,9},{9,8},{10,11... | collective-permute-start | bytes 589832 | tf_op jit(solution)/shard_map/ppermute | solution.py:542
  43.0 8.8 %collective-permute-start.13 = (bf16[512,128]{1,0:T(8,128)(2,1)S(1)}, bf16[512,128]{1,0:T(8,128)(2,1)S(1)}, u32[]{:S(2)}, u32[]{:S(2)}) collective-permute-start(bf16[512,128]{1,0:T(8,128)(2,1)S(1)} %get-tuple-element.66), channel_id=1, source_target_pairs={{0,2},{1,3},{2,0},{3,1},{4,6},{5,7},{6,4},{7,5},{8,10},{9,11},{10,... | collective-permute-start | bytes 393224 | tf_op jit(solution)/shard_map/ppermute | solution.py:480
  45.0 6.8 %collective-permute-start.14 = (bf16[512,128]{1,0:T(8,128)(2,1)S(1)}, bf16[512,128]{1,0:T(8,128)(2,1)S(1)}, u32[]{:S(2)}, u32[]{:S(2)}) collective-permute-start(bf16[512,128]{1,0:T(8,128)(2,1)S(1)} %get-tuple-element.67), channel_id=1, source_target_pairs={{0,3},{1,2},{2,1},{3,0},{4,7},{5,6},{6,5},{7,4},{8,11},{9,10},{10,... | collective-permute-start | bytes 393224 | tf_op jit(solution)/shard_map/ppermute | solution.py:480
  46.4 8.2 %collective-permute-start.15 = (bf16[512,128]{1,0:T(8,128)(2,1)S(1)}, bf16[512,128]{1,0:T(8,128)(2,1)S(1)}, u32[]{:S(2)}, u32[]{:S(2)}) collective-permute-start(bf16[512,128]{1,0:T(8,128)(2,1)S(1)} %get-tuple-element.68), channel_id=1, source_target_pairs={{2,4},{3,5},{4,2},{5,3},{10,12},{11,13},{12,10},{13,11},{18,20},{1... | collective-permute-start | bytes 393224 | tf_op jit(solution)/shard_map/ppermute | solution.py:480
  49.6 7.8 %collective-permute-start.16 = (bf16[512,128]{1,0:T(8,128)(2,1)S(1)}, bf16[512,128]{1,0:T(8,128)(2,1)S(1)}, u32[]{:S(2)}, u32[]{:S(2)}) collective-permute-start(bf16[512,128]{1,0:T(8,128)(2,1)S(1)} %get-tuple-element.69), channel_id=1, source_target_pairs={{2,5},{3,4},{4,3},{5,2},{10,13},{11,12},{12,11},{13,10},{18,21},{1... | collective-permute-start | bytes 393224 | tf_op jit(solution)/shard_map/ppermute | solution.py:480

commit v3 on v2

v3 whole, which is shorter than its diff:
```python
import jax
import jax.numpy as jnp
from jax import lax
from jax.experimental import pallas as pl
from jax.experimental.pallas import tpu as pltpu
from jax.sharding import Mesh
from jax.sharding import PartitionSpec as P

HEAD_DIM = 64
KERNEL = 31
REACH = 2
LANES = 128
QT = 256
HALO = 32
HALF = 16
NEG = -1e30
ONES = 16
F32 = jnp.float32
BF16 = jnp.bfloat16
NT_DIMS = (((1,), (1,)), ((), ()))
NN_DIMS = (((1,), (0,)), ((), ()))
VMEM_LIMIT = 12 * 1024 * 1024
CONV_COST = (6_000_000_000, 0, 0)
SCORES_COST = (9_000_000_000, 0, 0)
FAR_COST = (4_000_000_000, 0, 0)
NEAR_COST = (4_000_000_000, 0, 0)


def dot(a, b, dims):
    return lax.dot_general(a, b, dims, preferred_element_type=F32)


def call(body, outs, smem=(), raw=(), scratch=(), name=None, cost=None):
    on_vmem = pl.BlockSpec(memory_space=pltpu.VMEM)
    spaces = {i: pltpu.SMEM for i in smem} | {i: pltpu.HBM for i in raw}

    def run(*args):
        return pl.pallas_call(
            body,
            out_shape=outs,
            in_specs=[pl.BlockSpec(memory_space=spaces.get(i, pltpu.VMEM)) for i in range(len(args))],
            out_specs=[on_vmem] * len(outs),
            scratch_shapes=list(scratch),
            compiler_params=pltpu.CompilerParams(vmem_limit_bytes=VMEM_LIMIT),
            cost_estimate=None if cost is None else pl.CostEstimate(*cost),
            name=name,
        )(*args)

    return run


def arr(shape, dtype=BF16):
    return jax.ShapeDtypeStruct(shape, dtype)


def vmem(shape, dtype=BF16):
    return pltpu.VMEM(shape, dtype)


def on_chip(*arrays):
    return [pltpu.with_memory_space_constraint(x, pltpu.VMEM) for x in arrays]


def in_hbm(*arrays):
    return [pltpu.with_memory_space_constraint(x, pltpu.HBM) for x in arrays]


def on_device(sizes, query, key, value, resid_in, out_grad, out_weight, conv_kernel, frame_lengths):
    heads_axis, z_count, group = sizes
    ctx_count = z_count * group
    rows = query.shape[1]
    width = query.shape[2]
    channels = resid_in.shape[2]
    block = rows * heads_axis
    supers = group * block
    members = group * heads_axis
    chips = members // 2
    half = rows // 2
    near = -(-REACH // group)
    window = REACH * block
    tiles = 2 * window // QT + 1
    per_block = block // QT
    lead = near * supers - window
    ext = (2 * near + 1) * supers
    out_cols = channels // heads_axis
    scale = HEAD_DIM ** (-0.5)

    def head_of(member):
        return group * (member % heads_axis) + member // heads_axis

    def cols(head):
        return slice(head * HEAD_DIM, (head + 1) * HEAD_DIM)

    def sides(core, slots):
        first, second = slots
        return jnp.where(core == 0, first, second), jnp.where(core == 0, second, first)

    def member_of(chip, core):
        return chip * 2 + core

    def my_chip():
        return lax.axis_index("y") * (heads_axis // 2) + lax.axis_index("head") // 2

    def my_core():
        return lax.axis_index("head") % 2

    def pack_body(q_hbm, k_hbm, v_hbm, resid_ref, grad_ref, taps_ref, *refs):
        keep_ref, send_ref, first_ref, second_ref, resid_out, grad_out, taps_out, q_ref, k_ref, v_ref, sems = refs
        copies = [
            pltpu.make_async_copy(source, target, sems.at[i])
            for i, (source, target) in enumerate(
                (
                    (resid_ref, resid_out), (grad_ref, grad_out), (k_hbm, k_ref), (v_hbm, v_ref),
                    (q_hbm, q_ref), (taps_ref, taps_out),
                )
            )
        ]
        for copy in copies:
            copy.start()
        core = my_core()
        copies[0].wait()
        copies[1].wait()
        odd = core == 1
        for side_ref, low in ((first_ref, odd), (second_ref, jnp.logical_not(odd))):
            side_ref[0:HALO, :] = jnp.where(low, resid_out[0, 0:HALO, :], resid_out[0, rows - HALO : rows, :])
            side_ref[HALO : HALO + HALF, :] = jnp.where(
                low, grad_out[0, 0:HALF, :], grad_out[0, rows - HALF : rows, :]
            )
        for copy in copies[2:]:
            copy.wait()
        for chip in range(chips):
            heads = [cols(head_of(member_of(chip, c))) for c in (0, 1)]
            for at, width, c_ref, low, high in (
                (0, 0, k_ref, 0, rows),
                (0, HEAD_DIM, v_ref, 0, rows),
                (rows, 0, q_ref, 0, half),
                (rows, HEAD_DIM, q_ref, half, rows),
            ):
                stay, leave = sides(core, [c_ref[0, low:high, c] for c in heads])
                keep_ref[chip, at : at + high - low, width : width + HEAD_DIM] = stay
                send_ref[chip, at : at + high - low, width : width + HEAD_DIM] = leave

    slot = rows + half
    raw = pl.BlockSpec(memory_space=pltpu.HBM)
    on_vmem = pl.BlockSpec(memory_space=pltpu.VMEM)
    pack_outs = [
        vmem((chips, slot, LANES)), vmem((chips, slot, LANES)),
        vmem((HALO + HALF, channels)), vmem((HALO + HALF, channels)),
        vmem((1, rows, channels)), vmem((1, rows, channels)), vmem(conv_kernel.shape),
    ]
    keep, send, first, second, resid, upstream, taps_in = pl.pallas_call(
        pack_body,
        out_shape=pack_outs,
        in_specs=[raw] * 6,
        out_specs=[on_vmem] * 7,
        scratch_shapes=[pltpu.VMEM((1, rows, width), BF16)] * 3 + [pltpu.SemaphoreType.DMA((6,))],
        compiler_params=pltpu.CompilerParams(vmem_limit_bytes=VMEM_LIMIT),
        name="pack",
    )(*in_hbm(query, key, value, resid_in, out_grad, conv_kernel))

    mesh_axes = ("head", "z", "y")

    def place(head, z, y):
        return head * ctx_count + z * group + y

    def everyone(target):
        return [
            (place(h, z, y), place(*target(h, z, y)))
            for h in range(heads_axis)
            for z in range(z_count)
            for y in range(group)
        ]

    def core_swap(x):
        return lax.ppermute(x, mesh_axes, everyone(lambda h, z, y: (h ^ 1, z, y)))

    def step(x, d, phase):
        def target(h, z, y):
            partner = z + d if (z // d) % 2 == phase else z - d
            return (h, partner, y) if 0 <= partner < z_count else (h ^ 1, z, y)

        return lax.ppermute(x, mesh_axes, everyone(target))

    def exchange(keep, got, count, index, name):
        def body(keep_ref, got_ref, *out_refs):
            me = index()
            for m, out_ref in enumerate(out_refs, 1):
                out_ref[0] = keep_ref[me ^ m]
                out_ref[1] = got_ref[me ^ m]

        per_row = heads_axis // 2

        def target(m):
            def f(h, z, y):
                chip = (y * per_row + h // 2) ^ m
                return (chip % per_row) * 2 + h % 2, z, chip // per_row

            return f

        parts = call(body, [vmem((2,) + keep.shape[1:])] * (count - 1), name=name)(*on_chip(keep, got))
        return [lax.ppermute(part, mesh_axes, everyone(target(m))) for m, part in enumerate(parts, 1)]

    def arrivals(me, core, keep_ref, got_ref, part_refs):
        out = [(member_of(me, core), lambda: keep_ref[me]), (member_of(me, 1 - core), lambda: got_ref[me])]
        for m, ref in enumerate(part_refs, 1):
            out.append((member_of(me ^ m, core), lambda ref=ref: ref[0]))
            out.append((member_of(me ^ m, 1 - core), lambda ref=ref: ref[1]))
        return out

    got = core_swap(send)

    last_head = heads_axis - 1

    def inside(h, z, y):
        return (h + 1 if h % 2 else h - 1) if 0 < h < last_head else last_head - h, z, y

    outer = {}
    idle = []
    for ctx in range(ctx_count):
        for h in range(heads_axis):
            if h == last_head and ctx < ctx_count - 1:
                outer[h, ctx] = (0, ctx + 1)
                outer[0, ctx + 1] = (h, ctx)
            elif 0 < h < last_head or (h, ctx) in ((0, 0), (last_head, ctx_count - 1)):
                idle.append((h, ctx))
    for one, two in zip(idle[::2], idle[1::2]):
        outer[one], outer[two] = two, one

    def outside(h, z, y):
        head, ctx = outer[h, z * group + y]
        return head, ctx // group, ctx % group

    halos = [
        core_swap(first),
        lax.ppermute(second, mesh_axes, everyone(inside)),
        lax.ppermute(second, mesh_axes, everyone(outside)),
    ]
    mine = [keep, got] + exchange(keep, got, chips, my_chip, "regroup")

    def keys_body(keep_ref, got_ref, *refs):
        out_ref = refs[-1]
        for member, take in arrivals(my_chip(), my_core(), keep_ref, got_ref, refs[:-1]):
            out_ref[pl.ds(pl.multiple_of(member * rows, rows), rows), :] = take()[0:rows]

    (both,) = call(keys_body, [vmem((supers, LANES))], name="keys")(*on_chip(*mine))

    steps = [(d, phase) for d in range(1, near + 1) for phase in (0, 1)]
    around = [step(both, d, phase) for d, phase in steps]

    span = rows + 2 * HALF

    def conv_body(
        resid_ref, grad_ref, core_ref, inside_ref, outside_ref, taps_ref, weight_hbm,
        hg_keep, hg_send, dres_keep, dres_send, low_ref, weight_ref, sem,
    ):
        fetch = pltpu.make_async_copy(weight_hbm, weight_ref, sem)
        fetch.start()
        head, ctx = lax.axis_index("head"), lax.axis_index("z") * group + lax.axis_index("y")
        odd = (head % 2) == 1
        edge = jnp.logical_or(head == 0, head == heads_axis - 1)
        starts = jnp.logical_and(head == 0, ctx == 0)
        ends = jnp.logical_and(head == heads_axis - 1, ctx == ctx_count - 1)

        def taps_sum(x, tap_of, length):
            total = None
            for b in range(8):
                part = None
                for a in range(4):
                    offset = 8 * a + b
                    if offset < 1 or offset > KERNEL:
                        continue
                    term = tap_of(offset - 1) * x[8 * a : 8 * a + length + 8]
                    part = term if part is None else part + term
                if b:
                    part = pltpu.roll(part, length + 8 - b, 0)
                part = part[0:length]
                total = part if total is None else total + part
            return total

        def chunk(c, carry):
            at = pl.multiple_of(c * LANES, LANES)
            lane = pl.ds(at, LANES)
            first = core_ref[:, lane].astype(F32)
            second = jnp.where(edge, outside_ref[:, lane].astype(F32), inside_ref[:, lane].astype(F32))
            before = jnp.where(starts, 0.0, jnp.where(odd, first, second))
            after = jnp.where(ends, 0.0, jnp.where(odd, second, first))
            taps = taps_ref[:, lane].astype(F32)
            x = jnp.concatenate([before[0:HALO], resid_ref[0, :, lane].astype(F32), after[0:HALO]], axis=0)
            middle = grad_ref[0, :, lane].astype(F32)
            g = jnp.concatenate([before[HALO:], middle, after[HALO:]], axis=0)
            pre = taps_sum(x, lambda k: taps[k : k + 1], span)
            s = 1.0 / (1.0 + jnp.exp(-pre))
            cg = g * (s * (1.0 + pre * (1.0 - s)))
            out = middle + taps_sum(cg, lambda k: taps[KERNEL - 1 - k : KERNEL - k], rows)
            low_ref[:, lane] = out.astype(BF16)
            return carry

        lax.fori_loop(0, channels // LANES, chunk, 0)
        core = my_core()
        for x in range(heads_axis // 2):
            dres_keep[x], dres_send[x] = sides(
                core, [low_ref[:, h * out_cols : (h + 1) * out_cols] for h in (2 * x, 2 * x + 1)]
            )
        fetch.wait()
        hg = dot(low_ref[...], weight_ref[...], NT_DIMS).astype(BF16)
        for chip in range(chips):
            heads = [cols(head_of(member_of(chip, c))) for c in (0, 1)]
            for at, part in ((0, slice(0, half)), (HEAD_DIM, slice(half, rows))):
                stay, leave = sides(core, [hg[part, c] for c in heads])
                hg_keep[chip, :, at : at + HEAD_DIM] = stay
                hg_send[chip, :, at : at + HEAD_DIM] = leave

    hg_keep, hg_send, dres_keep, dres_send = call(
        conv_body,
        [vmem((chips, half, LANES))] * 2 + [vmem((heads_axis // 2, rows, out_cols))] * 2,
        raw=(6,),
        scratch=[
            pltpu.VMEM((rows, channels), BF16),
            pltpu.VMEM(out_weight.shape, BF16),
            pltpu.SemaphoreType.DMA,
        ],
        name="conv",
        cost=CONV_COST,
    )(*on_chip(resid, upstream, *halos, taps_in), *in_hbm(out_weight))
    hg_got = core_swap(hg_send)
    grads = [hg_keep, hg_got] + exchange(hg_keep, hg_got, chips, my_chip, "regroup_grads")
    n_dres = 2 + heads_axis // 2 - 1
    dres_shape = arr((1, block, out_cols))

    def resid_out(refs, out_ref):
        for member, take in arrivals(lax.axis_index("head") // 2, my_core(), refs[0], refs[1], refs[2:]):
            out_ref[0, pl.ds(pl.multiple_of(member * rows, rows), rows), :] = take()

    q_tiles = supers // QT
    k_tiles = ext // QT
    first_tile = lead // QT
    own_tiles = range(near * q_tiles, (near + 1) * q_tiles)

    def seen(a):
        return range(a + first_tile, a + first_tile + tiles)

    def at_tile(t):
        return slice(t * QT, (t + 1) * QT)

    def score_body(*refs):
        len_ref, both_ref = refs[:2]
        mine_refs = refs[2 : 3 + chips]
        around_refs = refs[3 + chips : 3 + chips + 2 * near]
        e_ref, inv_ref, out_ref, kv, kt, qz, kb, qs, vt, s_sc = refs[3 + chips + 2 * near :]
        z = lax.axis_index("z")
        low = lax.broadcasted_iota(jnp.int32, (half, LANES), 1) < HEAD_DIM
        lane = lax.broadcasted_iota(jnp.int32, (half, LANES), 1)
        kv[near * supers : (near + 1) * supers, :] = both_ref[...]
        for member, take in arrivals(my_chip(), my_core(), mine_refs[0], mine_refs[1], mine_refs[2:]):
            q = take()[rows:slot].astype(F32) * scale
            for i, part in enumerate((q, pltpu.roll(q, HEAD_DIM, 1))):
                at = pl.ds(pl.multiple_of(member * rows + i * half, half), half)
                part = jnp.where(low, part, 0.0)
                qz[at, :] = part.astype(BF16)
                qs[at, :] = jnp.where(lane == HEAD_DIM, 1.0, part).astype(BF16)
        for d in range(1, near + 1):
            left, right = (near - d) * supers, (near + d) * supers
            odd = ((z // d) % 2) == 1

            @pl.when(odd)
            def _():
                kv[left : left + supers, :] = around_refs[2 * d - 2][...]
                kv[right : right + supers, :] = around_refs[2 * d - 1][...]

            @pl.when(jnp.logical_not(odd))
            def _():
                kv[left : left + supers, :] = around_refs[2 * d - 1][...]
                kv[right : right + supers, :] = around_refs[2 * d - 2][...]

        def limit(t):
            index = (z - near) * group + t // per_block
            inside = jnp.logical_and(index >= 0, index < ctx_count)
            length = len_ref[jnp.clip(index, 0, ctx_count - 1)]
            return jnp.where(inside, length, 0) - (t % per_block) * QT

        tile_lane = lax.broadcasted_iota(jnp.int32, (QT, LANES), 1)
        tile_row = lax.broadcasted_iota(jnp.int32, (QT, LANES), 0)

        for t in range(k_tiles):
            tile = kv[at_tile(t), :].astype(F32)
            turned = jnp.transpose(tile).astype(BF16)
            kt[:, at_tile(t)] = turned[0:HEAD_DIM]
            vt[0:HEAD_DIM, at_tile(t)] = turned[HEAD_DIM:LANES]
            dead = jnp.logical_and(tile_lane == HEAD_DIM, tile_row >= limit(t))
            kb[at_tile(t), :] = jnp.where(tile_lane < HEAD_DIM, tile, jnp.where(dead, NEG, 0.0)).astype(BF16)
        vt[HEAD_DIM:, :] = jnp.ones((ONES, ext), BF16)
        key_at = lax.broadcasted_iota(jnp.int32, (QT, QT), 0)
        query_at = lax.broadcasted_iota(jnp.int32, (QT, QT), 1)

        def scores(a, j, top):
            s = dot(kb[at_tile(a + j + first_tile), :], qs[at_tile(a), :], NT_DIMS)
            if j == 0:
                s = jnp.where(key_at >= query_at, s, NEG)
            if j == tiles - 1:
                s = jnp.where(key_at <= query_at, s, NEG)
            s_sc[a % 2, j] = s
            return jnp.maximum(top, jnp.max(s.reshape(QT // 8, 8, QT), axis=0))

        tops = [jnp.full((8, QT), NEG, F32) for _ in range(q_tiles)]
        for j in range(tiles):
            tops[0] = scores(0, j, tops[0])
        for a in range(q_tiles):
            top = jnp.max(tops[a], axis=0, keepdims=True)
            for j in range(tiles):
                if a + 1 < q_tiles:
                    tops[a + 1] = scores(a + 1, j, tops[a + 1])
                e = jnp.exp(s_sc[a % 2, j] - top)
                e_ref[a, at_tile(j), :] = e.astype(BF16)
            keys = slice((a + first_tile) * QT, (a + first_tile + tiles) * QT)
            out = dot(vt[:, keys], e_ref[a], NN_DIMS)
            inverse = 1.0 / out[HEAD_DIM : HEAD_DIM + 1]
            inv_ref[a] = inverse
            out_ref[a] = out[0:HEAD_DIM] * inverse

    exps, inverse, outs, kv, kt, qz = call(
        score_body,
        [
            vmem((q_tiles, tiles * QT, QT)),
            vmem((q_tiles, 1, QT), F32),
            vmem((q_tiles, HEAD_DIM, QT), F32),
            vmem((ext, LANES)),
            vmem((HEAD_DIM, ext)),
            vmem((supers, LANES)),
        ],
        smem=(0,),
        scratch=[
            pltpu.VMEM((ext, LANES), BF16),
            pltpu.VMEM((supers, LANES), BF16),
            pltpu.VMEM((HEAD_DIM + ONES, ext), BF16),
            pltpu.VMEM((2, tiles, QT, QT), F32),
        ],
        name="scores",
        cost=SCORES_COST,
    )(frame_lengths, *on_chip(both, *mine, *around))

    def key_tiles(a, ts, e_ref, inv_ref, delta_ref, kv, kt, qz, hz, acc, ds_sc, base):
        q, g = qz[at_tile(a), :], hz[at_tile(a), :]
        for i, t in enumerate(ts):
            p = e_ref[a, at_tile(t - a - first_tile), :].astype(F32) * inv_ref[a]
            slopes = dot(kv[at_tile(t), :], g, NT_DIMS)
            ds = (p * (slopes - delta_ref[a])).astype(BF16)
            ds_sc[at_tile(i), :] = ds
            part = dot(ds, q, NN_DIMS) + dot(p.astype(BF16), g, NN_DIMS)
            fresh = not any(t in seen(b) for b in range(a))
            acc[at_tile(t - base), :] = part if fresh else acc[at_tile(t - base), :] + part
        keys = slice(ts[0] * QT, (ts[-1] + 1) * QT)
        return dot(kt[:, keys], ds_sc[0 : len(ts) * QT, :], NN_DIMS)

    n_back = 2 * near

    def arrived(i, ref):
        d, phase = steps[i]
        z = lax.axis_index("z")
        partner = jnp.where((z // d) % 2 == phase, z + d, z - d)
        real = jnp.logical_and(partner >= 0, partner < z_count)
        return jnp.where(real, ref[...].astype(F32), 0.0)

    def far_body(*refs):
        grad_refs = refs[: 1 + chips]
        e_ref, inv_ref, out_ref, kv, kt, qz, hz, delta_ref, dq = refs[1 + chips : 10 + chips]
        back_refs = refs[10 + chips : -2]
        acc, ds_sc = refs[-2:]
        z = lax.axis_index("z")
        low = lax.broadcasted_iota(jnp.int32, (half, LANES), 1) < HEAD_DIM
        for member, take in arrivals(my_chip(), my_core(), grad_refs[0], grad_refs[1], grad_refs[2:]):
            g = take().astype(F32)
            for i, part in enumerate((pltpu.roll(g, HEAD_DIM, 1), g)):
                at = pl.ds(pl.multiple_of(member * rows + i * half, half), half)
                hz[at, :] = jnp.where(low, 0.0, part).astype(BF16)
        for a in range(q_tiles):
            g = jnp.transpose(hz[at_tile(a), :].astype(F32))[HEAD_DIM:LANES]
            delta_ref[a] = jnp.sum(g * out_ref[a], axis=0, keepdims=True)
        for t in range(k_tiles):
            if not any(t in seen(a) for a in range(q_tiles)):
                acc[at_tile(t), :] = jnp.zeros((QT, LANES), F32)
        for a in range(q_tiles):
            left = [t for t in seen(a) if t < own_tiles[0]]
            right = [t for t in seen(a) if t > own_tiles[-1]]
            dq[a] = sum(
                key_tiles(a, ts, e_ref, inv_ref, delta_ref, kv, kt, qz, hz, acc, ds_sc.at[side], 0)
                for side, ts in enumerate((left, right))
            )
        for i, (d, phase) in enumerate(steps):
            odd = ((z // d) % 2) == 1
            right = odd if phase else jnp.logical_not(odd)
            side = jnp.where(right, near + d, near - d) * supers
            back_refs[i][...] = acc[pl.ds(pl.multiple_of(side, supers), supers), :].astype(BF16)

    far = call(
        far_body,
        [vmem((supers, LANES)), vmem((q_tiles, 1, QT), F32), vmem((q_tiles, HEAD_DIM, QT), F32)]
        + [vmem((supers, LANES))] * n_back,
        scratch=[pltpu.VMEM((ext, LANES), F32), pltpu.VMEM((2, tiles * QT, QT), BF16)],
        name="far",
        cost=FAR_COST,
    )(*on_chip(*grads, exps, inverse, outs, kv, kt, qz))
    hz, delta, dq_far = far[:3]
    back = [step(far[3 + i], d, phase) for i, (d, phase) in enumerate(steps)]

    hb = block // 2

    def near_body(*refs):
        e_ref, inv_ref, delta_ref, kv, kt, qz, hz, far_ref = refs[:8]
        acc, dq_ref = refs[8:10]
        dq_sc, ds_sc = refs[-2:]
        for a in range(q_tiles):
            dq = far_ref[a] + key_tiles(
                a, own_tiles, e_ref, inv_ref, delta_ref, kv, kt, qz, hz, acc, ds_sc.at[a % 2], own_tiles[0]
            )
            dq_sc[at_tile(a), 0:HEAD_DIM] = jnp.transpose(dq * scale)
        if group == 1:
            dq_ref[0] = dq_sc[:, 0:HEAD_DIM].astype(BF16)
            return
        y = lax.axis_index("y")
        for ref, slot in ((dq_ref, y), (refs[10], 1 - y)):
            at = pl.multiple_of(slot * block, block)
            upper = dq_sc[pl.ds(at, hb), 0:HEAD_DIM]
            lower = dq_sc[pl.ds(pl.multiple_of(at + hb, hb), hb), 0:HEAD_DIM]
            ref[...] = jnp.concatenate([upper, lower], axis=1).astype(BF16)

    results = call(
        near_body,
        [vmem((supers, LANES), F32)]
        + ([arr((1, block, HEAD_DIM))] if group == 1 else [vmem((hb, LANES))] * 2),
        scratch=[
            pltpu.VMEM((supers, LANES), F32),
            pltpu.VMEM((2, supers, QT), BF16),
        ],
        name="near",
        cost=NEAR_COST,
    )(*on_chip(exps, inverse, delta, kv, kt, qz, hz, dq_far))
    own, dq = results[:2]
    dres_keep, dres_send, _ = lax.optimization_barrier((dres_keep, dres_send, results[0]))
    dres_got = core_swap(dres_send)
    dres = [dres_keep, dres_got] + exchange(
        dres_keep, dres_got, heads_axis // 2, lambda: lax.axis_index("head") // 2, "regroup_resid"
    )


    if group == 1:

        def last_body(*refs):
            total = refs[0][...]
            for i in range(n_back):
                total = total + arrived(i, refs[1 + i])
            total = total.astype(BF16)
            refs[-2][0] = total[:, 0:HEAD_DIM]
            refs[-1][0] = total[:, HEAD_DIM:LANES]
            resid_out(refs[1 + n_back : 1 + n_back + n_dres], refs[-3])

        d_resid, d_key, d_value = call(last_body, [dres_shape] + [arr((1, block, HEAD_DIM))] * 2, name="last")(
            *on_chip(own, *back, *dres)
        )
        return d_resid, dq, d_key, d_value

    def y_swap(x):
        return lax.ppermute(x, mesh_axes, everyone(lambda h, z, y: (h, z, 1 - y)))

    dq_other = y_swap(results[2])

    def sum_body(own_ref, *refs):
        keep_ref, send_ref = refs[-2:]
        total = own_ref[...]
        for i in range(n_back):
            total = total + arrived(i, refs[i])
        total = total.astype(BF16)
        first = lax.axis_index("y") == 0
        keep_ref[...] = jnp.where(first, total[0:block], total[block:supers])
        send_ref[...] = jnp.where(first, total[block:supers], total[0:block])

    keep, send = call(sum_body, [vmem((block, LANES))] * 2, name="sum")(*on_chip(own, *back))
    other = y_swap(send)

    def last_body(*refs):
        keep_ref, other_ref, dq_keep_ref, dq_other_ref = refs[:4]
        dq_ref, dk_ref, dv_ref = refs[-3:]
        resid_out(refs[4 : 4 + n_dres], refs[-4])
        first = lax.axis_index("y") == 0
        low = lax.broadcasted_iota(jnp.int32, (block, LANES), 1) < HEAD_DIM

        def ordered(mine_ref, peer_ref):
            mine, peer = mine_ref[...].astype(F32), peer_ref[...].astype(F32)
            return jnp.where(first, mine, peer), jnp.where(first, peer, mine)

        lo, up = ordered(keep_ref, other_ref)
        dk_ref[0] = jnp.where(low, lo, pltpu.roll(up, HEAD_DIM, 1)).astype(BF16)
        dv_ref[0] = jnp.where(low, pltpu.roll(lo, HEAD_DIM, 1), up).astype(BF16)
        lo, up = ordered(dq_keep_ref, dq_other_ref)
        low = low[0:hb]
        dq_ref[0, 0:hb, :] = jnp.where(low, lo, pltpu.roll(up, HEAD_DIM, 1)).astype(BF16)
        dq_ref[0, hb:block, :] = jnp.where(low, pltpu.roll(lo, HEAD_DIM, 1), up).astype(BF16)

    d_resid, d_query, d_key, d_value = call(
        last_body, [dres_shape] + [arr((1, block, LANES))] * 3, name="last"
    )(*on_chip(keep, other, dq, dq_other, *dres))
    return d_resid, d_query, d_key, d_value


def solution(mesh):
    heads_axis = mesh.shape["head"]
    ctx_count = mesh.shape["ctx"]

    def run(query, *rest):
        group = query.shape[2] // HEAD_DIM // heads_axis
        z_count = ctx_count // group
        fine = Mesh(mesh.devices.reshape(heads_axis, z_count, group), ("head", "z", "y"))
        rows_spec = P(("z", "y"), "head", None)
        cols_spec = P(("z", "y"), None, "head")
        sizes = (heads_axis, z_count, group)
        return jax.shard_map(
            lambda *args: on_device(sizes, *args),
            mesh=fine,
            in_specs=(rows_spec,) * 5 + (P(),) * 3,
            out_specs=(cols_spec,) * 4,
            check_vma=False,
        )(query, *rest)

    return run
```

time: 58.6 us -> 51.5 us (0.88)
  the two profiles are of different devices: /device:TPU:12 before, /device:TPU:0 now
where the time goes in v3:
time: 51.5 us; the launch traced here: 51.4 us
  starting transfers between devices  19.5 us (38%)
  Pallas kernels  18.3 us (36%)
  waiting for transfers between devices  12.8 us (25%)
  between operations  0.77 us (1%)
    pallas_call x10, Pallas kernels, run(): pl.pallas_call(body, out_shape=outs, in_specs=[pl.BlockSpec(memory_space=...  16.8 us
    ppermute x7, starting transfers between devices, exchange(): lax.ppermute(part, mesh_axes, everyone(target(m)))  9.55 us
    ppermute x4, starting transfers between devices, step(): return lax.ppermute(x, mesh_axes, everyone(target))  4.68 us
    ppermute x7, waiting for transfers between devices, exchange(): lax.ppermute(part, mesh_axes, everyone(target(m)))  4.31 us
    ppermute x2, waiting for transfers between devices, y_swap(): return lax.ppermute(x, mesh_axes, everyone(lambda h, z, y: (h, z, 1 - y)))  3.65 us
    ppermute x4, waiting for transfers between devices, core_swap(): return lax.ppermute(x, mesh_axes, everyone(lambda h, z, y: (h ^ 1, z, y)))  3.3 us
    ppermute x2, starting transfers between devices, y_swap(): return lax.ppermute(x, mesh_axes, everyone(lambda h, z, y: (h, z, 1 - y)))  2.09 us
    ppermute x1, starting transfers between devices, on_device(): lax.ppermute(second, mesh_axes, everyone(inside))  1.55 us
  transfers between devices with their start and end apart: 19, of which 7 were waited for; matrix products, arithmetic and copies ran while one was open for 0% of the time, Pallas kernels for 24%

profile of v3, /device:TPU:0, one launch (start us, length us, event | category | flops | bytes accessed | tf_op | source)
XLA Modules:
  0.0 51.4 jit_solution(7994597894270684682)
XLA Ops:
  0.6 1.5 %pack.1 = (bf16[4,192,128]{2,1,0:T(8,128)(2,1)S(1)}, bf16[4,192,128]{2,1,0:T(8,128)(2,1)S(1)}, bf16[48,1024]{1,0:T(8,128)(2,1)S(1)}, bf16[48,1024]{1,0:T(8,128)(...) custom-call(bf16[1,128,512]{2,1,0:T(8,128)(2,1)} %q_hbm.1, ...), custom_call_target="tpu_custom_call" | custom-call | tf_op jit(solution)/shard_map/pack/pallas_call | solution.py:151
  2.1 0.5 %collective-permute-start = (bf16[4,192,128]{2,1,0:T(8,128)(2,1)S(1)}, bf16[4,192,128]{2,1,0:T(8,128)(2,1)S(1)}, u32[]{:S(2)}, u32[]{:S(2)}) collective-permute-start(bf16[4,192,128]{2,1,0:T(8,128)(2,1)S(1)} %get-tuple-element.40), channel_id=1, source_target_pairs={{0,8},{1,9},{2,10},{3,11},{4,12},{5,13},{6,14},{7,15},{8,0},{9,1},... | collective-permute-start | bytes 589832 | tf_op jit(solution)/shard_map/ppermute | solution.py:175
  2.6 1.1 %collective-permute-done.got_ref.refs_3_ = bf16[4,192,128]{2,1,0:T(8,128)(2,1)S(1)} collective-permute-done((bf16[4,192,128]{2,1,0:T(8,128)(2,1)S(1)}, bf16[4,192,128]{2,1,0:T(8,128)(2,1)S(1)}, u32[]{:S(2)}, u32[]{:S(2)}) %collective-permute-start) | collective-permute-done | bytes 196640 | tf_op jit(solution)/shard_map/ppermute | solution.py:175
  3.7 2.9 %collective-permute-start.1 = (bf16[2,192,128]{2,1,0:T(8,128)(2,1)S(1)}, bf16[2,192,128]{2,1,0:T(8,128)(2,1)S(1)}, u32[]{:S(2)}, u32[]{:S(2)}) collective-permute-start(bf16[2,192,128]{2,1,0:T(8,128)(2,1)S(1)} %get-tuple-element.41), channel_id=1, source_target_pairs={{0,16},{1,17},{2,18},{3,19},{4,20},{5,21},{6,22},{7,23},{8,24},{9,... | collective-permute-start | bytes 294920 | tf_op jit(solution)/shard_map/ppermute | solution.py:201
  6.6 1.5 %collective-permute-start.2 = (bf16[2,192,128]{2,1,0:T(8,128)(2,1)S(1)}, bf16[2,192,128]{2,1,0:T(8,128)(2,1)S(1)}, u32[]{:S(2)}, u32[]{:S(2)}) collective-permute-start(bf16[2,192,128]{2,1,0:T(8,128)(2,1)S(1)} %get-tuple-element.42), channel_id=1, source_target_pairs={{0,1},{1,0},{2,3},{3,2},{4,5},{5,4},{6,7},{7,6},{8,9},{9,8},{10,11... | collective-permute-start | bytes 294920 | tf_op jit(solution)/shard_map/ppermute | solution.py:201
  8.2 0.0 collective-permute-start.3
  8.2 0.0 collective-permute-start.6
  8.2 0.5 collective-permute-start.8
  8.7 1.1 %collective-permute-done.1.refs_0_.refs_4_ = bf16[2,192,128]{2,1,0:T(8,128)(2,1)S(1)} collective-permute-done((bf16[2,192,128]{2,1,0:T(8,128)(2,1)S(1)}, bf16[2,192,128]{2,1,0:T(8,128)(2,1)S(1)}, u32[]{:S(2)}, u32[]{:S(2)}) %collective-permute-start.1) | collective-permute-done | bytes 98336 | tf_op jit(solution)/shard_map/ppermute | solution.py:201
  9.8 1.5 %collective-permute-start.7 = (bf16[48,1024]{1,0:T(8,128)(2,1)S(1)}, bf16[48,1024]{1,0:T(8,128)(2,1)S(1)}, u32[]{:S(2)}, u32[]{:S(2)}) collective-permute-start(bf16[48,1024]{1,0:T(8,128)(2,1)S(1)} %get-tuple-element.49), channel_id=1, source_target_pairs={{0,24},{1,25},{2,26},{3,27},{4,28},{5,29},{6,30},{7,31},{8,16},{9,... | collective-permute-start | bytes 294920 | tf_op jit(solution)/shard_map/ppermute | solution.py:235
  11.4 3.2 %collective-permute-done.2.refs_1_.refs_5_ = bf16[2,192,128]{2,1,0:T(8,128)(2,1)S(1)} collective-permute-done((bf16[2,192,128]{2,1,0:T(8,128)(2,1)S(1)}, bf16[2,192,128]{2,1,0:T(8,128)(2,1)S(1)}, u32[]{:S(2)}, u32[]{:S(2)}) %collective-permute-start.2) | collective-permute-done | bytes 98336 | tf_op jit(solution)/shard_map/ppermute | solution.py:201
  14.5 0.0 collective-permute-done.3.refs_2_.refs_6_
  14.6 0.1 collective-permute-start.5
  14.7 4.5 %collective-permute-start.4 = (bf16[1024,128]{1,0:T(8,128)(2,1)S(1)}, bf16[1024,128]{1,0:T(8,128)(2,1)S(1)}, u32[]{:S(2)}, u32[]{:S(2)}) collective-permute-start(bf16[1024,128]{1,0:T(8,128)(2,1)S(1)} %keys.1.refs_1_), channel_id=1, source_target_pairs={{0,2},{1,3},{2,0},{3,1},{4,6},{5,7},{6,4},{7,5},{8,10},{9,11},{10,... | collective-permute-start | bytes 786440 | tf_op jit(solution)/shard_map/ppermute | solution.py:182
  19.1 0.0 collective-permute-done.6.core_ref
  19.1 0.0 collective-permute-done.8.outside_ref
  19.1 0.0 collective-permute-done.7.inside_ref
  19.1 0.0 copy-start
  19.2 4.5 %conv.1 = (bf16[4,64,128]{2,1,0:T(8,128)(2,1)S(1)}, bf16[4,64,128]{2,1,0:T(8,128)(2,1)S(1)}, bf16[2,128,256]{2,1,0:T(8,128)(2,1)S(1)}, bf16[2,128,256]{2,1,0:T(8,128)(2,1)S(1)}) custom-call(bf16[1,128,1024]{2,1,0:T(8,128)(2,1)S(1)} %get-tuple-element.46.resid_ref, bf16[1,128,1024]{2,1,0:T(8,128)(2,1)S(1)} %get-tuple-element.47.grad_ref, ...), custom_call_target="tpu_custom_call" | custom-call | flops 6000000000 | tf_op jit(solution)/shard_map/conv/pallas_call | solution.py:38
  23.7 0.1 collective-permute-start.9
  23.7 1.2 %collective-permute-done.9.got_ref.refs_1_ = bf16[4,64,128]{2,1,0:T(8,128)(2,1)S(1)} collective-permute-done((bf16[4,64,128]{2,1,0:T(8,128)(2,1)S(1)}, bf16[4,64,128]{2,1,0:T(8,128)(2,1)S(1)}, u32[]{:S(2)}, u32[]{:S(2)}) %collective-permute-start.9) | collective-permute-done | bytes 65568 | tf_op jit(solution)/shard_map/ppermute | solution.py:175
  25.0 0.1 collective-permute-start.10
  25.1 1.2 %collective-permute-start.11 = (bf16[2,64,128]{2,1,0:T(8,128)(2,1)S(1)}, bf16[2,64,128]{2,1,0:T(8,128)(2,1)S(1)}, u32[]{:S(2)}, u32[]{:S(2)}) collective-permute-start(bf16[2,64,128]{2,1,0:T(8,128)(2,1)S(1)} %get-tuple-element.54), channel_id=1, source_target_pairs={{0,1},{1,0},{2,3},{3,2},{4,5},{5,4},{6,7},{7,6},{8,9},{9,8},{10,11... | collective-permute-start | bytes 98312 | tf_op jit(solution)/shard_map/ppermute | solution.py:201
  26.3 2.3 %collective-permute-start.12 = (bf16[2,64,128]{2,1,0:T(8,128)(2,1)S(1)}, bf16[2,64,128]{2,1,0:T(8,128)(2,1)S(1)}, u32[]{:S(2)}, u32[]{:S(2)}) collective-permute-start(bf16[2,64,128]{2,1,0:T(8,128)(2,1)S(1)} %get-tuple-element.55), channel_id=1, source_target_pairs={{0,17},{1,16},{2,19},{3,18},{4,21},{5,20},{6,23},{7,22},{8,25},{9,... | collective-permute-start | bytes 98312 | tf_op jit(solution)/shard_map/ppermute | solution.py:201
  28.5 0.0 collective-permute-done.5.refs_8_
  28.5 0.0 collective-permute-done.4.refs_7_
  28.5 0.0 copy-done
  28.6 4.8 %scores.1 = (bf16[4,2304,256]{2,1,0:T(8,128)(2,1)S(1)}, f32[4,1,256]{2,1,0:T(1,128)S(1)}, f32[4,64,256]{2,1,0:T(8,128)S(1)}, bf16[3072,128]{1,0:T(8,128)(2,1)S(1...) custom-call(s32[8]{0:T(128)S(1)} %copy-done, bf16[1024,128]{1,0:T(8,128)(2,1)S(1)} %keys.1.refs_1_, ...), custom_call_target="tpu_custom_call" | custom-call | flops 8999999488 | tf_op jit(solution)/shard_map/scores/pallas_call | solution.py:38
  33.4 0.0 collective-permute-done.10.refs_2_
  33.4 0.0 collective-permute-done.11.refs_3_
  33.4 0.0 collective-permute-done.12.refs_4_
  33.4 3.5 %far.1 = (bf16[1024,128]{1,0:T(8,128)(2,1)S(1)}, f32[4,1,256]{2,1,0:T(1,128)S(1)}, f32[4,64,256]{2,1,0:T(8,128)S(1)}, bf16[1024,128]{1,0:T(8,128)(2,1)S(1)}, bf16[1024,128]{1,0:T(8,128)(2,1)S(1)}) custom-call(bf16[4,64,128]{2,1,0:T(8,128)(2,1)S(1)} %get-tuple-element.51.keep_ref.refs_0_, bf16[4,64,128]{2,1,0:T(8,128)(2,1)S(1)} %collective-permute-done.9.got_ref.refs_1_, ...), custom_call_target="tpu_custom_call" | custom-call | flops 4000000000 | tf_op jit(solution)/shard_map/far/pallas_call | solution.py:38
  36.9 0.1 collective-permute-start.13
  37.0 0.1 collective-permute-start.14
  37.1 2.8 %near.1 = (f32[1024,128]{1,0:T(8,128)S(1)}, bf16[256,128]{1,0:T(8,128)(2,1)S(1)}, bf16[256,128]{1,0:T(8,128)(2,1)S(1)}) custom-call(bf16[4,2304,256]{2,1,0:T(8,128)(2,1)S(1)} %get-tuple-element.44.refs_5_.refs_0_, f32[4,1,256]{2,1,0:T(1,128)S(1)} %get-tuple-element.45.refs_6_.refs_1_, f32[4,1,256]{2,1,0:T(1,128)S(1)} %get-tuple-element.60.refs_2_, ...), custom_call_target="tpu_custom_call" | custom-call | flops 4000000000 | tf_op jit(solution)/shard_map/near/pallas_call | solution.py:38
  39.9 0.6 %collective-permute-start.17 = (bf16[2,128,256]{2,1,0:T(8,128)(2,1)S(1)}, bf16[2,128,256]{2,1,0:T(8,128)(2,1)S(1)}, u32[]{:S(2)}, u32[]{:S(2)}) collective-permute-start(bf16[2,128,256]{2,1,0:T(8,128)(2,1)S(1)} %get-tuple-element.73), channel_id=1, source_target_pairs={{0,8},{1,9},{2,10},{3,11},{4,12},{5,13},{6,14},{7,15},{8,0},{9,1},... | collective-permute-start | bytes 393224 | tf_op jit(solution)/shard_map/ppermute | solution.py:175
  40.4 1.0 %collective-permute-done.17.got_ref.refs_5_ = bf16[2,128,256]{2,1,0:T(8,128)(2,1)S(1)} collective-permute-done((bf16[2,128,256]{2,1,0:T(8,128)(2,1)S(1)}, bf16[2,128,256]{2,1,0:T(8,128)(2,1)S(1)}, u32[]{:S(2)}, u32[]{:S(2)}) %collective-permute-start.17) | collective-permute-done | bytes 131104 | tf_op jit(solution)/shard_map/ppermute | solution.py:175
  41.4 1.5 %collective-permute-start.18 = (bf16[2,128,256]{2,1,0:T(8,128)(2,1)S(1)}, bf16[2,128,256]{2,1,0:T(8,128)(2,1)S(1)}, u32[]{:S(2)}, u32[]{:S(2)}) collective-permute-start(bf16[2,128,256]{2,1,0:T(8,128)(2,1)S(1)} %regroup_resid.1), channel_id=1, source_target_pairs={{0,16},{1,17},{2,18},{3,19},{4,20},{5,21},{6,22},{7,23},{8,24},{9,... | collective-permute-start | bytes 393224 | tf_op jit(solution)/shard_map/ppermute | solution.py:201
  43.0 1.5 %collective-permute-done.13.refs_0_ = bf16[1024,128]{1,0:T(8,128)(2,1)S(1)} collective-permute-done((bf16[1024,128]{1,0:T(8,128)(2,1)S(1)}, bf16[1024,128]{1,0:T(8,128)(2,1)S(1)}, u32[]{:S(2)}, u32[]{:S(2)}) %collective-permute-start.13) | collective-permute-done | bytes 262176 | tf_op jit(solution)/shard_map/ppermute | solution.py:182
  44.4 0.0 collective-permute-done.14.refs_1_
  44.5 0.2 sum.1
  44.6 1.2 %collective-permute-start.15 = (bf16[512,128]{1,0:T(8,128)(2,1)S(1)}, bf16[512,128]{1,0:T(8,128)(2,1)S(1)}, u32[]{:S(2)}, u32[]{:S(2)}) collective-permute-start(bf16[512,128]{1,0:T(8,128)(2,1)S(1)} %get-tuple-element.67), channel_id=1, source_target_pairs={{0,1},{1,0},{2,3},{3,2},{4,5},{5,4},{6,7},{7,6},{8,9},{9,8},{10,11... | collective-permute-start | bytes 393224 | tf_op jit(solution)/shard_map/ppermute | solution.py:562
  45.8 0.9 %collective-permute-start.16 = (bf16[256,128]{1,0:T(8,128)(2,1)S(1)}, bf16[256,128]{1,0:T(8,128)(2,1)S(1)}, u32[]{:S(2)}, u32[]{:S(2)}) collective-permute-start(bf16[256,128]{1,0:T(8,128)(2,1)S(1)} %get-tuple-element.69), channel_id=1, source_target_pairs={{0,1},{1,0},{2,3},{3,2},{4,5},{5,4},{6,7},{7,6},{8,9},{9,8},{10,11... | collective-permute-start | bytes 196616 | tf_op jit(solution)/shard_map/ppermute | solution.py:562
  46.7 3.6 %collective-permute-done.16.refs_3_ = bf16[256,128]{1,0:T(8,128)(2,1)S(1)} collective-permute-done((bf16[256,128]{1,0:T(8,128)(2,1)S(1)}, bf16[256,128]{1,0:T(8,128)(2,1)S(1)}, u32[]{:S(2)}, u32[]{:S(2)}) %collective-permute-start.16) | collective-permute-done | bytes 65568 | tf_op jit(solution)/shard_map/ppermute | solution.py:562
  50.4 0.0 collective-permute-done.18.refs_6_
  50.4 0.0 collective-permute-done.15.refs_1_
  50.4 1.0 %last.1 = (bf16[1,512,256]{2,1,0:T(8,128)(2,1)}, bf16[1,512,128]{2,1,0:T(8,128)(2,1)}, bf16[1,512,128]{2,1,0:T(8,128)(2,1)}, bf16[1,512,128]{2,1,0:T(8,128)(2,1)}) custom-call(bf16[512,128]{1,0:T(8,128)(2,1)S(1)} %get-tuple-element.66.refs_0_, bf16[512,128]{1,0:T(8,128)(2,1)S(1)} %collective-permute-done.15.refs_1_, ...), custom_call_target="tpu_custom_call" | custom-call | tf_op jit(solution)/shard_map/last/pallas_call | solution.py:38
  (4 shorter events, 0.1 us)
Async XLA Ops:
  2.1 1.6 %collective-permute-start = (bf16[4,192,128]{2,1,0:T(8,128)(2,1)S(1)}, bf16[4,192,128]{2,1,0:T(8,128)(2,1)S(1)}, u32[]{:S(2)}, u32[]{:S(2)}) collective-permute-start(bf16[4,192,128]{2,1,0:T(8,128)(2,1)S(1)} %get-tuple-element.40), channel_id=1, source_target_pairs={{0,8},{1,9},{2,10},{3,11},{4,12},{5,13},{6,14},{7,15},{8,0},{9,1},... | collective-permute-start | bytes 589832 | tf_op jit(solution)/shard_map/ppermute | solution.py:175
  3.7 6.1 %collective-permute-start.1 = (bf16[2,192,128]{2,1,0:T(8,128)(2,1)S(1)}, bf16[2,192,128]{2,1,0:T(8,128)(2,1)S(1)}, u32[]{:S(2)}, u32[]{:S(2)}) collective-permute-start(bf16[2,192,128]{2,1,0:T(8,128)(2,1)S(1)} %get-tuple-element.41), channel_id=1, source_target_pairs={{0,16},{1,17},{2,18},{3,19},{4,20},{5,21},{6,22},{7,23},{8,24},{9,... | collective-permute-start | bytes 294920 | tf_op jit(solution)/shard_map/ppermute | solution.py:201
  6.6 7.9 %collective-permute-start.2 = (bf16[2,192,128]{2,1,0:T(8,128)(2,1)S(1)}, bf16[2,192,128]{2,1,0:T(8,128)(2,1)S(1)}, u32[]{:S(2)}, u32[]{:S(2)}) collective-permute-start(bf16[2,192,128]{2,1,0:T(8,128)(2,1)S(1)} %get-tuple-element.42), channel_id=1, source_target_pairs={{0,1},{1,0},{2,3},{3,2},{4,5},{5,4},{6,7},{7,6},{8,9},{9,8},{10,11... | collective-permute-start | bytes 294920 | tf_op jit(solution)/shard_map/ppermute | solution.py:201
  8.2 6.4 %collective-permute-start.3 = (bf16[2,192,128]{2,1,0:T(8,128)(2,1)S(1)}, bf16[2,192,128]{2,1,0:T(8,128)(2,1)S(1)}, u32[]{:S(2)}, u32[]{:S(2)}) collective-permute-start(bf16[2,192,128]{2,1,0:T(8,128)(2,1)S(1)} %get-tuple-element.43), channel_id=1, source_target_pairs={{0,17},{1,16},{2,19},{3,18},{4,21},{5,20},{6,23},{7,22},{8,25},{9,... | collective-permute-start | bytes 294920 | tf_op jit(solution)/shard_map/ppermute | solution.py:201
  8.2 10.9 %collective-permute-start.6 = (bf16[48,1024]{1,0:T(8,128)(2,1)S(1)}, bf16[48,1024]{1,0:T(8,128)(2,1)S(1)}, u32[]{:S(2)}, u32[]{:S(2)}) collective-permute-start(bf16[48,1024]{1,0:T(8,128)(2,1)S(1)} %get-tuple-element.48), channel_id=1, source_target_pairs={{0,8},{1,9},{2,10},{3,11},{4,12},{5,13},{6,14},{7,15},{8,0},{9,1},... | collective-permute-start | bytes 294920 | tf_op jit(solution)/shard_map/ppermute | solution.py:175
  8.2 10.9 %collective-permute-start.8 = (bf16[48,1024]{1,0:T(8,128)(2,1)S(1)}, bf16[48,1024]{1,0:T(8,128)(2,1)S(1)}, u32[]{:S(2)}, u32[]{:S(2)}) collective-permute-start(bf16[48,1024]{1,0:T(8,128)(2,1)S(1)} %get-tuple-element.49), channel_id=1, source_target_pairs={{0,8},{1,24},{2,25},{3,26},{4,27},{5,28},{6,29},{7,30},{8,0},{9,16... | collective-permute-start | bytes 294920 | tf_op jit(solution)/shard_map/ppermute | solution.py:236
  9.8 9.3 %collective-permute-start.7 = (bf16[48,1024]{1,0:T(8,128)(2,1)S(1)}, bf16[48,1024]{1,0:T(8,128)(2,1)S(1)}, u32[]{:S(2)}, u32[]{:S(2)}) collective-permute-start(bf16[48,1024]{1,0:T(8,128)(2,1)S(1)} %get-tuple-element.49), channel_id=1, source_target_pairs={{0,24},{1,25},{2,26},{3,27},{4,28},{5,29},{6,30},{7,31},{8,16},{9,... | collective-permute-start | bytes 294920 | tf_op jit(solution)/shard_map/ppermute | solution.py:235
  14.6 14.0 %collective-permute-start.5 = (bf16[1024,128]{1,0:T(8,128)(2,1)S(1)}, bf16[1024,128]{1,0:T(8,128)(2,1)S(1)}, u32[]{:S(2)}, u32[]{:S(2)}) collective-permute-start(bf16[1024,128]{1,0:T(8,128)(2,1)S(1)} %keys.1.refs_1_), channel_id=1, source_target_pairs={{0,8},{1,9},{2,4},{3,5},{4,2},{5,3},{6,14},{7,15},{8,0},{9,1},{10,... | collective-permute-start | bytes 786440 | tf_op jit(solution)/shard_map/ppermute | solution.py:182
  14.7 13.9 %collective-permute-start.4 = (bf16[1024,128]{1,0:T(8,128)(2,1)S(1)}, bf16[1024,128]{1,0:T(8,128)(2,1)S(1)}, u32[]{:S(2)}, u32[]{:S(2)}) collective-permute-start(bf16[1024,128]{1,0:T(8,128)(2,1)S(1)} %keys.1.refs_1_), channel_id=1, source_target_pairs={{0,2},{1,3},{2,0},{3,1},{4,6},{5,7},{6,4},{7,5},{8,10},{9,11},{10,... | collective-permute-start | bytes 786440 | tf_op jit(solution)/shard_map/ppermute | solution.py:182
  19.1 9.4 %copy-start = (s32[8]{0:T(128)S(1)}, s32[8]{0:T(128)}, u32[]{:S(2)}) copy-start(s32[8]{0:T(128)} %refs_0_.1) | copy-start | bytes 100
  23.7 1.3 %collective-permute-start.9 = (bf16[4,64,128]{2,1,0:T(8,128)(2,1)S(1)}, bf16[4,64,128]{2,1,0:T(8,128)(2,1)S(1)}, u32[]{:S(2)}, u32[]{:S(2)}) collective-permute-start(bf16[4,64,128]{2,1,0:T(8,128)(2,1)S(1)} %get-tuple-element.52), channel_id=1, source_target_pairs={{0,8},{1,9},{2,10},{3,11},{4,12},{5,13},{6,14},{7,15},{8,0},{9,1},... | collective-permute-start | bytes 196616 | tf_op jit(solution)/shard_map/ppermute | solution.py:175
  25.0 8.4 %collective-permute-start.10 = (bf16[2,64,128]{2,1,0:T(8,128)(2,1)S(1)}, bf16[2,64,128]{2,1,0:T(8,128)(2,1)S(1)}, u32[]{:S(2)}, u32[]{:S(2)}) collective-permute-start(bf16[2,64,128]{2,1,0:T(8,128)(2,1)S(1)} %get-tuple-element.53), channel_id=1, source_target_pairs={{0,16},{1,17},{2,18},{3,19},{4,20},{5,21},{6,22},{7,23},{8,24},{9,... | collective-permute-start | bytes 98312 | tf_op jit(solution)/shard_map/ppermute | solution.py:201
  25.1 8.3 %collective-permute-start.11 = (bf16[2,64,128]{2,1,0:T(8,128)(2,1)S(1)}, bf16[2,64,128]{2,1,0:T(8,128)(2,1)S(1)}, u32[]{:S(2)}, u32[]{:S(2)}) collective-permute-start(bf16[2,64,128]{2,1,0:T(8,128)(2,1)S(1)} %get-tuple-element.54), channel_id=1, source_target_pairs={{0,1},{1,0},{2,3},{3,2},{4,5},{5,4},{6,7},{7,6},{8,9},{9,8},{10,11... | collective-permute-start | bytes 98312 | tf_op jit(solution)/shard_map/ppermute | solution.py:201
  26.3 7.1 %collective-permute-start.12 = (bf16[2,64,128]{2,1,0:T(8,128)(2,1)S(1)}, bf16[2,64,128]{2,1,0:T(8,128)(2,1)S(1)}, u32[]{:S(2)}, u32[]{:S(2)}) collective-permute-start(bf16[2,64,128]{2,1,0:T(8,128)(2,1)S(1)} %get-tuple-element.55), channel_id=1, source_target_pairs={{0,17},{1,16},{2,19},{3,18},{4,21},{5,20},{6,23},{7,22},{8,25},{9,... | collective-permute-start | bytes 98312 | tf_op jit(solution)/shard_map/ppermute | solution.py:201
  36.9 7.5 %collective-permute-start.13 = (bf16[1024,128]{1,0:T(8,128)(2,1)S(1)}, bf16[1024,128]{1,0:T(8,128)(2,1)S(1)}, u32[]{:S(2)}, u32[]{:S(2)}) collective-permute-start(bf16[1024,128]{1,0:T(8,128)(2,1)S(1)} %get-tuple-element.64), channel_id=1, source_target_pairs={{0,2},{1,3},{2,0},{3,1},{4,6},{5,7},{6,4},{7,5},{8,10},{9,11},{10,... | collective-permute-start | bytes 786440 | tf_op jit(solution)/shard_map/ppermute | solution.py:182
  37.0 7.5 %collective-permute-start.14 = (bf16[1024,128]{1,0:T(8,128)(2,1)S(1)}, bf16[1024,128]{1,0:T(8,128)(2,1)S(1)}, u32[]{:S(2)}, u32[]{:S(2)}) collective-permute-start(bf16[1024,128]{1,0:T(8,128)(2,1)S(1)} %get-tuple-element.65), channel_id=1, source_target_pairs={{0,8},{1,9},{2,4},{3,5},{4,2},{5,3},{6,14},{7,15},{8,0},{9,1},{10,... | collective-permute-start | bytes 786440 | tf_op jit(solution)/shard_map/ppermute | solution.py:182
  39.9 1.5 %collective-permute-start.17 = (bf16[2,128,256]{2,1,0:T(8,128)(2,1)S(1)}, bf16[2,128,256]{2,1,0:T(8,128)(2,1)S(1)}, u32[]{:S(2)}, u32[]{:S(2)}) collective-permute-start(bf16[2,128,256]{2,1,0:T(8,128)(2,1)S(1)} %get-tuple-element.73), channel_id=1, source_target_pairs={{0,8},{1,9},{2,10},{3,11},{4,12},{5,13},{6,14},{7,15},{8,0},{9,1},... | collective-permute-start | bytes 393224 | tf_op jit(solution)/shard_map/ppermute | solution.py:175
  41.4 8.9 %collective-permute-start.18 = (bf16[2,128,256]{2,1,0:T(8,128)(2,1)S(1)}, bf16[2,128,256]{2,1,0:T(8,128)(2,1)S(1)}, u32[]{:S(2)}, u32[]{:S(2)}) collective-permute-start(bf16[2,128,256]{2,1,0:T(8,128)(2,1)S(1)} %regroup_resid.1), channel_id=1, source_target_pairs={{0,16},{1,17},{2,18},{3,19},{4,20},{5,21},{6,22},{7,23},{8,24},{9,... | collective-permute-start | bytes 393224 | tf_op jit(solution)/shard_map/ppermute | solution.py:201
  44.6 5.7 %collective-permute-start.15 = (bf16[512,128]{1,0:T(8,128)(2,1)S(1)}, bf16[512,128]{1,0:T(8,128)(2,1)S(1)}, u32[]{:S(2)}, u32[]{:S(2)}) collective-permute-start(bf16[512,128]{1,0:T(8,128)(2,1)S(1)} %get-tuple-element.67), channel_id=1, source_target_pairs={{0,1},{1,0},{2,3},{3,2},{4,5},{5,4},{6,7},{7,6},{8,9},{9,8},{10,11... | collective-permute-start | bytes 393224 | tf_op jit(solution)/shard_map/ppermute | solution.py:562
  45.8 4.5 %collective-permute-start.16 = (bf16[256,128]{1,0:T(8,128)(2,1)S(1)}, bf16[256,128]{1,0:T(8,128)(2,1)S(1)}, u32[]{:S(2)}, u32[]{:S(2)}) collective-permute-start(bf16[256,128]{1,0:T(8,128)(2,1)S(1)} %get-tuple-element.69), channel_id=1, source_target_pairs={{0,1},{1,0},{2,3},{3,2},{4,5},{5,4},{6,7},{7,6},{8,9},{9,8},{10,11... | collective-permute-start | bytes 196616 | tf_op jit(solution)/shard_map/ppermute | solution.py:562

commit v4 on v3

--- a/solution.py
+++ b/solution.py
@@ -20,10 +20,11 @@
 NT_DIMS = (((1,), (1,)), ((), ()))
 NN_DIMS = (((1,), (0,)), ((), ()))
 VMEM_LIMIT = 12 * 1024 * 1024
-CONV_COST = (6_000_000_000, 0, 0)
+CONV_COST = (3_000_000_000, 0, 0)
 SCORES_COST = (9_000_000_000, 0, 0)
 FAR_COST = (4_000_000_000, 0, 0)
 NEAR_COST = (4_000_000_000, 0, 0)
+RESID_COST = (1_000_000_000, 0, 0)
 
 
 def dot(a, b, dims):
@@ -104,8 +105,11 @@
     def my_core():
         return lax.axis_index("head") % 2
 
+    slot = rows + half
+    edge_rows = HALO + HALF
+
     def pack_body(q_hbm, k_hbm, v_hbm, resid_ref, grad_ref, taps_ref, *refs):
-        keep_ref, send_ref, first_ref, second_ref, resid_out, grad_out, taps_out, q_ref, k_ref, v_ref, sems = refs
+        keep_ref, send_ref, second_ref, resid_out, grad_out, taps_out, q_ref, k_ref, v_ref, sems = refs
         copies = [
             pltpu.make_async_copy(source, target, sems.at[i])
             for i, (source, target) in enumerate(
@@ -121,11 +125,17 @@
         copies[0].wait()
         copies[1].wait()
         odd = core == 1
-        for side_ref, low in ((first_ref, odd), (second_ref, jnp.logical_not(odd))):
-            side_ref[0:HALO, :] = jnp.where(low, resid_out[0, 0:HALO, :], resid_out[0, rows - HALO : rows, :])
-            side_ref[HALO : HALO + HALF, :] = jnp.where(
-                low, grad_out[0, 0:HALF, :], grad_out[0, rows - HALF : rows, :]
-            )
+        resid_top, resid_low = resid_out[0, 0:HALO, :], resid_out[0, rows - HALO : rows, :]
+        grad_top, grad_low = grad_out[0, 0:HALF, :], grad_out[0, rows - HALF : rows, :]
+        second_ref[0:HALO, :] = jnp.where(odd, resid_low, resid_top)
+        second_ref[HALO:edge_rows, :] = jnp.where(odd, grad_low, grad_top)
+        resid_first = jnp.where(odd, resid_top, resid_low)
+        grad_first = jnp.where(odd, grad_top, grad_low)
+        for c in range(channels // LANES):
+            at = chips * slot + c * edge_rows
+            lane = slice(c * LANES, (c + 1) * LANES)
+            send_ref[at : at + HALO, :] = resid_first[:, lane]
+            send_ref[at + HALO : at + edge_rows, :] = grad_first[:, lane]
         for copy in copies[2:]:
             copy.wait()
         for chip in range(chips):
@@ -138,21 +148,21 @@
             ):
                 stay, leave = sides(core, [c_ref[0, low:high, c] for c in heads])
                 keep_ref[chip, at : at + high - low, width : width + HEAD_DIM] = stay
-                send_ref[chip, at : at + high - low, width : width + HEAD_DIM] = leave
-
-    slot = rows + half
+                at = at + chip * slot
+                send_ref[at : at + high - low, width : width + HEAD_DIM] = leave
+
     raw = pl.BlockSpec(memory_space=pltpu.HBM)
     on_vmem = pl.BlockSpec(memory_space=pltpu.VMEM)
     pack_outs = [
-        vmem((chips, slot, LANES)), vmem((chips, slot, LANES)),
-        vmem((HALO + HALF, channels)), vmem((HALO + HALF, channels)),
+        vmem((chips, slot, LANES)), vmem((chips * slot + edge_rows * channels // LANES, LANES)),
+        vmem((edge_rows, channels)),
         vmem((1, rows, channels)), vmem((1, rows, channels)), vmem(conv_kernel.shape),
     ]
-    keep, send, first, second, resid, upstream, taps_in = pl.pallas_call(
+    keep, send, second, resid, upstream, taps_in = pl.pallas_call(
         pack_body,
         out_shape=pack_outs,
         in_specs=[raw] * 6,
-        out_specs=[on_vmem] * 7,
+        out_specs=[on_vmem] * 6,
         scratch_shapes=[pltpu.VMEM((1, rows, width), BF16)] * 3 + [pltpu.SemaphoreType.DMA((6,))],
         compiler_params=pltpu.CompilerParams(vmem_limit_bytes=VMEM_LIMIT),
         name="pack",
@@ -181,12 +191,16 @@
 
         return lax.ppermute(x, mesh_axes, everyone(target))
 
+    def slot_of(ref, i, like):
+        size = like.shape[1]
+        return ref[i] if len(ref.shape) == 3 else ref[pl.ds(pl.multiple_of(i * size, size), size), :]
+
     def exchange(keep, got, count, index, name):
         def body(keep_ref, got_ref, *out_refs):
             me = index()
             for m, out_ref in enumerate(out_refs, 1):
                 out_ref[0] = keep_ref[me ^ m]
-                out_ref[1] = got_ref[me ^ m]
+                out_ref[1] = slot_of(got_ref, me ^ m, keep_ref)
 
         per_row = heads_axis // 2
 
@@ -201,7 +215,7 @@
         return [lax.ppermute(part, mesh_axes, everyone(target(m))) for m, part in enumerate(parts, 1)]
 
     def arrivals(me, core, keep_ref, got_ref, part_refs):
-        out = [(member_of(me, core), lambda: keep_ref[me]), (member_of(me, 1 - core), lambda: got_ref[me])]
+        out = [(member_of(me, core), lambda: keep_ref[me]), (member_of(me, 1 - core), lambda: slot_of(got_ref, me, keep_ref))]
         for m, ref in enumerate(part_refs, 1):
             out.append((member_of(me ^ m, core), lambda ref=ref: ref[0]))
             out.append((member_of(me ^ m, 1 - core), lambda ref=ref: ref[1]))
@@ -212,7 +226,9 @@
     last_head = heads_axis - 1
 
     def inside(h, z, y):
-        return (h + 1 if h % 2 else h - 1) if 0 < h < last_head else last_head - h, z, y
+        if 0 < h < last_head:
+            return (h + 1 if h % 2 else h - 1), z, y
+        return (h, z, 1 - y) if group == 2 else (last_head - h, z, y)
 
     outer = {}
     idle = []
@@ -231,30 +247,15 @@
         return head, ctx // group, ctx % group
 
     halos = [
-        core_swap(first),
         lax.ppermute(second, mesh_axes, everyone(inside)),
         lax.ppermute(second, mesh_axes, everyone(outside)),
     ]
-    mine = [keep, got] + exchange(keep, got, chips, my_chip, "regroup")
-
-    def keys_body(keep_ref, got_ref, *refs):
-        out_ref = refs[-1]
-        for member, take in arrivals(my_chip(), my_core(), keep_ref, got_ref, refs[:-1]):
-            out_ref[pl.ds(pl.multiple_of(member * rows, rows), rows), :] = take()[0:rows]
-
-    (both,) = call(keys_body, [vmem((supers, LANES))], name="keys")(*on_chip(*mine))
-
-    steps = [(d, phase) for d in range(1, near + 1) for phase in (0, 1)]
-    around = [step(both, d, phase) for d, phase in steps]
-
     span = rows + 2 * HALF
 
-    def conv_body(
-        resid_ref, grad_ref, core_ref, inside_ref, outside_ref, taps_ref, weight_hbm,
-        hg_keep, hg_send, dres_keep, dres_send, low_ref, weight_ref, sem,
-    ):
-        fetch = pltpu.make_async_copy(weight_hbm, weight_ref, sem)
-        fetch.start()
+    part_chunks = channels // LANES // 2
+    part_cols = part_chunks * LANES
+
+    def conv_chunks(start, resid_ref, grad_ref, core_ref, inside_ref, outside_ref, taps_ref, low_ref):
         head, ctx = lax.axis_index("head"), lax.axis_index("z") * group + lax.axis_index("y")
         odd = (head % 2) == 1
         edge = jnp.logical_or(head == 0, head == heads_axis - 1)
@@ -280,7 +281,8 @@
         def chunk(c, carry):
             at = pl.multiple_of(c * LANES, LANES)
             lane = pl.ds(at, LANES)
-            first = core_ref[:, lane].astype(F32)
+            at = pl.multiple_of(chips * slot + c * edge_rows, HALF)
+            first = core_ref[pl.ds(at, edge_rows), :].astype(F32)
             second = jnp.where(edge, outside_ref[:, lane].astype(F32), inside_ref[:, lane].astype(F32))
             before = jnp.where(starts, 0.0, jnp.where(odd, first, second))
             after = jnp.where(ends, 0.0, jnp.where(odd, second, first))
@@ -295,7 +297,17 @@
             low_ref[:, lane] = out.astype(BF16)
             return carry
 
-        lax.fori_loop(0, channels // LANES, chunk, 0)
+        lax.fori_loop(start, start + part_chunks, chunk, 0)
+
+    def conv_first(*refs):
+        conv_chunks(0, *refs)
+
+    def conv_second(*refs):
+        first_ref, weight_hbm, hg_keep, hg_send, dres_keep, dres_send, low_ref, weight_ref, sem = refs[6:]
+        fetch = pltpu.make_async_copy(weight_hbm, weight_ref, sem)
+        fetch.start()
+        low_ref[:, 0:part_cols] = first_ref[...]
+        conv_chunks(part_chunks, *refs[:6], low_ref)
         core = my_core()
         for x in range(heads_axis // 2):
             dres_keep[x], dres_send[x] = sides(
@@ -310,27 +322,36 @@
                 hg_keep[chip, :, at : at + HEAD_DIM] = stay
                 hg_send[chip, :, at : at + HEAD_DIM] = leave
 
+    conv_in = (resid, upstream, got, *halos, taps_in)
+    (conv_low,) = call(conv_first, [vmem((rows, part_cols))], name="conv", cost=CONV_COST)(*on_chip(*conv_in))
+    mine = [keep, got] + exchange(keep, got, chips, my_chip, "regroup")
+
+    def keys_body(keep_ref, got_ref, *refs):
+        out_ref = refs[-1]
+        for member, take in arrivals(my_chip(), my_core(), keep_ref, got_ref, refs[:-1]):
+            out_ref[pl.ds(pl.multiple_of(member * rows, rows), rows), :] = take()[0:rows]
+
+    *mine_here, _ = lax.optimization_barrier((*mine, conv_low))
+    (both,) = call(keys_body, [vmem((supers, LANES))], name="keys")(*on_chip(*mine_here))
+
+    steps = [(d, phase) for d in range(1, near + 1) for phase in (0, 1)]
+    around = [step(both, d, phase) for d, phase in steps]
+
+    conv_low, both_here = lax.optimization_barrier((conv_low, both))
     hg_keep, hg_send, dres_keep, dres_send = call(
-        conv_body,
+        conv_second,
         [vmem((chips, half, LANES))] * 2 + [vmem((heads_axis // 2, rows, out_cols))] * 2,
-        raw=(6,),
+        raw=(7,),
         scratch=[
             pltpu.VMEM((rows, channels), BF16),
             pltpu.VMEM(out_weight.shape, BF16),
             pltpu.SemaphoreType.DMA,
         ],
-        name="conv",
+        name="conv_last",
         cost=CONV_COST,
-    )(*on_chip(resid, upstream, *halos, taps_in), *in_hbm(out_weight))
+    )(*on_chip(*conv_in, conv_low), *in_hbm(out_weight))
     hg_got = core_swap(hg_send)
     grads = [hg_keep, hg_got] + exchange(hg_keep, hg_got, chips, my_chip, "regroup_grads")
-    n_dres = 2 + heads_axis // 2 - 1
-    dres_shape = arr((1, block, out_cols))
-
-    def resid_out(refs, out_ref):
-        for member, take in arrivals(lax.axis_index("head") // 2, my_core(), refs[0], refs[1], refs[2:]):
-            out_ref[0, pl.ds(pl.multiple_of(member * rows, rows), rows), :] = take()
-
     q_tiles = supers // QT
     k_tiles = ext // QT
     first_tile = lead // QT
@@ -541,6 +562,11 @@
         dres_keep, dres_got, heads_axis // 2, lambda: lax.axis_index("head") // 2, "regroup_resid"
     )
 
+    def resid_body(*refs):
+        for member, take in arrivals(lax.axis_index("head") // 2, my_core(), refs[0], refs[1], refs[2:-1]):
+            refs[-1][0, pl.ds(pl.multiple_of(member * rows, rows), rows), :] = take()
+
+    (d_resid,) = call(resid_body, [arr((1, block, out_cols))], name="resid", cost=RESID_COST)(*on_chip(*dres))
 
     if group == 1:
 
@@ -551,19 +577,14 @@
             total = total.astype(BF16)
             refs[-2][0] = total[:, 0:HEAD_DIM]
             refs[-1][0] = total[:, HEAD_DIM:LANES]
-            resid_out(refs[1 + n_back : 1 + n_back + n_dres], refs[-3])
-
-        d_resid, d_key, d_value = call(last_body, [dres_shape] + [arr((1, block, HEAD_DIM))] * 2, name="last")(
-            *on_chip(own, *back, *dres)
-        )
+
+        d_key, d_value = call(last_body, [arr((1, block, HEAD_DIM))] * 2, name="last")(*on_chip(own, *back))
         return d_resid, dq, d_key, d_value
 
     def y_swap(x):
         return lax.ppermute(x, mesh_axes, everyone(lambda h, z, y: (h, z, 1 - y)))
 
-    dq_other = y_swap(results[2])
-
-    def sum_body(own_ref, *refs):
+    def sum_body(own_ref, dq_send_ref, *refs):
         keep_ref, send_ref = refs[-2:]
         total = own_ref[...]
         for i in range(n_back):
@@ -571,33 +592,35 @@
         total = total.astype(BF16)
         first = lax.axis_index("y") == 0
         keep_ref[...] = jnp.where(first, total[0:block], total[block:supers])
-        send_ref[...] = jnp.where(first, total[block:supers], total[0:block])
-
-    keep, send = call(sum_body, [vmem((block, LANES))] * 2, name="sum")(*on_chip(own, *back))
+        send_ref[0:block, :] = jnp.where(first, total[block:supers], total[0:block])
+        send_ref[block:, :] = dq_send_ref[...]
+
+    keep, send = call(sum_body, [vmem((block, LANES)), vmem((block + hb, LANES))], name="sum")(
+        *on_chip(own, results[2], *back)
+    )
     other = y_swap(send)
 
     def last_body(*refs):
-        keep_ref, other_ref, dq_keep_ref, dq_other_ref = refs[:4]
+        keep_ref, other_ref, dq_keep_ref = refs[:3]
         dq_ref, dk_ref, dv_ref = refs[-3:]
-        resid_out(refs[4 : 4 + n_dres], refs[-4])
         first = lax.axis_index("y") == 0
         low = lax.broadcasted_iota(jnp.int32, (block, LANES), 1) < HEAD_DIM
 
-        def ordered(mine_ref, peer_ref):
-            mine, peer = mine_ref[...].astype(F32), peer_ref[...].astype(F32)
+        def ordered(mine, peer):
+            mine, peer = mine.astype(F32), peer.astype(F32)
             return jnp.where(first, mine, peer), jnp.where(first, peer, mine)
 
-        lo, up = ordered(keep_ref, other_ref)
+        lo, up = ordered(keep_ref[...], other_ref[0:block, :])
         dk_ref[0] = jnp.where(low, lo, pltpu.roll(up, HEAD_DIM, 1)).astype(BF16)
         dv_ref[0] = jnp.where(low, pltpu.roll(lo, HEAD_DIM, 1), up).astype(BF16)
-        lo, up = ordered(dq_keep_ref, dq_other_ref)
+        lo, up = ordered(dq_keep_ref[...], other_ref[block:, :])
         low = low[0:hb]
         dq_ref[0, 0:hb, :] = jnp.where(low, lo, pltpu.roll(up, HEAD_DIM, 1)).astype(BF16)
         dq_ref[0, hb:block, :] = jnp.where(low, pltpu.roll(lo, HEAD_DIM, 1), up).astype(BF16)
 
-    d_resid, d_query, d_key, d_value = call(
-        last_body, [dres_shape] + [arr((1, block, LANES))] * 3, name="last"
-    )(*on_chip(keep, other, dq, dq_other, *dres))
+    d_query, d_key, d_value = call(last_body, [arr((1, block, LANES))] * 3, name="last")(
+        *on_chip(keep, other, dq)
+    )
     return d_resid, d_query, d_key, d_value
 
 

time: 51.5 us -> 49.8 us (0.967)
  waiting for transfers between devices: 12.8 us -> 11.4 us
  starting transfers between devices: 19.5 us -> 18.7 us
    ppermute x7, waiting for transfers between devices: 4.31 us -> 7.52 us  [exchange(): lax.ppermute(part, mesh_axes, everyone(target(m)))]
    ppermute x2 -> x1, waiting for transfers between devices: 3.65 us -> 1.11 us  [y_swap(): return lax.ppermute(x, mesh_axes, everyone(lambda h, z, y: (h, z, 1 - y)))]
    ppermute x2 -> x1, starting transfers between devices: 2.09 us -> 0.35 us  [y_swap(): return lax.ppermute(x, mesh_axes, everyone(lambda h, z, y: (h, z, 1 - y)))]
    ppermute x4 -> x3, waiting for transfers between devices: 3.3 us -> 1.89 us  [core_swap(): return lax.ppermute(x, mesh_axes, everyone(lambda h, z, y: (h ^ 1, z, y)))]
    ppermute x7, starting transfers between devices: 9.55 us -> 8.26 us  [exchange(): lax.ppermute(part, mesh_axes, everyone(target(m)))]
    ppermute x4, starting transfers between devices: 4.68 us -> 5.77 us  [step(): return lax.ppermute(x, mesh_axes, everyone(target))]
    ppermute x1, starting transfers between devices: 1.55 us -> 2.59 us  [on_device(): lax.ppermute(second, mesh_axes, everyone(inside))]
    ppermute x4, waiting for transfers between devices: 1.49 us -> 0.83 us  [step(): return lax.ppermute(x, mesh_axes, everyone(target))]
  transfers between devices with their start and end apart: 19 -> 17, of which waited for: 7 -> 8; matrix products, arithmetic and copies ran while one was open for 0% -> 0% of each run, Pallas kernels for 24% -> 26%
where the time goes in v4:
time: 49.8 us; the launch traced here: 49.7 us
  Pallas kernels  18.8 us (38%)
  starting transfers between devices  18.7 us (38%)
  waiting for transfers between devices  11.4 us (23%)
  between operations  0.74 us (1%)
    pallas_call x12, Pallas kernels, run(): pl.pallas_call(body, out_shape=outs, in_specs=[pl.BlockSpec(memory_space=...  17.4 us
    ppermute x7, starting transfers between devices, exchange(): lax.ppermute(part, mesh_axes, everyone(target(m)))  8.26 us
    ppermute x7, waiting for transfers between devices, exchange(): lax.ppermute(part, mesh_axes, everyone(target(m)))  7.52 us
    ppermute x4, starting transfers between devices, step(): return lax.ppermute(x, mesh_axes, everyone(target))  5.77 us
    ppermute x1, starting transfers between devices, on_device(): lax.ppermute(second, mesh_axes, everyone(inside))  2.59 us
    ppermute x3, waiting for transfers between devices, core_swap(): return lax.ppermute(x, mesh_axes, everyone(lambda h, z, y: (h ^ 1, z, y)))  1.89 us
    ppermute x3, starting transfers between devices, core_swap(): return lax.ppermute(x, mesh_axes, everyone(lambda h, z, y: (h ^ 1, z, y)))  1.66 us
    pallas_call x1, Pallas kernels, on_device(): pl.pallas_call(pack_body, out_shape=pack_outs, in_specs=[raw] * 6, out_sp...  1.47 us
  transfers between devices with their start and end apart: 17, of which 8 were waited for; matrix products, arithmetic and copies ran while one was open for 0% of the time, Pallas kernels for 26%

profile of v4, /device:TPU:0, one launch (start us, length us, event | category | flops | bytes accessed | tf_op | source)
XLA Modules:
  0.0 49.7 jit_solution(16175888356168348189)
XLA Ops:
  0.6 1.5 %pack.1 = (bf16[4,192,128]{2,1,0:T(8,128)(2,1)S(1)}, bf16[1152,128]{1,0:T(8,128)(2,1)S(1)}, bf16[48,1024]{1,0:T(8,128)(2,1)S(1)}, bf16[1,128,1024]{2,1,0:T(8,128...) custom-call(bf16[1,128,512]{2,1,0:T(8,128)(2,1)} %q_hbm.1, bf16[1,128,512]{2,1,0:T(8,128)(2,1)} %k_hbm.1, ...), custom_call_target="tpu_custom_call" | custom-call | tf_op jit(solution)/shard_map/pack/pallas_call | solution.py:161
  2.1 0.5 %collective-permute-start = (bf16[1152,128]{1,0:T(8,128)(2,1)S(1)}, bf16[1152,128]{1,0:T(8,128)(2,1)S(1)}, u32[]{:S(2)}, u32[]{:S(2)}) collective-permute-start(bf16[1152,128]{1,0:T(8,128)(2,1)S(1)} %get-tuple-element.49), channel_id=1, source_target_pairs={{0,8},{1,9},{2,10},{3,11},{4,12},{5,13},{6,14},{7,15},{8,0},{9,1},... | collective-permute-start | bytes 884744 | tf_op jit(solution)/shard_map/ppermute | solution.py:185
  2.6 2.6 %collective-permute-start.1 = (bf16[48,1024]{1,0:T(8,128)(2,1)S(1)}, bf16[48,1024]{1,0:T(8,128)(2,1)S(1)}, u32[]{:S(2)}, u32[]{:S(2)}) collective-permute-start(bf16[48,1024]{1,0:T(8,128)(2,1)S(1)} %get-tuple-element.50), channel_id=1, source_target_pairs={{0,1},{1,0},{2,3},{3,2},{4,5},{5,4},{6,7},{7,6},{8,16},{9,17},{10,... | collective-permute-start | bytes 294920 | tf_op jit(solution)/shard_map/ppermute | solution.py:250
  5.2 0.1 collective-permute-start.2
  5.3 0.0 collective-permute-done.refs_2_.got_ref.refs_3_
  5.3 2.7 %collective-permute-start.3 = (bf16[2,192,128]{2,1,0:T(8,128)(2,1)S(1)}, bf16[2,192,128]{2,1,0:T(8,128)(2,1)S(1)}, u32[]{:S(2)}, u32[]{:S(2)}) collective-permute-start(bf16[2,192,128]{2,1,0:T(8,128)(2,1)S(1)} %get-tuple-element.53), channel_id=1, source_target_pairs={{0,16},{1,17},{2,18},{3,19},{4,20},{5,21},{6,22},{7,23},{8,24},{9,... | collective-permute-start | bytes 294920 | tf_op jit(solution)/shard_map/ppermute | solution.py:215
  8.0 1.5 %collective-permute-start.4 = (bf16[2,192,128]{2,1,0:T(8,128)(2,1)S(1)}, bf16[2,192,128]{2,1,0:T(8,128)(2,1)S(1)}, u32[]{:S(2)}, u32[]{:S(2)}) collective-permute-start(bf16[2,192,128]{2,1,0:T(8,128)(2,1)S(1)} %get-tuple-element.54), channel_id=1, source_target_pairs={{0,1},{1,0},{2,3},{3,2},{4,5},{5,4},{6,7},{7,6},{8,9},{9,8},{10,11... | collective-permute-start | bytes 294920 | tf_op jit(solution)/shard_map/ppermute | solution.py:215
  9.5 0.0 collective-permute-start.5
  9.5 0.0 collective-permute-done.1.refs_3_
  9.5 0.0 collective-permute-done.2.refs_4_
  9.5 1.9 %conv.1.refs_6_ = bf16[128,512]{1,0:T(8,128)(2,1)S(1)} custom-call(bf16[1,128,1024]{2,1,0:T(8,128)(2,1)S(1)} %get-tuple-element.47.refs_0_, bf16[1,128,1024]{2,1,0:T(8,128)(2,1)S(1)} %get-tuple-element.48.refs_1_, bf16[1152,128]{1,0:T(8,128)(2,1)S(1)} %collective-permute-done.refs_2_.got_ref.refs_3_, bf16[48,1024]{1,0:T(8,128)(2,1)S(1)} %collective-permute-done.1.refs_3_, ...), custom_call_target="tpu_custom_call" | custom-call | flops 3000000000 | tf_op jit(solution)/shard_map/conv/pallas_call | solution.py:39
  11.4 0.8 %collective-permute-done.3.refs_0_.refs_4_ = bf16[2,192,128]{2,1,0:T(8,128)(2,1)S(1)} collective-permute-done((bf16[2,192,128]{2,1,0:T(8,128)(2,1)S(1)}, bf16[2,192,128]{2,1,0:T(8,128)(2,1)S(1)}, u32[]{:S(2)}, u32[]{:S(2)}) %collective-permute-start.3) | collective-permute-done | bytes 98336 | tf_op jit(solution)/shard_map/ppermute | solution.py:215
  12.3 1.9 %collective-permute-done.4.refs_1_.refs_5_ = bf16[2,192,128]{2,1,0:T(8,128)(2,1)S(1)} collective-permute-done((bf16[2,192,128]{2,1,0:T(8,128)(2,1)S(1)}, bf16[2,192,128]{2,1,0:T(8,128)(2,1)S(1)}, u32[]{:S(2)}, u32[]{:S(2)}) %collective-permute-start.4) | collective-permute-done | bytes 98336 | tf_op jit(solution)/shard_map/ppermute | solution.py:215
  14.1 0.9 %collective-permute-done.5.refs_2_.refs_6_ = bf16[2,192,128]{2,1,0:T(8,128)(2,1)S(1)} collective-permute-done((bf16[2,192,128]{2,1,0:T(8,128)(2,1)S(1)}, bf16[2,192,128]{2,1,0:T(8,128)(2,1)S(1)}, u32[]{:S(2)}, u32[]{:S(2)}) %collective-permute-start.5) | collective-permute-done | bytes 98336 | tf_op jit(solution)/shard_map/ppermute | solution.py:215
  15.1 0.0 copy-start
  15.1 3.0 %collective-permute-start.6 = (bf16[1024,128]{1,0:T(8,128)(2,1)S(1)}, bf16[1024,128]{1,0:T(8,128)(2,1)S(1)}, u32[]{:S(2)}, u32[]{:S(2)}) collective-permute-start(bf16[1024,128]{1,0:T(8,128)(2,1)S(1)} %keys.1.refs_1_), channel_id=1, source_target_pairs={{0,2},{1,3},{2,0},{3,1},{4,6},{5,7},{6,4},{7,5},{8,10},{9,11},{10,... | collective-permute-start | bytes 786440 | tf_op jit(solution)/shard_map/ppermute | solution.py:192
  18.1 0.0 collective-permute-start.7
  18.1 2.5 %conv_last.1 = (bf16[4,64,128]{2,1,0:T(8,128)(2,1)S(1)}, bf16[4,64,128]{2,1,0:T(8,128)(2,1)S(1)}, bf16[2,128,256]{2,1,0:T(8,128)(2,1)S(1)}, bf16[2,128,256]{2,1,0:T(8,128)(2,1)S(1)}) custom-call(bf16[1,128,1024]{2,1,0:T(8,128)(2,1)S(1)} %get-tuple-element.47.refs_0_, bf16[1,128,1024]{2,1,0:T(8,128)(2,1)S(1)} %get-tuple-element.48.refs_1_, ...), custom_call_target="tpu_custom_call" | custom-call | flops 3000000000 | tf_op jit(solution)/shard_map/conv_last/pallas_call | solution.py:39
  20.6 0.6 %collective-permute-start.8 = (bf16[4,64,128]{2,1,0:T(8,128)(2,1)S(1)}, bf16[4,64,128]{2,1,0:T(8,128)(2,1)S(1)}, u32[]{:S(2)}, u32[]{:S(2)}) collective-permute-start(bf16[4,64,128]{2,1,0:T(8,128)(2,1)S(1)} %get-tuple-element.67), channel_id=1, source_target_pairs={{0,8},{1,9},{2,10},{3,11},{4,12},{5,13},{6,14},{7,15},{8,0},{9,1},... | collective-permute-start | bytes 196616 | tf_op jit(solution)/shard_map/ppermute | solution.py:185
  21.2 0.9 %collective-permute-done.8.got_ref.refs_1_ = bf16[4,64,128]{2,1,0:T(8,128)(2,1)S(1)} collective-permute-done((bf16[4,64,128]{2,1,0:T(8,128)(2,1)S(1)}, bf16[4,64,128]{2,1,0:T(8,128)(2,1)S(1)}, u32[]{:S(2)}, u32[]{:S(2)}) %collective-permute-start.8) | collective-permute-done | bytes 65568 | tf_op jit(solution)/shard_map/ppermute | solution.py:185
  22.1 0.2 collective-permute-start.9
  22.3 2.0 %collective-permute-start.10 = (bf16[2,64,128]{2,1,0:T(8,128)(2,1)S(1)}, bf16[2,64,128]{2,1,0:T(8,128)(2,1)S(1)}, u32[]{:S(2)}, u32[]{:S(2)}) collective-permute-start(bf16[2,64,128]{2,1,0:T(8,128)(2,1)S(1)} %get-tuple-element.69), channel_id=1, source_target_pairs={{0,1},{1,0},{2,3},{3,2},{4,5},{5,4},{6,7},{7,6},{8,9},{9,8},{10,11... | collective-permute-start | bytes 98312 | tf_op jit(solution)/shard_map/ppermute | solution.py:215
  24.2 1.3 %collective-permute-start.11 = (bf16[2,64,128]{2,1,0:T(8,128)(2,1)S(1)}, bf16[2,64,128]{2,1,0:T(8,128)(2,1)S(1)}, u32[]{:S(2)}, u32[]{:S(2)}) collective-permute-start(bf16[2,64,128]{2,1,0:T(8,128)(2,1)S(1)} %get-tuple-element.70), channel_id=1, source_target_pairs={{0,17},{1,16},{2,19},{3,18},{4,21},{5,20},{6,23},{7,22},{8,25},{9,... | collective-permute-start | bytes 98312 | tf_op jit(solution)/shard_map/ppermute | solution.py:215
  25.6 0.0 collective-permute-done.6.refs_7_
  25.6 0.0 collective-permute-done.7.refs_8_
  25.6 0.0 copy-done
  25.6 4.8 %scores.1 = (bf16[4,2304,256]{2,1,0:T(8,128)(2,1)S(1)}, f32[4,1,256]{2,1,0:T(1,128)S(1)}, f32[4,64,256]{2,1,0:T(8,128)S(1)}, bf16[3072,128]{1,0:T(8,128)(2,1)S(1...) custom-call(s32[8]{0:T(128)S(1)} %copy-done, bf16[1024,128]{1,0:T(8,128)(2,1)S(1)} %keys.1.refs_1_, ...), custom_call_target="tpu_custom_call" | custom-call | flops 8999999488 | tf_op jit(solution)/shard_map/scores/pallas_call | solution.py:39
  30.4 0.0 collective-permute-done.9.refs_2_
  30.4 0.0 collective-permute-done.10.refs_3_
  30.4 0.0 collective-permute-done.11.refs_4_
  30.5 3.5 %far.1 = (bf16[1024,128]{1,0:T(8,128)(2,1)S(1)}, f32[4,1,256]{2,1,0:T(1,128)S(1)}, f32[4,64,256]{2,1,0:T(8,128)S(1)}, bf16[1024,128]{1,0:T(8,128)(2,1)S(1)}, bf16[1024,128]{1,0:T(8,128)(2,1)S(1)}) custom-call(bf16[4,64,128]{2,1,0:T(8,128)(2,1)S(1)} %get-tuple-element.66.keep_ref.refs_0_, bf16[4,64,128]{2,1,0:T(8,128)(2,1)S(1)} %collective-permute-done.8.got_ref.refs_1_, ...), custom_call_target="tpu_custom_call" | custom-call | flops 4000000000 | tf_op jit(solution)/shard_map/far/pallas_call | solution.py:39
  33.9 2.8 %collective-permute-start.14 = (bf16[1024,128]{1,0:T(8,128)(2,1)S(1)}, bf16[1024,128]{1,0:T(8,128)(2,1)S(1)}, u32[]{:S(2)}, u32[]{:S(2)}) collective-permute-start(bf16[1024,128]{1,0:T(8,128)(2,1)S(1)} %get-tuple-element.82), channel_id=1, source_target_pairs={{0,2},{1,3},{2,0},{3,1},{4,6},{5,7},{6,4},{7,5},{8,10},{9,11},{10,... | collective-permute-start | bytes 786440 | tf_op jit(solution)/shard_map/ppermute | solution.py:192
  36.7 0.0 collective-permute-start.15
  36.7 2.8 %near.1 = (f32[1024,128]{1,0:T(8,128)S(1)}, bf16[256,128]{1,0:T(8,128)(2,1)S(1)}, bf16[256,128]{1,0:T(8,128)(2,1)S(1)}) custom-call(bf16[4,2304,256]{2,1,0:T(8,128)(2,1)S(1)} %get-tuple-element.64.refs_5_.refs_0_, f32[4,1,256]{2,1,0:T(1,128)S(1)} %get-tuple-element.65.refs_6_.refs_1_, f32[4,1,256]{2,1,0:T(1,128)S(1)} %get-tuple-element.75.refs_2_, ...), custom_call_target="tpu_custom_call" | custom-call | flops 4000000000 | tf_op jit(solution)/shard_map/near/pallas_call | solution.py:39
  39.5 0.6 %collective-permute-start.12 = (bf16[2,128,256]{2,1,0:T(8,128)(2,1)S(1)}, bf16[2,128,256]{2,1,0:T(8,128)(2,1)S(1)}, u32[]{:S(2)}, u32[]{:S(2)}) collective-permute-start(bf16[2,128,256]{2,1,0:T(8,128)(2,1)S(1)} %get-tuple-element.80), channel_id=1, source_target_pairs={{0,8},{1,9},{2,10},{3,11},{4,12},{5,13},{6,14},{7,15},{8,0},{9,1},... | collective-permute-start | bytes 393224 | tf_op jit(solution)/shard_map/ppermute | solution.py:185
  40.1 1.0 %collective-permute-done.12.got_ref.refs_1_ = bf16[2,128,256]{2,1,0:T(8,128)(2,1)S(1)} collective-permute-done((bf16[2,128,256]{2,1,0:T(8,128)(2,1)S(1)}, bf16[2,128,256]{2,1,0:T(8,128)(2,1)S(1)}, u32[]{:S(2)}, u32[]{:S(2)}) %collective-permute-start.12) | collective-permute-done | bytes 131104 | tf_op jit(solution)/shard_map/ppermute | solution.py:185
  41.1 0.6 %collective-permute-start.13 = (bf16[2,128,256]{2,1,0:T(8,128)(2,1)S(1)}, bf16[2,128,256]{2,1,0:T(8,128)(2,1)S(1)}, u32[]{:S(2)}, u32[]{:S(2)}) collective-permute-start(bf16[2,128,256]{2,1,0:T(8,128)(2,1)S(1)} %regroup_resid.1), channel_id=1, source_target_pairs={{0,16},{1,17},{2,18},{3,19},{4,20},{5,21},{6,22},{7,23},{8,24},{9,... | collective-permute-start | bytes 393224 | tf_op jit(solution)/shard_map/ppermute | solution.py:215
  41.7 0.8 %collective-permute-done.14.refs_0_ = bf16[1024,128]{1,0:T(8,128)(2,1)S(1)} collective-permute-done((bf16[1024,128]{1,0:T(8,128)(2,1)S(1)}, bf16[1024,128]{1,0:T(8,128)(2,1)S(1)}, u32[]{:S(2)}, u32[]{:S(2)}) %collective-permute-start.14) | collective-permute-done | bytes 262176 | tf_op jit(solution)/shard_map/ppermute | solution.py:192
  42.5 0.0 collective-permute-done.15.refs_1_
  42.5 0.2 sum.1
  42.6 0.4 collective-permute-start.16
  43.0 3.9 %collective-permute-done.13.refs_2_ = bf16[2,128,256]{2,1,0:T(8,128)(2,1)S(1)} collective-permute-done((bf16[2,128,256]{2,1,0:T(8,128)(2,1)S(1)}, bf16[2,128,256]{2,1,0:T(8,128)(2,1)S(1)}, u32[]{:S(2)}, u32[]{:S(2)}) %collective-permute-start.13) | collective-permute-done | bytes 131104 | tf_op jit(solution)/shard_map/ppermute | solution.py:215
  46.9 0.7 %resid.1 = bf16[1,512,256]{2,1,0:T(8,128)(2,1)} custom-call(bf16[2,128,256]{2,1,0:T(8,128)(2,1)S(1)} %get-tuple-element.79.keep_ref.refs_0_, bf16[2,128,256]{2,1,0:T(8,128)(2,1)S(1)} %collective-permute-done.12.got_ref.refs_1_, bf16[2,128,256]{2,1,0:T(8,128)(2,1)S(1)} %collective-permute-done.13.refs_2_), custom_call_target="tpu_custom_call" | custom-call | flops 1000000000 | tf_op jit(solution)/shard_map/resid/pallas_call | solution.py:39
  47.7 1.1 %collective-permute-done.16.refs_1_ = bf16[768,128]{1,0:T(8,128)(2,1)S(1)} collective-permute-done((bf16[768,128]{1,0:T(8,128)(2,1)S(1)}, bf16[768,128]{1,0:T(8,128)(2,1)S(1)}, u32[]{:S(2)}, u32[]{:S(2)}) %collective-permute-start.16) | collective-permute-done | bytes 196640 | tf_op jit(solution)/shard_map/ppermute | solution.py:585
  48.8 0.9 %last.1 = (bf16[1,512,128]{2,1,0:T(8,128)(2,1)}, bf16[1,512,128]{2,1,0:T(8,128)(2,1)}, bf16[1,512,128]{2,1,0:T(8,128)(2,1)}) custom-call(bf16[512,128]{1,0:T(8,128)(2,1)S(1)} %get-tuple-element.84.refs_0_, bf16[768,128]{1,0:T(8,128)(2,1)S(1)} %collective-permute-done.16.refs_1_, bf16[256,128]{1,0:T(8,128)(2,1)S(1)} %get-tuple-element.86.refs_2_), custom_call_target="tpu_custom_call" | custom-call | tf_op jit(solution)/shard_map/last/pallas_call | solution.py:39
  (4 shorter events, 0.1 us)
Async XLA Ops:
  2.1 3.2 %collective-permute-start = (bf16[1152,128]{1,0:T(8,128)(2,1)S(1)}, bf16[1152,128]{1,0:T(8,128)(2,1)S(1)}, u32[]{:S(2)}, u32[]{:S(2)}) collective-permute-start(bf16[1152,128]{1,0:T(8,128)(2,1)S(1)} %get-tuple-element.49), channel_id=1, source_target_pairs={{0,8},{1,9},{2,10},{3,11},{4,12},{5,13},{6,14},{7,15},{8,0},{9,1},... | collective-permute-start | bytes 884744 | tf_op jit(solution)/shard_map/ppermute | solution.py:185
  2.6 6.9 %collective-permute-start.1 = (bf16[48,1024]{1,0:T(8,128)(2,1)S(1)}, bf16[48,1024]{1,0:T(8,128)(2,1)S(1)}, u32[]{:S(2)}, u32[]{:S(2)}) collective-permute-start(bf16[48,1024]{1,0:T(8,128)(2,1)S(1)} %get-tuple-element.50), channel_id=1, source_target_pairs={{0,1},{1,0},{2,3},{3,2},{4,5},{5,4},{6,7},{7,6},{8,16},{9,17},{10,... | collective-permute-start | bytes 294920 | tf_op jit(solution)/shard_map/ppermute | solution.py:250
  5.2 4.3 %collective-permute-start.2 = (bf16[48,1024]{1,0:T(8,128)(2,1)S(1)}, bf16[48,1024]{1,0:T(8,128)(2,1)S(1)}, u32[]{:S(2)}, u32[]{:S(2)}) collective-permute-start(bf16[48,1024]{1,0:T(8,128)(2,1)S(1)} %get-tuple-element.50), channel_id=1, source_target_pairs={{0,8},{1,24},{2,25},{3,26},{4,27},{5,28},{6,29},{7,30},{8,0},{9,16... | collective-permute-start | bytes 294920 | tf_op jit(solution)/shard_map/ppermute | solution.py:251
  5.3 6.9 %collective-permute-start.3 = (bf16[2,192,128]{2,1,0:T(8,128)(2,1)S(1)}, bf16[2,192,128]{2,1,0:T(8,128)(2,1)S(1)}, u32[]{:S(2)}, u32[]{:S(2)}) collective-permute-start(bf16[2,192,128]{2,1,0:T(8,128)(2,1)S(1)} %get-tuple-element.53), channel_id=1, source_target_pairs={{0,16},{1,17},{2,18},{3,19},{4,20},{5,21},{6,22},{7,23},{8,24},{9,... | collective-permute-start | bytes 294920 | tf_op jit(solution)/shard_map/ppermute | solution.py:215
  8.0 6.2 %collective-permute-start.4 = (bf16[2,192,128]{2,1,0:T(8,128)(2,1)S(1)}, bf16[2,192,128]{2,1,0:T(8,128)(2,1)S(1)}, u32[]{:S(2)}, u32[]{:S(2)}) collective-permute-start(bf16[2,192,128]{2,1,0:T(8,128)(2,1)S(1)} %get-tuple-element.54), channel_id=1, source_target_pairs={{0,1},{1,0},{2,3},{3,2},{4,5},{5,4},{6,7},{7,6},{8,9},{9,8},{10,11... | collective-permute-start | bytes 294920 | tf_op jit(solution)/shard_map/ppermute | solution.py:215
  9.5 5.5 %collective-permute-start.5 = (bf16[2,192,128]{2,1,0:T(8,128)(2,1)S(1)}, bf16[2,192,128]{2,1,0:T(8,128)(2,1)S(1)}, u32[]{:S(2)}, u32[]{:S(2)}) collective-permute-start(bf16[2,192,128]{2,1,0:T(8,128)(2,1)S(1)} %get-tuple-element.55), channel_id=1, source_target_pairs={{0,17},{1,16},{2,19},{3,18},{4,21},{5,20},{6,23},{7,22},{8,25},{9,... | collective-permute-start | bytes 294920 | tf_op jit(solution)/shard_map/ppermute | solution.py:215
  15.1 10.5 %copy-start = (s32[8]{0:T(128)S(1)}, s32[8]{0:T(128)}, u32[]{:S(2)}) copy-start(s32[8]{0:T(128)} %refs_0_.1) | copy-start | bytes 100
  15.1 10.5 %collective-permute-start.6 = (bf16[1024,128]{1,0:T(8,128)(2,1)S(1)}, bf16[1024,128]{1,0:T(8,128)(2,1)S(1)}, u32[]{:S(2)}, u32[]{:S(2)}) collective-permute-start(bf16[1024,128]{1,0:T(8,128)(2,1)S(1)} %keys.1.refs_1_), channel_id=1, source_target_pairs={{0,2},{1,3},{2,0},{3,1},{4,6},{5,7},{6,4},{7,5},{8,10},{9,11},{10,... | collective-permute-start | bytes 786440 | tf_op jit(solution)/shard_map/ppermute | solution.py:192
  18.1 7.5 %collective-permute-start.7 = (bf16[1024,128]{1,0:T(8,128)(2,1)S(1)}, bf16[1024,128]{1,0:T(8,128)(2,1)S(1)}, u32[]{:S(2)}, u32[]{:S(2)}) collective-permute-start(bf16[1024,128]{1,0:T(8,128)(2,1)S(1)} %keys.1.refs_1_), channel_id=1, source_target_pairs={{0,8},{1,9},{2,4},{3,5},{4,2},{5,3},{6,14},{7,15},{8,0},{9,1},{10,... | collective-permute-start | bytes 786440 | tf_op jit(solution)/shard_map/ppermute | solution.py:192
  20.6 1.5 %collective-permute-start.8 = (bf16[4,64,128]{2,1,0:T(8,128)(2,1)S(1)}, bf16[4,64,128]{2,1,0:T(8,128)(2,1)S(1)}, u32[]{:S(2)}, u32[]{:S(2)}) collective-permute-start(bf16[4,64,128]{2,1,0:T(8,128)(2,1)S(1)} %get-tuple-element.67), channel_id=1, source_target_pairs={{0,8},{1,9},{2,10},{3,11},{4,12},{5,13},{6,14},{7,15},{8,0},{9,1},... | collective-permute-start | bytes 196616 | tf_op jit(solution)/shard_map/ppermute | solution.py:185
  22.1 8.3 %collective-permute-start.9 = (bf16[2,64,128]{2,1,0:T(8,128)(2,1)S(1)}, bf16[2,64,128]{2,1,0:T(8,128)(2,1)S(1)}, u32[]{:S(2)}, u32[]{:S(2)}) collective-permute-start(bf16[2,64,128]{2,1,0:T(8,128)(2,1)S(1)} %get-tuple-element.68), channel_id=1, source_target_pairs={{0,16},{1,17},{2,18},{3,19},{4,20},{5,21},{6,22},{7,23},{8,24},{9,... | collective-permute-start | bytes 98312 | tf_op jit(solution)/shard_map/ppermute | solution.py:215
  22.3 8.2 %collective-permute-start.10 = (bf16[2,64,128]{2,1,0:T(8,128)(2,1)S(1)}, bf16[2,64,128]{2,1,0:T(8,128)(2,1)S(1)}, u32[]{:S(2)}, u32[]{:S(2)}) collective-permute-start(bf16[2,64,128]{2,1,0:T(8,128)(2,1)S(1)} %get-tuple-element.69), channel_id=1, source_target_pairs={{0,1},{1,0},{2,3},{3,2},{4,5},{5,4},{6,7},{7,6},{8,9},{9,8},{10,11... | collective-permute-start | bytes 98312 | tf_op jit(solution)/shard_map/ppermute | solution.py:215
  24.2 6.2 %collective-permute-start.11 = (bf16[2,64,128]{2,1,0:T(8,128)(2,1)S(1)}, bf16[2,64,128]{2,1,0:T(8,128)(2,1)S(1)}, u32[]{:S(2)}, u32[]{:S(2)}) collective-permute-start(bf16[2,64,128]{2,1,0:T(8,128)(2,1)S(1)} %get-tuple-element.70), channel_id=1, source_target_pairs={{0,17},{1,16},{2,19},{3,18},{4,21},{5,20},{6,23},{7,22},{8,25},{9,... | collective-permute-start | bytes 98312 | tf_op jit(solution)/shard_map/ppermute | solution.py:215
  33.9 8.5 %collective-permute-start.14 = (bf16[1024,128]{1,0:T(8,128)(2,1)S(1)}, bf16[1024,128]{1,0:T(8,128)(2,1)S(1)}, u32[]{:S(2)}, u32[]{:S(2)}) collective-permute-start(bf16[1024,128]{1,0:T(8,128)(2,1)S(1)} %get-tuple-element.82), channel_id=1, source_target_pairs={{0,2},{1,3},{2,0},{3,1},{4,6},{5,7},{6,4},{7,5},{8,10},{9,11},{10,... | collective-permute-start | bytes 786440 | tf_op jit(solution)/shard_map/ppermute | solution.py:192
  36.7 5.7 %collective-permute-start.15 = (bf16[1024,128]{1,0:T(8,128)(2,1)S(1)}, bf16[1024,128]{1,0:T(8,128)(2,1)S(1)}, u32[]{:S(2)}, u32[]{:S(2)}) collective-permute-start(bf16[1024,128]{1,0:T(8,128)(2,1)S(1)} %get-tuple-element.83), channel_id=1, source_target_pairs={{0,8},{1,9},{2,4},{3,5},{4,2},{5,3},{6,14},{7,15},{8,0},{9,1},{10,... | collective-permute-start | bytes 786440 | tf_op jit(solution)/shard_map/ppermute | solution.py:192
  39.5 1.6 %collective-permute-start.12 = (bf16[2,128,256]{2,1,0:T(8,128)(2,1)S(1)}, bf16[2,128,256]{2,1,0:T(8,128)(2,1)S(1)}, u32[]{:S(2)}, u32[]{:S(2)}) collective-permute-start(bf16[2,128,256]{2,1,0:T(8,128)(2,1)S(1)} %get-tuple-element.80), channel_id=1, source_target_pairs={{0,8},{1,9},{2,10},{3,11},{4,12},{5,13},{6,14},{7,15},{8,0},{9,1},... | collective-permute-start | bytes 393224 | tf_op jit(solution)/shard_map/ppermute | solution.py:185
  41.1 5.8 %collective-permute-start.13 = (bf16[2,128,256]{2,1,0:T(8,128)(2,1)S(1)}, bf16[2,128,256]{2,1,0:T(8,128)(2,1)S(1)}, u32[]{:S(2)}, u32[]{:S(2)}) collective-permute-start(bf16[2,128,256]{2,1,0:T(8,128)(2,1)S(1)} %regroup_resid.1), channel_id=1, source_target_pairs={{0,16},{1,17},{2,18},{3,19},{4,20},{5,21},{6,22},{7,23},{8,24},{9,... | collective-permute-start | bytes 393224 | tf_op jit(solution)/shard_map/ppermute | solution.py:215
  42.6 6.1 %collective-permute-start.16 = (bf16[768,128]{1,0:T(8,128)(2,1)S(1)}, bf16[768,128]{1,0:T(8,128)(2,1)S(1)}, u32[]{:S(2)}, u32[]{:S(2)}) collective-permute-start(bf16[768,128]{1,0:T(8,128)(2,1)S(1)} %get-tuple-element.85), channel_id=1, source_target_pairs={{0,1},{1,0},{2,3},{3,2},{4,5},{5,4},{6,7},{7,6},{8,9},{9,8},{10,11... | collective-permute-start | bytes 589832 | tf_op jit(solution)/shard_map/ppermute | solution.py:585

commit v5 on v4

--- a/solution.py
+++ b/solution.py
@@ -252,10 +252,10 @@
     ]
     span = rows + 2 * HALF
 
-    part_chunks = channels // LANES // 2
+    part_chunks = channels // LANES * 6 // 8
     part_cols = part_chunks * LANES
 
-    def conv_chunks(start, resid_ref, grad_ref, core_ref, inside_ref, outside_ref, taps_ref, low_ref):
+    def conv_chunks(start, stop, resid_ref, grad_ref, core_ref, inside_ref, outside_ref, taps_ref, low_ref):
         head, ctx = lax.axis_index("head"), lax.axis_index("z") * group + lax.axis_index("y")
         odd = (head % 2) == 1
         edge = jnp.logical_or(head == 0, head == heads_axis - 1)
@@ -297,17 +297,17 @@
             low_ref[:, lane] = out.astype(BF16)
             return carry
 
-        lax.fori_loop(start, start + part_chunks, chunk, 0)
+        lax.fori_loop(start, stop, chunk, 0)
 
     def conv_first(*refs):
-        conv_chunks(0, *refs)
+        conv_chunks(0, part_chunks, *refs)
 
     def conv_second(*refs):
         first_ref, weight_hbm, hg_keep, hg_send, dres_keep, dres_send, low_ref, weight_ref, sem = refs[6:]
         fetch = pltpu.make_async_copy(weight_hbm, weight_ref, sem)
         fetch.start()
         low_ref[:, 0:part_cols] = first_ref[...]
-        conv_chunks(part_chunks, *refs[:6], low_ref)
+        conv_chunks(part_chunks, channels // LANES, *refs[:6], low_ref)
         core = my_core()
         for x in range(heads_axis // 2):
             dres_keep[x], dres_send[x] = sides(
@@ -459,17 +459,17 @@
         cost=SCORES_COST,
     )(frame_lengths, *on_chip(both, *mine, *around))
 
-    def key_tiles(a, ts, e_ref, inv_ref, delta_ref, kv, kt, qz, hz, acc, ds_sc, base):
+    def key_tiles(a, ts, e_ref, inv_ref, delta_ref, kv, kt, qz, hz, acc, ds_sc, slopes_sc, base):
         q, g = qz[at_tile(a), :], hz[at_tile(a), :]
+        keys = slice(ts[0] * QT, (ts[-1] + 1) * QT)
+        slopes_sc[0 : len(ts) * QT, :] = dot(kv[keys, :], g, NT_DIMS)
         for i, t in enumerate(ts):
             p = e_ref[a, at_tile(t - a - first_tile), :].astype(F32) * inv_ref[a]
-            slopes = dot(kv[at_tile(t), :], g, NT_DIMS)
-            ds = (p * (slopes - delta_ref[a])).astype(BF16)
+            ds = (p * (slopes_sc[at_tile(i), :] - delta_ref[a])).astype(BF16)
             ds_sc[at_tile(i), :] = ds
             part = dot(ds, q, NN_DIMS) + dot(p.astype(BF16), g, NN_DIMS)
             fresh = not any(t in seen(b) for b in range(a))
             acc[at_tile(t - base), :] = part if fresh else acc[at_tile(t - base), :] + part
-        keys = slice(ts[0] * QT, (ts[-1] + 1) * QT)
         return dot(kt[:, keys], ds_sc[0 : len(ts) * QT, :], NN_DIMS)
 
     n_back = 2 * near
@@ -484,8 +484,8 @@
     def far_body(*refs):
         grad_refs = refs[: 1 + chips]
         e_ref, inv_ref, out_ref, kv, kt, qz, hz, delta_ref, dq = refs[1 + chips : 10 + chips]
-        back_refs = refs[10 + chips : -2]
-        acc, ds_sc = refs[-2:]
+        back_refs = refs[10 + chips : -3]
+        acc, ds_sc, slopes_sc = refs[-3:]
         z = lax.axis_index("z")
         low = lax.broadcasted_iota(jnp.int32, (half, LANES), 1) < HEAD_DIM
         for member, take in arrivals(my_chip(), my_core(), grad_refs[0], grad_refs[1], grad_refs[2:]):
@@ -503,7 +503,7 @@
             left = [t for t in seen(a) if t < own_tiles[0]]
             right = [t for t in seen(a) if t > own_tiles[-1]]
             dq[a] = sum(
-                key_tiles(a, ts, e_ref, inv_ref, delta_ref, kv, kt, qz, hz, acc, ds_sc.at[side], 0)
+                key_tiles(a, ts, e_ref, inv_ref, delta_ref, kv, kt, qz, hz, acc, ds_sc.at[side], slopes_sc.at[side], 0)
                 for side, ts in enumerate((left, right))
             )
         for i, (d, phase) in enumerate(steps):
@@ -516,7 +516,11 @@
         far_body,
         [vmem((supers, LANES)), vmem((q_tiles, 1, QT), F32), vmem((q_tiles, HEAD_DIM, QT), F32)]
         + [vmem((supers, LANES))] * n_back,
-        scratch=[pltpu.VMEM((ext, LANES), F32), pltpu.VMEM((2, tiles * QT, QT), BF16)],
+        scratch=[
+            pltpu.VMEM((ext, LANES), F32),
+            pltpu.VMEM((2, near * supers, QT), BF16),
+            pltpu.VMEM((2, near * supers, QT), F32),
+        ],
         name="far",
         cost=FAR_COST,
     )(*on_chip(*grads, exps, inverse, outs, kv, kt, qz))
@@ -528,10 +532,11 @@
     def near_body(*refs):
         e_ref, inv_ref, delta_ref, kv, kt, qz, hz, far_ref = refs[:8]
         acc, dq_ref = refs[8:10]
-        dq_sc, ds_sc = refs[-2:]
+        dq_sc, ds_sc, slopes_sc = refs[-3:]
         for a in range(q_tiles):
             dq = far_ref[a] + key_tiles(
-                a, own_tiles, e_ref, inv_ref, delta_ref, kv, kt, qz, hz, acc, ds_sc.at[a % 2], own_tiles[0]
+                a, own_tiles, e_ref, inv_ref, delta_ref, kv, kt, qz, hz, acc, ds_sc.at[a % 2], slopes_sc.at[a % 2],
+                own_tiles[0],
             )
             dq_sc[at_tile(a), 0:HEAD_DIM] = jnp.transpose(dq * scale)
         if group == 1:
@@ -551,13 +556,14 @@
         scratch=[
             pltpu.VMEM((supers, LANES), F32),
             pltpu.VMEM((2, supers, QT), BF16),
+            pltpu.VMEM((2, supers, QT), F32),
         ],
         name="near",
         cost=NEAR_COST,
     )(*on_chip(exps, inverse, delta, kv, kt, qz, hz, dq_far))
     own, dq = results[:2]
-    dres_keep, dres_send, _ = lax.optimization_barrier((dres_keep, dres_send, results[0]))
     dres_got = core_swap(dres_send)
+    dres_keep, dres_got, _ = lax.optimization_barrier((dres_keep, dres_got, results[0]))
     dres = [dres_keep, dres_got] + exchange(
         dres_keep, dres_got, heads_axis // 2, lambda: lax.axis_index("head") // 2, "regroup_resid"
     )

time: 49.8 us -> 48.4 us (0.972)
  starting transfers between devices: 18.7 us -> 17.2 us
  waiting for transfers between devices: 11.4 us -> 11.9 us
    ppermute x4, waiting for transfers between devices: 0.83 us -> 3.76 us  [step(): return lax.ppermute(x, mesh_axes, everyone(target))]
    ppermute x7, waiting for transfers between devices: 7.52 us -> 5.07 us  [exchange(): lax.ppermute(part, mesh_axes, everyone(target(m)))]
    ppermute x1, waiting for transfers between devices: 1.11 us -> 2.22 us  [y_swap(): return lax.ppermute(x, mesh_axes, everyone(lambda h, z, y: (h, z, 1 - y)))]
    ppermute x3, waiting for transfers between devices: 1.89 us -> 0.83 us  [core_swap(): return lax.ppermute(x, mesh_axes, everyone(lambda h, z, y: (h ^ 1, z, y)))]
    ppermute x4, starting transfers between devices: 5.77 us -> 4.71 us  [step(): return lax.ppermute(x, mesh_axes, everyone(target))]
    ppermute x3, starting transfers between devices: 1.66 us -> 1.16 us  [core_swap(): return lax.ppermute(x, mesh_axes, everyone(lambda h, z, y: (h ^ 1, z, y)))]
  transfers between devices with their start and end apart: 17 -> 17, of which waited for: 8 -> 7; matrix products, arithmetic and copies ran while one was open for 0% -> 0% of each run, Pallas kernels for 26% -> 33%
where the time goes in v5:
time: 48.4 us; the launch traced here: 48.2 us
  Pallas kernels  18.4 us (38%)
  starting transfers between devices  17.2 us (36%)
  waiting for transfers between devices  11.9 us (25%)
  between operations  0.76 us (2%)
    pallas_call x12, Pallas kernels, run(): pl.pallas_call(body, out_shape=outs, in_specs=[pl.BlockSpec(memory_space=...  16.9 us
    ppermute x7, starting transfers between devices, exchange(): lax.ppermute(part, mesh_axes, everyone(target(m)))  8.28 us
    ppermute x7, waiting for transfers between devices, exchange(): lax.ppermute(part, mesh_axes, everyone(target(m)))  5.07 us
    ppermute x4, starting transfers between devices, step(): return lax.ppermute(x, mesh_axes, everyone(target))  4.71 us
    ppermute x4, waiting for transfers between devices, step(): return lax.ppermute(x, mesh_axes, everyone(target))  3.76 us
    ppermute x1, starting transfers between devices, on_device(): lax.ppermute(second, mesh_axes, everyone(inside))  2.59 us
    ppermute x1, waiting for transfers between devices, y_swap(): return lax.ppermute(x, mesh_axes, everyone(lambda h, z, y: (h, z, 1 - y)))  2.22 us
    pallas_call x1, Pallas kernels, on_device(): pl.pallas_call(pack_body, out_shape=pack_outs, in_specs=[raw] * 6, out_sp...  1.47 us
  transfers between devices with their start and end apart: 17, of which 7 were waited for; matrix products, arithmetic and copies ran while one was open for 0% of the time, Pallas kernels for 33%

profile of v5, /device:TPU:0, one launch (start us, length us, event | category | flops | bytes accessed | tf_op | source)
XLA Modules:
  0.0 48.2 jit_solution(610242705975787307)
XLA Ops:
  0.6 1.5 %pack.1 = (bf16[4,192,128]{2,1,0:T(8,128)(2,1)S(1)}, bf16[1152,128]{1,0:T(8,128)(2,1)S(1)}, bf16[48,1024]{1,0:T(8,128)(2,1)S(1)}, bf16[1,128,1024]{2,1,0:T(8,128...) custom-call(bf16[1,128,512]{2,1,0:T(8,128)(2,1)} %q_hbm.1, bf16[1,128,512]{2,1,0:T(8,128)(2,1)} %k_hbm.1, ...), custom_call_target="tpu_custom_call" | custom-call | tf_op jit(solution)/shard_map/pack/pallas_call | solution.py:161
  2.1 0.5 %collective-permute-start = (bf16[1152,128]{1,0:T(8,128)(2,1)S(1)}, bf16[1152,128]{1,0:T(8,128)(2,1)S(1)}, u32[]{:S(2)}, u32[]{:S(2)}) collective-permute-start(bf16[1152,128]{1,0:T(8,128)(2,1)S(1)} %get-tuple-element.49), channel_id=1, source_target_pairs={{0,8},{1,9},{2,10},{3,11},{4,12},{5,13},{6,14},{7,15},{8,0},{9,1},... | collective-permute-start | bytes 884744 | tf_op jit(solution)/shard_map/ppermute | solution.py:185
  2.6 2.6 %collective-permute-start.1 = (bf16[48,1024]{1,0:T(8,128)(2,1)S(1)}, bf16[48,1024]{1,0:T(8,128)(2,1)S(1)}, u32[]{:S(2)}, u32[]{:S(2)}) collective-permute-start(bf16[48,1024]{1,0:T(8,128)(2,1)S(1)} %get-tuple-element.50), channel_id=1, source_target_pairs={{0,1},{1,0},{2,3},{3,2},{4,5},{5,4},{6,7},{7,6},{8,16},{9,17},{10,... | collective-permute-start | bytes 294920 | tf_op jit(solution)/shard_map/ppermute | solution.py:250
  5.2 0.1 collective-permute-start.2
  5.3 0.0 collective-permute-done.refs_2_.got_ref.refs_3_
  5.3 2.7 %collective-permute-start.3 = (bf16[2,192,128]{2,1,0:T(8,128)(2,1)S(1)}, bf16[2,192,128]{2,1,0:T(8,128)(2,1)S(1)}, u32[]{:S(2)}, u32[]{:S(2)}) collective-permute-start(bf16[2,192,128]{2,1,0:T(8,128)(2,1)S(1)} %get-tuple-element.53), channel_id=1, source_target_pairs={{0,16},{1,17},{2,18},{3,19},{4,20},{5,21},{6,22},{7,23},{8,24},{9,... | collective-permute-start | bytes 294920 | tf_op jit(solution)/shard_map/ppermute | solution.py:215
  8.0 1.5 %collective-permute-start.4 = (bf16[2,192,128]{2,1,0:T(8,128)(2,1)S(1)}, bf16[2,192,128]{2,1,0:T(8,128)(2,1)S(1)}, u32[]{:S(2)}, u32[]{:S(2)}) collective-permute-start(bf16[2,192,128]{2,1,0:T(8,128)(2,1)S(1)} %get-tuple-element.54), channel_id=1, source_target_pairs={{0,1},{1,0},{2,3},{3,2},{4,5},{5,4},{6,7},{7,6},{8,9},{9,8},{10,11... | collective-permute-start | bytes 294920 | tf_op jit(solution)/shard_map/ppermute | solution.py:215
  9.5 0.0 collective-permute-start.5
  9.5 0.0 collective-permute-done.1.refs_3_
  9.5 0.0 collective-permute-done.2.refs_4_
  9.5 2.9 %conv.1.refs_6_ = bf16[128,768]{1,0:T(8,128)(2,1)S(1)} custom-call(bf16[1,128,1024]{2,1,0:T(8,128)(2,1)S(1)} %get-tuple-element.47.refs_0_, bf16[1,128,1024]{2,1,0:T(8,128)(2,1)S(1)} %get-tuple-element.48.refs_1_, bf16[1152,128]{1,0:T(8,128)(2,1)S(1)} %collective-permute-done.refs_2_.got_ref.refs_3_, bf16[48,1024]{1,0:T(8,128)(2,1)S(1)} %collective-permute-done.1.refs_3_, ...), custom_call_target="tpu_custom_call" | custom-call | flops 3000000000 | tf_op jit(solution)/shard_map/conv/pallas_call | solution.py:39
  12.4 0.0 collective-permute-done.3.refs_0_.refs_4_
  12.4 1.7 %collective-permute-done.4.refs_1_.refs_5_ = bf16[2,192,128]{2,1,0:T(8,128)(2,1)S(1)} collective-permute-done((bf16[2,192,128]{2,1,0:T(8,128)(2,1)S(1)}, bf16[2,192,128]{2,1,0:T(8,128)(2,1)S(1)}, u32[]{:S(2)}, u32[]{:S(2)}) %collective-permute-start.4) | collective-permute-done | bytes 98336 | tf_op jit(solution)/shard_map/ppermute | solution.py:215
  14.1 0.9 %collective-permute-done.5.refs_2_.refs_6_ = bf16[2,192,128]{2,1,0:T(8,128)(2,1)S(1)} collective-permute-done((bf16[2,192,128]{2,1,0:T(8,128)(2,1)S(1)}, bf16[2,192,128]{2,1,0:T(8,128)(2,1)S(1)}, u32[]{:S(2)}, u32[]{:S(2)}) %collective-permute-start.5) | collective-permute-done | bytes 98336 | tf_op jit(solution)/shard_map/ppermute | solution.py:215
  15.1 0.0 copy-start
  15.1 3.0 %collective-permute-start.7 = (bf16[1024,128]{1,0:T(8,128)(2,1)S(1)}, bf16[1024,128]{1,0:T(8,128)(2,1)S(1)}, u32[]{:S(2)}, u32[]{:S(2)}) collective-permute-start(bf16[1024,128]{1,0:T(8,128)(2,1)S(1)} %keys.1.refs_1_), channel_id=1, source_target_pairs={{0,2},{1,3},{2,0},{3,1},{4,6},{5,7},{6,4},{7,5},{8,10},{9,11},{10,... | collective-permute-start | bytes 786440 | tf_op jit(solution)/shard_map/ppermute | solution.py:192
  18.1 0.0 collective-permute-start.8
  18.1 1.8 %conv_last.1 = (bf16[4,64,128]{2,1,0:T(8,128)(2,1)S(1)}, bf16[4,64,128]{2,1,0:T(8,128)(2,1)S(1)}, bf16[2,128,256]{2,1,0:T(8,128)(2,1)S(1)}, bf16[2,128,256]{2,1,0:T(8,128)(2,1)S(1)}) custom-call(bf16[1,128,1024]{2,1,0:T(8,128)(2,1)S(1)} %get-tuple-element.47.refs_0_, bf16[1,128,1024]{2,1,0:T(8,128)(2,1)S(1)} %get-tuple-element.48.refs_1_, ...), custom_call_target="tpu_custom_call" | custom-call | flops 3000000000 | tf_op jit(solution)/shard_map/conv_last/pallas_call | solution.py:39
  19.9 0.6 %collective-permute-start.9 = (bf16[4,64,128]{2,1,0:T(8,128)(2,1)S(1)}, bf16[4,64,128]{2,1,0:T(8,128)(2,1)S(1)}, u32[]{:S(2)}, u32[]{:S(2)}) collective-permute-start(bf16[4,64,128]{2,1,0:T(8,128)(2,1)S(1)} %get-tuple-element.67), channel_id=1, source_target_pairs={{0,8},{1,9},{2,10},{3,11},{4,12},{5,13},{6,14},{7,15},{8,0},{9,1},... | collective-permute-start | bytes 196616 | tf_op jit(solution)/shard_map/ppermute | solution.py:185
  20.5 0.1 collective-permute-start.6
  20.5 0.8 %collective-permute-done.9.got_ref.refs_1_ = bf16[4,64,128]{2,1,0:T(8,128)(2,1)S(1)} collective-permute-done((bf16[4,64,128]{2,1,0:T(8,128)(2,1)S(1)}, bf16[4,64,128]{2,1,0:T(8,128)(2,1)S(1)}, u32[]{:S(2)}, u32[]{:S(2)}) %collective-permute-start.9) | collective-permute-done | bytes 65568 | tf_op jit(solution)/shard_map/ppermute | solution.py:185
  21.4 0.2 collective-permute-start.10
  21.5 2.0 %collective-permute-start.11 = (bf16[2,64,128]{2,1,0:T(8,128)(2,1)S(1)}, bf16[2,64,128]{2,1,0:T(8,128)(2,1)S(1)}, u32[]{:S(2)}, u32[]{:S(2)}) collective-permute-start(bf16[2,64,128]{2,1,0:T(8,128)(2,1)S(1)} %get-tuple-element.69), channel_id=1, source_target_pairs={{0,1},{1,0},{2,3},{3,2},{4,5},{5,4},{6,7},{7,6},{8,9},{9,8},{10,11... | collective-permute-start | bytes 98312 | tf_op jit(solution)/shard_map/ppermute | solution.py:215
  23.5 1.0 %collective-permute-done.7.refs_7_ = bf16[1024,128]{1,0:T(8,128)(2,1)S(1)} collective-permute-done((bf16[1024,128]{1,0:T(8,128)(2,1)S(1)}, bf16[1024,128]{1,0:T(8,128)(2,1)S(1)}, u32[]{:S(2)}, u32[]{:S(2)}) %collective-permute-start.7) | collective-permute-done | bytes 262176 | tf_op jit(solution)/shard_map/ppermute | solution.py:192
  24.5 1.7 %collective-permute-start.12 = (bf16[2,64,128]{2,1,0:T(8,128)(2,1)S(1)}, bf16[2,64,128]{2,1,0:T(8,128)(2,1)S(1)}, u32[]{:S(2)}, u32[]{:S(2)}) collective-permute-start(bf16[2,64,128]{2,1,0:T(8,128)(2,1)S(1)} %get-tuple-element.70), channel_id=1, source_target_pairs={{0,17},{1,16},{2,19},{3,18},{4,21},{5,20},{6,23},{7,22},{8,25},{9,... | collective-permute-start | bytes 98312 | tf_op jit(solution)/shard_map/ppermute | solution.py:215
  26.2 0.0 collective-permute-done.8.refs_8_
  26.2 0.0 copy-done
  26.2 4.8 %scores.1 = (bf16[4,2304,256]{2,1,0:T(8,128)(2,1)S(1)}, f32[4,1,256]{2,1,0:T(1,128)S(1)}, f32[4,64,256]{2,1,0:T(8,128)S(1)}, bf16[3072,128]{1,0:T(8,128)(2,1)S(1...) custom-call(s32[8]{0:T(128)S(1)} %copy-done, bf16[1024,128]{1,0:T(8,128)(2,1)S(1)} %keys.1.refs_1_, ...), custom_call_target="tpu_custom_call" | custom-call | flops 8999999488 | tf_op jit(solution)/shard_map/scores/pallas_call | solution.py:39
  31.0 0.0 collective-permute-done.10.refs_2_
  31.0 0.0 collective-permute-done.11.refs_3_
  31.0 0.0 collective-permute-done.12.refs_4_
  31.0 3.2 %far.1 = (bf16[1024,128]{1,0:T(8,128)(2,1)S(1)}, f32[4,1,256]{2,1,0:T(1,128)S(1)}, f32[4,64,256]{2,1,0:T(8,128)S(1)}, bf16[1024,128]{1,0:T(8,128)(2,1)S(1)}, bf16[1024,128]{1,0:T(8,128)(2,1)S(1)}) custom-call(bf16[4,64,128]{2,1,0:T(8,128)(2,1)S(1)} %get-tuple-element.66.keep_ref.refs_0_, bf16[4,64,128]{2,1,0:T(8,128)(2,1)S(1)} %collective-permute-done.9.got_ref.refs_1_, ...), custom_call_target="tpu_custom_call" | custom-call | flops 4000000000 | tf_op jit(solution)/shard_map/far/pallas_call | solution.py:39
  34.2 1.7 %collective-permute-start.14 = (bf16[1024,128]{1,0:T(8,128)(2,1)S(1)}, bf16[1024,128]{1,0:T(8,128)(2,1)S(1)}, u32[]{:S(2)}, u32[]{:S(2)}) collective-permute-start(bf16[1024,128]{1,0:T(8,128)(2,1)S(1)} %get-tuple-element.82), channel_id=1, source_target_pairs={{0,2},{1,3},{2,0},{3,1},{4,6},{5,7},{6,4},{7,5},{8,10},{9,11},{10,... | collective-permute-start | bytes 786440 | tf_op jit(solution)/shard_map/ppermute | solution.py:192
  36.0 0.0 collective-permute-start.15
  36.0 2.4 %near.1 = (f32[1024,128]{1,0:T(8,128)S(1)}, bf16[256,128]{1,0:T(8,128)(2,1)S(1)}, bf16[256,128]{1,0:T(8,128)(2,1)S(1)}) custom-call(bf16[4,2304,256]{2,1,0:T(8,128)(2,1)S(1)} %get-tuple-element.64.refs_5_.refs_0_, f32[4,1,256]{2,1,0:T(1,128)S(1)} %get-tuple-element.65.refs_6_.refs_1_, f32[4,1,256]{2,1,0:T(1,128)S(1)} %get-tuple-element.75.refs_2_, ...), custom_call_target="tpu_custom_call" | custom-call | flops 4000000000 | tf_op jit(solution)/shard_map/near/pallas_call | solution.py:39
  38.4 0.0 collective-permute-done.6.got_ref.refs_1_
  38.4 0.3 collective-permute-start.13
  38.7 2.7 %collective-permute-done.14.refs_0_ = bf16[1024,128]{1,0:T(8,128)(2,1)S(1)} collective-permute-done((bf16[1024,128]{1,0:T(8,128)(2,1)S(1)}, bf16[1024,128]{1,0:T(8,128)(2,1)S(1)}, u32[]{:S(2)}, u32[]{:S(2)}) %collective-permute-start.14) | collective-permute-done | bytes 262176 | tf_op jit(solution)/shard_map/ppermute | solution.py:192
  41.4 0.0 collective-permute-done.15.refs_1_
  41.5 0.2 sum.1
  41.6 0.3 collective-permute-start.16
  42.0 2.4 %collective-permute-done.13.refs_2_ = bf16[2,128,256]{2,1,0:T(8,128)(2,1)S(1)} collective-permute-done((bf16[2,128,256]{2,1,0:T(8,128)(2,1)S(1)}, bf16[2,128,256]{2,1,0:T(8,128)(2,1)S(1)}, u32[]{:S(2)}, u32[]{:S(2)}) %collective-permute-start.13) | collective-permute-done | bytes 131104 | tf_op jit(solution)/shard_map/ppermute | solution.py:215
  44.4 0.7 %resid.1 = bf16[1,512,256]{2,1,0:T(8,128)(2,1)} custom-call(bf16[2,128,256]{2,1,0:T(8,128)(2,1)S(1)} %get-tuple-element.79.keep_ref.refs_0_, bf16[2,128,256]{2,1,0:T(8,128)(2,1)S(1)} %collective-permute-done.6.got_ref.refs_1_, bf16[2,128,256]{2,1,0:T(8,128)(2,1)S(1)} %collective-permute-done.13.refs_2_), custom_call_target="tpu_custom_call" | custom-call | flops 1000000000 | tf_op jit(solution)/shard_map/resid/pallas_call | solution.py:39
  45.1 2.2 %collective-permute-done.16.refs_1_ = bf16[768,128]{1,0:T(8,128)(2,1)S(1)} collective-permute-done((bf16[768,128]{1,0:T(8,128)(2,1)S(1)}, bf16[768,128]{1,0:T(8,128)(2,1)S(1)}, u32[]{:S(2)}, u32[]{:S(2)}) %collective-permute-start.16) | collective-permute-done | bytes 196640 | tf_op jit(solution)/shard_map/ppermute | solution.py:591
  47.4 0.9 %last.1 = (bf16[1,512,128]{2,1,0:T(8,128)(2,1)}, bf16[1,512,128]{2,1,0:T(8,128)(2,1)}, bf16[1,512,128]{2,1,0:T(8,128)(2,1)}) custom-call(bf16[512,128]{1,0:T(8,128)(2,1)S(1)} %get-tuple-element.84.refs_0_, bf16[768,128]{1,0:T(8,128)(2,1)S(1)} %collective-permute-done.16.refs_1_, bf16[256,128]{1,0:T(8,128)(2,1)S(1)} %get-tuple-element.86.refs_2_), custom_call_target="tpu_custom_call" | custom-call | tf_op jit(solution)/shard_map/last/pallas_call | solution.py:39
  (4 shorter events, 0.1 us)
Async XLA Ops:
  2.1 3.2 %collective-permute-start = (bf16[1152,128]{1,0:T(8,128)(2,1)S(1)}, bf16[1152,128]{1,0:T(8,128)(2,1)S(1)}, u32[]{:S(2)}, u32[]{:S(2)}) collective-permute-start(bf16[1152,128]{1,0:T(8,128)(2,1)S(1)} %get-tuple-element.49), channel_id=1, source_target_pairs={{0,8},{1,9},{2,10},{3,11},{4,12},{5,13},{6,14},{7,15},{8,0},{9,1},... | collective-permute-start | bytes 884744 | tf_op jit(solution)/shard_map/ppermute | solution.py:185
  2.6 6.9 %collective-permute-start.1 = (bf16[48,1024]{1,0:T(8,128)(2,1)S(1)}, bf16[48,1024]{1,0:T(8,128)(2,1)S(1)}, u32[]{:S(2)}, u32[]{:S(2)}) collective-permute-start(bf16[48,1024]{1,0:T(8,128)(2,1)S(1)} %get-tuple-element.50), channel_id=1, source_target_pairs={{0,1},{1,0},{2,3},{3,2},{4,5},{5,4},{6,7},{7,6},{8,16},{9,17},{10,... | collective-permute-start | bytes 294920 | tf_op jit(solution)/shard_map/ppermute | solution.py:250
  5.2 4.3 %collective-permute-start.2 = (bf16[48,1024]{1,0:T(8,128)(2,1)S(1)}, bf16[48,1024]{1,0:T(8,128)(2,1)S(1)}, u32[]{:S(2)}, u32[]{:S(2)}) collective-permute-start(bf16[48,1024]{1,0:T(8,128)(2,1)S(1)} %get-tuple-element.50), channel_id=1, source_target_pairs={{0,8},{1,24},{2,25},{3,26},{4,27},{5,28},{6,29},{7,30},{8,0},{9,16... | collective-permute-start | bytes 294920 | tf_op jit(solution)/shard_map/ppermute | solution.py:251
  5.3 7.1 %collective-permute-start.3 = (bf16[2,192,128]{2,1,0:T(8,128)(2,1)S(1)}, bf16[2,192,128]{2,1,0:T(8,128)(2,1)S(1)}, u32[]{:S(2)}, u32[]{:S(2)}) collective-permute-start(bf16[2,192,128]{2,1,0:T(8,128)(2,1)S(1)} %get-tuple-element.53), channel_id=1, source_target_pairs={{0,16},{1,17},{2,18},{3,19},{4,20},{5,21},{6,22},{7,23},{8,24},{9,... | collective-permute-start | bytes 294920 | tf_op jit(solution)/shard_map/ppermute | solution.py:215
  8.0 6.2 %collective-permute-start.4 = (bf16[2,192,128]{2,1,0:T(8,128)(2,1)S(1)}, bf16[2,192,128]{2,1,0:T(8,128)(2,1)S(1)}, u32[]{:S(2)}, u32[]{:S(2)}) collective-permute-start(bf16[2,192,128]{2,1,0:T(8,128)(2,1)S(1)} %get-tuple-element.54), channel_id=1, source_target_pairs={{0,1},{1,0},{2,3},{3,2},{4,5},{5,4},{6,7},{7,6},{8,9},{9,8},{10,11... | collective-permute-start | bytes 294920 | tf_op jit(solution)/shard_map/ppermute | solution.py:215
  9.5 5.5 %collective-permute-start.5 = (bf16[2,192,128]{2,1,0:T(8,128)(2,1)S(1)}, bf16[2,192,128]{2,1,0:T(8,128)(2,1)S(1)}, u32[]{:S(2)}, u32[]{:S(2)}) collective-permute-start(bf16[2,192,128]{2,1,0:T(8,128)(2,1)S(1)} %get-tuple-element.55), channel_id=1, source_target_pairs={{0,17},{1,16},{2,19},{3,18},{4,21},{5,20},{6,23},{7,22},{8,25},{9,... | collective-permute-start | bytes 294920 | tf_op jit(solution)/shard_map/ppermute | solution.py:215
  15.1 11.1 %copy-start = (s32[8]{0:T(128)S(1)}, s32[8]{0:T(128)}, u32[]{:S(2)}) copy-start(s32[8]{0:T(128)} %refs_0_.1) | copy-start | bytes 100
  15.1 9.5 %collective-permute-start.7 = (bf16[1024,128]{1,0:T(8,128)(2,1)S(1)}, bf16[1024,128]{1,0:T(8,128)(2,1)S(1)}, u32[]{:S(2)}, u32[]{:S(2)}) collective-permute-start(bf16[1024,128]{1,0:T(8,128)(2,1)S(1)} %keys.1.refs_1_), channel_id=1, source_target_pairs={{0,2},{1,3},{2,0},{3,1},{4,6},{5,7},{6,4},{7,5},{8,10},{9,11},{10,... | collective-permute-start | bytes 786440 | tf_op jit(solution)/shard_map/ppermute | solution.py:192
  18.1 8.1 %collective-permute-start.8 = (bf16[1024,128]{1,0:T(8,128)(2,1)S(1)}, bf16[1024,128]{1,0:T(8,128)(2,1)S(1)}, u32[]{:S(2)}, u32[]{:S(2)}) collective-permute-start(bf16[1024,128]{1,0:T(8,128)(2,1)S(1)} %keys.1.refs_1_), channel_id=1, source_target_pairs={{0,8},{1,9},{2,4},{3,5},{4,2},{5,3},{6,14},{7,15},{8,0},{9,1},{10,... | collective-permute-start | bytes 786440 | tf_op jit(solution)/shard_map/ppermute | solution.py:192
  19.9 1.5 %collective-permute-start.9 = (bf16[4,64,128]{2,1,0:T(8,128)(2,1)S(1)}, bf16[4,64,128]{2,1,0:T(8,128)(2,1)S(1)}, u32[]{:S(2)}, u32[]{:S(2)}) collective-permute-start(bf16[4,64,128]{2,1,0:T(8,128)(2,1)S(1)} %get-tuple-element.67), channel_id=1, source_target_pairs={{0,8},{1,9},{2,10},{3,11},{4,12},{5,13},{6,14},{7,15},{8,0},{9,1},... | collective-permute-start | bytes 196616 | tf_op jit(solution)/shard_map/ppermute | solution.py:185
  20.5 17.9 %collective-permute-start.6 = (bf16[2,128,256]{2,1,0:T(8,128)(2,1)S(1)}, bf16[2,128,256]{2,1,0:T(8,128)(2,1)S(1)}, u32[]{:S(2)}, u32[]{:S(2)}) collective-permute-start(bf16[2,128,256]{2,1,0:T(8,128)(2,1)S(1)} %get-tuple-element.63), channel_id=1, source_target_pairs={{0,8},{1,9},{2,10},{3,11},{4,12},{5,13},{6,14},{7,15},{8,0},{9,1},... | collective-permute-start | bytes 393224 | tf_op jit(solution)/shard_map/ppermute | solution.py:185
  21.4 9.7 %collective-permute-start.10 = (bf16[2,64,128]{2,1,0:T(8,128)(2,1)S(1)}, bf16[2,64,128]{2,1,0:T(8,128)(2,1)S(1)}, u32[]{:S(2)}, u32[]{:S(2)}) collective-permute-start(bf16[2,64,128]{2,1,0:T(8,128)(2,1)S(1)} %get-tuple-element.68), channel_id=1, source_target_pairs={{0,16},{1,17},{2,18},{3,19},{4,20},{5,21},{6,22},{7,23},{8,24},{9,... | collective-permute-start | bytes 98312 | tf_op jit(solution)/shard_map/ppermute | solution.py:215
  21.5 9.5 %collective-permute-start.11 = (bf16[2,64,128]{2,1,0:T(8,128)(2,1)S(1)}, bf16[2,64,128]{2,1,0:T(8,128)(2,1)S(1)}, u32[]{:S(2)}, u32[]{:S(2)}) collective-permute-start(bf16[2,64,128]{2,1,0:T(8,128)(2,1)S(1)} %get-tuple-element.69), channel_id=1, source_target_pairs={{0,1},{1,0},{2,3},{3,2},{4,5},{5,4},{6,7},{7,6},{8,9},{9,8},{10,11... | collective-permute-start | bytes 98312 | tf_op jit(solution)/shard_map/ppermute | solution.py:215
  24.5 6.5 %collective-permute-start.12 = (bf16[2,64,128]{2,1,0:T(8,128)(2,1)S(1)}, bf16[2,64,128]{2,1,0:T(8,128)(2,1)S(1)}, u32[]{:S(2)}, u32[]{:S(2)}) collective-permute-start(bf16[2,64,128]{2,1,0:T(8,128)(2,1)S(1)} %get-tuple-element.70), channel_id=1, source_target_pairs={{0,17},{1,16},{2,19},{3,18},{4,21},{5,20},{6,23},{7,22},{8,25},{9,... | collective-permute-start | bytes 98312 | tf_op jit(solution)/shard_map/ppermute | solution.py:215
  34.2 7.2 %collective-permute-start.14 = (bf16[1024,128]{1,0:T(8,128)(2,1)S(1)}, bf16[1024,128]{1,0:T(8,128)(2,1)S(1)}, u32[]{:S(2)}, u32[]{:S(2)}) collective-permute-start(bf16[1024,128]{1,0:T(8,128)(2,1)S(1)} %get-tuple-element.82), channel_id=1, source_target_pairs={{0,2},{1,3},{2,0},{3,1},{4,6},{5,7},{6,4},{7,5},{8,10},{9,11},{10,... | collective-permute-start | bytes 786440 | tf_op jit(solution)/shard_map/ppermute | solution.py:192
  36.0 5.5 %collective-permute-start.15 = (bf16[1024,128]{1,0:T(8,128)(2,1)S(1)}, bf16[1024,128]{1,0:T(8,128)(2,1)S(1)}, u32[]{:S(2)}, u32[]{:S(2)}) collective-permute-start(bf16[1024,128]{1,0:T(8,128)(2,1)S(1)} %get-tuple-element.83), channel_id=1, source_target_pairs={{0,8},{1,9},{2,4},{3,5},{4,2},{5,3},{6,14},{7,15},{8,0},{9,1},{10,... | collective-permute-start | bytes 786440 | tf_op jit(solution)/shard_map/ppermute | solution.py:192
  38.4 6.0 %collective-permute-start.13 = (bf16[2,128,256]{2,1,0:T(8,128)(2,1)S(1)}, bf16[2,128,256]{2,1,0:T(8,128)(2,1)S(1)}, u32[]{:S(2)}, u32[]{:S(2)}) collective-permute-start(bf16[2,128,256]{2,1,0:T(8,128)(2,1)S(1)} %regroup_resid.1), channel_id=1, source_target_pairs={{0,16},{1,17},{2,18},{3,19},{4,20},{5,21},{6,22},{7,23},{8,24},{9,... | collective-permute-start | bytes 393224 | tf_op jit(solution)/shard_map/ppermute | solution.py:215
  41.6 5.7 %collective-permute-start.16 = (bf16[768,128]{1,0:T(8,128)(2,1)S(1)}, bf16[768,128]{1,0:T(8,128)(2,1)S(1)}, u32[]{:S(2)}, u32[]{:S(2)}) collective-permute-start(bf16[768,128]{1,0:T(8,128)(2,1)S(1)} %get-tuple-element.85), channel_id=1, source_target_pairs={{0,1},{1,0},{2,3},{3,2},{4,5},{5,4},{6,7},{7,6},{8,9},{9,8},{10,11... | collective-permute-start | bytes 589832 | tf_op jit(solution)/shard_map/ppermute | solution.py:591

commit v6 on v5

--- a/solution.py
+++ b/solution.py
@@ -22,7 +22,7 @@
 VMEM_LIMIT = 12 * 1024 * 1024
 CONV_COST = (3_000_000_000, 0, 0)
 SCORES_COST = (9_000_000_000, 0, 0)
-FAR_COST = (4_000_000_000, 0, 0)
+FAR_COST = (2_000_000_000, 0, 0)
 NEAR_COST = (4_000_000_000, 0, 0)
 RESID_COST = (1_000_000_000, 0, 0)
 
@@ -481,51 +481,73 @@
         real = jnp.logical_and(partner >= 0, partner < z_count)
         return jnp.where(real, ref[...].astype(F32), 0.0)
 
-    def far_body(*refs):
-        grad_refs = refs[: 1 + chips]
-        e_ref, inv_ref, out_ref, kv, kt, qz, hz, delta_ref, dq = refs[1 + chips : 10 + chips]
-        back_refs = refs[10 + chips : -3]
-        acc, ds_sc, slopes_sc = refs[-3:]
-        z = lax.axis_index("z")
-        low = lax.broadcasted_iota(jnp.int32, (half, LANES), 1) < HEAD_DIM
-        for member, take in arrivals(my_chip(), my_core(), grad_refs[0], grad_refs[1], grad_refs[2:]):
-            g = take().astype(F32)
-            for i, part in enumerate((pltpu.roll(g, HEAD_DIM, 1), g)):
-                at = pl.ds(pl.multiple_of(member * rows + i * half, half), half)
-                hz[at, :] = jnp.where(low, 0.0, part).astype(BF16)
-        for a in range(q_tiles):
-            g = jnp.transpose(hz[at_tile(a), :].astype(F32))[HEAD_DIM:LANES]
-            delta_ref[a] = jnp.sum(g * out_ref[a], axis=0, keepdims=True)
-        for t in range(k_tiles):
-            if not any(t in seen(a) for a in range(q_tiles)):
-                acc[at_tile(t), :] = jnp.zeros((QT, LANES), F32)
-        for a in range(q_tiles):
-            left = [t for t in seen(a) if t < own_tiles[0]]
-            right = [t for t in seen(a) if t > own_tiles[-1]]
-            dq[a] = sum(
-                key_tiles(a, ts, e_ref, inv_ref, delta_ref, kv, kt, qz, hz, acc, ds_sc.at[side], slopes_sc.at[side], 0)
-                for side, ts in enumerate((left, right))
-            )
-        for i, (d, phase) in enumerate(steps):
-            odd = ((z // d) % 2) == 1
+    def far_call(i, first, ins):
+        d, phase = steps[i]
+
+        def body(*refs):
+            if first:
+                grad_refs = refs[: 1 + chips]
+                e_ref, inv_ref, out_ref, kv, kt, qz, hz, delta_ref, dq, back_ref = refs[1 + chips : 11 + chips]
+                low = lax.broadcasted_iota(jnp.int32, (half, LANES), 1) < HEAD_DIM
+                for member, take in arrivals(my_chip(), my_core(), grad_refs[0], grad_refs[1], grad_refs[2:]):
+                    g = take().astype(F32)
+                    for k, piece in enumerate((pltpu.roll(g, HEAD_DIM, 1), g)):
+                        at = pl.ds(pl.multiple_of(member * rows + k * half, half), half)
+                        hz[at, :] = jnp.where(low, 0.0, piece).astype(BF16)
+                for a in range(q_tiles):
+                    g = jnp.transpose(hz[at_tile(a), :].astype(F32))[HEAD_DIM:LANES]
+                    delta_ref[a] = jnp.sum(g * out_ref[a], axis=0, keepdims=True)
+            else:
+                e_ref, inv_ref, kv, kt, qz, hz, delta_ref, dq_in, dq, back_ref = refs[:10]
+            acc, ds_sc, slopes_sc = refs[-3:]
+            odd = ((lax.axis_index("z") // d) % 2) == 1
             right = odd if phase else jnp.logical_not(odd)
-            side = jnp.where(right, near + d, near - d) * supers
-            back_refs[i][...] = acc[pl.ds(pl.multiple_of(side, supers), supers), :].astype(BF16)
-
-    far = call(
-        far_body,
-        [vmem((supers, LANES)), vmem((q_tiles, 1, QT), F32), vmem((q_tiles, HEAD_DIM, QT), F32)]
-        + [vmem((supers, LANES))] * n_back,
-        scratch=[
-            pltpu.VMEM((ext, LANES), F32),
-            pltpu.VMEM((2, near * supers, QT), BF16),
-            pltpu.VMEM((2, near * supers, QT), F32),
-        ],
-        name="far",
-        cost=FAR_COST,
-    )(*on_chip(*grads, exps, inverse, outs, kv, kt, qz))
-    hz, delta, dq_far = far[:3]
-    back = [step(far[3 + i], d, phase) for i, (d, phase) in enumerate(steps)]
+
+            def side(tiles_here):
+                for t in tiles_here:
+                    if not any(t in seen(a) for a in range(q_tiles)):
+                        acc[at_tile(t - tiles_here[0]), :] = jnp.zeros((QT, LANES), F32)
+                for a in range(q_tiles):
+                    ts = [t for t in tiles_here if t in seen(a)]
+                    total = jnp.zeros((HEAD_DIM, QT), F32) if first else dq_in[a]
+                    if ts:
+                        total = total + key_tiles(
+                            a, ts, e_ref, inv_ref, delta_ref, kv, kt, qz, hz, acc,
+                            ds_sc.at[a % 2], slopes_sc.at[a % 2], tiles_here[0],
+                        )
+                    dq[a] = total
+
+            def tiles_at(distance):
+                return range((near + distance) * q_tiles, (near + distance + 1) * q_tiles)
+
+            @pl.when(right)
+            def _():
+                side(tiles_at(d))
+
+            @pl.when(jnp.logical_not(right))
+            def _():
+                side(tiles_at(-d))
+
+            back_ref[...] = acc[...].astype(BF16)
+
+        ready = [vmem((supers, LANES)), vmem((q_tiles, 1, QT), F32)] if first else []
+        return call(
+            body,
+            ready + [vmem((q_tiles, HEAD_DIM, QT), F32), vmem((supers, LANES))],
+            scratch=[
+                pltpu.VMEM((supers, LANES), F32),
+                pltpu.VMEM((2, supers, QT), BF16),
+                pltpu.VMEM((2, supers, QT), F32),
+            ],
+            name="far" if first else "far_next",
+            cost=FAR_COST,
+        )(*on_chip(*ins))
+
+    hz, delta, dq_far, part_here = far_call(0, True, (*grads, exps, inverse, outs, kv, kt, qz))
+    back = [step(part_here, *steps[0])]
+    for i in range(1, n_back):
+        dq_far, part_here = far_call(i, False, (exps, inverse, kv, kt, qz, hz, delta, dq_far))
+        back.append(step(part_here, *steps[i]))
 
     hb = block // 2
 

time: 48.4 us -> 47.6 us (0.983)
  waiting for transfers between devices: 11.9 us -> 10.2 us
    ppermute x4, waiting for transfers between devices: 3.76 us -> 2.06 us  [step(): return lax.ppermute(x, mesh_axes, everyone(target))]
    ppermute x7, waiting for transfers between devices: 5.07 us -> 6.37 us  [exchange(): lax.ppermute(part, mesh_axes, everyone(target(m)))]
    ppermute x1, waiting for transfers between devices: 2.22 us -> 0.95 us  [y_swap(): return lax.ppermute(x, mesh_axes, everyone(lambda h, z, y: (h, z, 1 - y)))]
    pallas_call x12 -> x13, Pallas kernels: 16.9 us -> 17.1 us  [run(): pl.pallas_call(body, out_shape=outs, in_specs=[pl.BlockSpec(memory_space=...]
  transfers between devices with their start and end apart: 17 -> 17, of which waited for: 7 -> 7; matrix products, arithmetic and copies ran while one was open for 0% -> 0% of each run, Pallas kernels for 33% -> 34%
where the time goes in v6:
time: 47.6 us; the launch traced here: 47.2 us
  Pallas kernels  18.6 us (39%)
  starting transfers between devices  17.6 us (37%)
  waiting for transfers between devices  10.2 us (21%)
  between operations  0.78 us (2%)
    pallas_call x13, Pallas kernels, run(): pl.pallas_call(body, out_shape=outs, in_specs=[pl.BlockSpec(memory_space=...  17.1 us
    ppermute x7, starting transfers between devices, exchange(): lax.ppermute(part, mesh_axes, everyone(target(m)))  8.29 us
    ppermute x7, waiting for transfers between devices, exchange(): lax.ppermute(part, mesh_axes, everyone(target(m)))  6.37 us
    ppermute x4, starting transfers between devices, step(): return lax.ppermute(x, mesh_axes, everyone(target))  4.73 us
    ppermute x1, starting transfers between devices, on_device(): lax.ppermute(second, mesh_axes, everyone(inside))  2.59 us
    ppermute x4, waiting for transfers between devices, step(): return lax.ppermute(x, mesh_axes, everyone(target))  2.06 us
    pallas_call x1, Pallas kernels, on_device(): pl.pallas_call(pack_body, out_shape=pack_outs, in_specs=[raw] * 6, out_sp...  1.47 us
    ppermute x3, starting transfers between devices, core_swap(): return lax.ppermute(x, mesh_axes, everyone(lambda h, z, y: (h ^ 1, z, y)))  1.16 us
  transfers between devices with their start and end apart: 17, of which 7 were waited for; matrix products, arithmetic and copies ran while one was open for 0% of the time, Pallas kernels for 34%

profile of v6, /device:TPU:0, one launch (start us, length us, event | category | flops | bytes accessed | tf_op | source)
XLA Modules:
  0.0 47.2 jit_solution(13204065655939843897)
XLA Ops:
  0.6 1.5 %pack.1 = (bf16[4,192,128]{2,1,0:T(8,128)(2,1)S(1)}, bf16[1152,128]{1,0:T(8,128)(2,1)S(1)}, bf16[48,1024]{1,0:T(8,128)(2,1)S(1)}, bf16[1,128,1024]{2,1,0:T(8,128...) custom-call(bf16[1,128,512]{2,1,0:T(8,128)(2,1)} %q_hbm.1, bf16[1,128,512]{2,1,0:T(8,128)(2,1)} %k_hbm.1, ...), custom_call_target="tpu_custom_call" | custom-call | tf_op jit(solution)/shard_map/pack/pallas_call | solution.py:161
  2.1 0.5 %collective-permute-start = (bf16[1152,128]{1,0:T(8,128)(2,1)S(1)}, bf16[1152,128]{1,0:T(8,128)(2,1)S(1)}, u32[]{:S(2)}, u32[]{:S(2)}) collective-permute-start(bf16[1152,128]{1,0:T(8,128)(2,1)S(1)} %get-tuple-element.50), channel_id=1, source_target_pairs={{0,8},{1,9},{2,10},{3,11},{4,12},{5,13},{6,14},{7,15},{8,0},{9,1},... | collective-permute-start | bytes 884744 | tf_op jit(solution)/shard_map/ppermute | solution.py:185
  2.6 2.6 %collective-permute-start.1 = (bf16[48,1024]{1,0:T(8,128)(2,1)S(1)}, bf16[48,1024]{1,0:T(8,128)(2,1)S(1)}, u32[]{:S(2)}, u32[]{:S(2)}) collective-permute-start(bf16[48,1024]{1,0:T(8,128)(2,1)S(1)} %get-tuple-element.51), channel_id=1, source_target_pairs={{0,1},{1,0},{2,3},{3,2},{4,5},{5,4},{6,7},{7,6},{8,16},{9,17},{10,... | collective-permute-start | bytes 294920 | tf_op jit(solution)/shard_map/ppermute | solution.py:250
  5.2 0.1 collective-permute-start.2
  5.3 0.0 collective-permute-done.refs_2_.got_ref.refs_3_
  5.3 2.7 %collective-permute-start.3 = (bf16[2,192,128]{2,1,0:T(8,128)(2,1)S(1)}, bf16[2,192,128]{2,1,0:T(8,128)(2,1)S(1)}, u32[]{:S(2)}, u32[]{:S(2)}) collective-permute-start(bf16[2,192,128]{2,1,0:T(8,128)(2,1)S(1)} %get-tuple-element.54), channel_id=1, source_target_pairs={{0,16},{1,17},{2,18},{3,19},{4,20},{5,21},{6,22},{7,23},{8,24},{9,... | collective-permute-start | bytes 294920 | tf_op jit(solution)/shard_map/ppermute | solution.py:215
  8.0 1.5 %collective-permute-start.4 = (bf16[2,192,128]{2,1,0:T(8,128)(2,1)S(1)}, bf16[2,192,128]{2,1,0:T(8,128)(2,1)S(1)}, u32[]{:S(2)}, u32[]{:S(2)}) collective-permute-start(bf16[2,192,128]{2,1,0:T(8,128)(2,1)S(1)} %get-tuple-element.55), channel_id=1, source_target_pairs={{0,1},{1,0},{2,3},{3,2},{4,5},{5,4},{6,7},{7,6},{8,9},{9,8},{10,11... | collective-permute-start | bytes 294920 | tf_op jit(solution)/shard_map/ppermute | solution.py:215
  9.5 0.0 collective-permute-start.5
  9.5 0.0 collective-permute-done.1.refs_3_
  9.5 0.0 collective-permute-done.2.refs_4_
  9.5 2.9 %conv.1.refs_6_ = bf16[128,768]{1,0:T(8,128)(2,1)S(1)} custom-call(bf16[1,128,1024]{2,1,0:T(8,128)(2,1)S(1)} %get-tuple-element.48.refs_0_, bf16[1,128,1024]{2,1,0:T(8,128)(2,1)S(1)} %get-tuple-element.49.refs_1_, bf16[1152,128]{1,0:T(8,128)(2,1)S(1)} %collective-permute-done.refs_2_.got_ref.refs_3_, bf16[48,1024]{1,0:T(8,128)(2,1)S(1)} %collective-permute-done.1.refs_3_, ...), custom_call_target="tpu_custom_call" | custom-call | flops 3000000000 | tf_op jit(solution)/shard_map/conv/pallas_call | solution.py:39
  12.4 0.0 collective-permute-done.3.refs_0_.refs_4_
  12.4 1.7 %collective-permute-done.4.refs_1_.refs_5_ = bf16[2,192,128]{2,1,0:T(8,128)(2,1)S(1)} collective-permute-done((bf16[2,192,128]{2,1,0:T(8,128)(2,1)S(1)}, bf16[2,192,128]{2,1,0:T(8,128)(2,1)S(1)}, u32[]{:S(2)}, u32[]{:S(2)}) %collective-permute-start.4) | collective-permute-done | bytes 98336 | tf_op jit(solution)/shard_map/ppermute | solution.py:215
  14.1 0.9 %collective-permute-done.5.refs_2_.refs_6_ = bf16[2,192,128]{2,1,0:T(8,128)(2,1)S(1)} collective-permute-done((bf16[2,192,128]{2,1,0:T(8,128)(2,1)S(1)}, bf16[2,192,128]{2,1,0:T(8,128)(2,1)S(1)}, u32[]{:S(2)}, u32[]{:S(2)}) %collective-permute-start.5) | collective-permute-done | bytes 98336 | tf_op jit(solution)/shard_map/ppermute | solution.py:215
  15.1 0.0 copy-start
  15.1 3.0 %collective-permute-start.7 = (bf16[1024,128]{1,0:T(8,128)(2,1)S(1)}, bf16[1024,128]{1,0:T(8,128)(2,1)S(1)}, u32[]{:S(2)}, u32[]{:S(2)}) collective-permute-start(bf16[1024,128]{1,0:T(8,128)(2,1)S(1)} %keys.1.refs_1_), channel_id=1, source_target_pairs={{0,2},{1,3},{2,0},{3,1},{4,6},{5,7},{6,4},{7,5},{8,10},{9,11},{10,... | collective-permute-start | bytes 786440 | tf_op jit(solution)/shard_map/ppermute | solution.py:192
  18.1 0.0 collective-permute-start.8
  18.1 1.8 %conv_last.1 = (bf16[4,64,128]{2,1,0:T(8,128)(2,1)S(1)}, bf16[4,64,128]{2,1,0:T(8,128)(2,1)S(1)}, bf16[2,128,256]{2,1,0:T(8,128)(2,1)S(1)}, bf16[2,128,256]{2,1,0:T(8,128)(2,1)S(1)}) custom-call(bf16[1,128,1024]{2,1,0:T(8,128)(2,1)S(1)} %get-tuple-element.48.refs_0_, bf16[1,128,1024]{2,1,0:T(8,128)(2,1)S(1)} %get-tuple-element.49.refs_1_, ...), custom_call_target="tpu_custom_call" | custom-call | flops 3000000000 | tf_op jit(solution)/shard_map/conv_last/pallas_call | solution.py:39
  19.9 0.6 %collective-permute-start.9 = (bf16[4,64,128]{2,1,0:T(8,128)(2,1)S(1)}, bf16[4,64,128]{2,1,0:T(8,128)(2,1)S(1)}, u32[]{:S(2)}, u32[]{:S(2)}) collective-permute-start(bf16[4,64,128]{2,1,0:T(8,128)(2,1)S(1)} %get-tuple-element.68), channel_id=1, source_target_pairs={{0,8},{1,9},{2,10},{3,11},{4,12},{5,13},{6,14},{7,15},{8,0},{9,1},... | collective-permute-start | bytes 196616 | tf_op jit(solution)/shard_map/ppermute | solution.py:185
  20.5 0.1 collective-permute-start.6
  20.5 0.8 %collective-permute-done.9.got_ref.refs_1_ = bf16[4,64,128]{2,1,0:T(8,128)(2,1)S(1)} collective-permute-done((bf16[4,64,128]{2,1,0:T(8,128)(2,1)S(1)}, bf16[4,64,128]{2,1,0:T(8,128)(2,1)S(1)}, u32[]{:S(2)}, u32[]{:S(2)}) %collective-permute-start.9) | collective-permute-done | bytes 65568 | tf_op jit(solution)/shard_map/ppermute | solution.py:185
  21.4 0.2 collective-permute-start.10
  21.5 2.0 %collective-permute-start.11 = (bf16[2,64,128]{2,1,0:T(8,128)(2,1)S(1)}, bf16[2,64,128]{2,1,0:T(8,128)(2,1)S(1)}, u32[]{:S(2)}, u32[]{:S(2)}) collective-permute-start(bf16[2,64,128]{2,1,0:T(8,128)(2,1)S(1)} %get-tuple-element.70), channel_id=1, source_target_pairs={{0,1},{1,0},{2,3},{3,2},{4,5},{5,4},{6,7},{7,6},{8,9},{9,8},{10,11... | collective-permute-start | bytes 98312 | tf_op jit(solution)/shard_map/ppermute | solution.py:215
  23.5 1.0 %collective-permute-done.7.refs_7_ = bf16[1024,128]{1,0:T(8,128)(2,1)S(1)} collective-permute-done((bf16[1024,128]{1,0:T(8,128)(2,1)S(1)}, bf16[1024,128]{1,0:T(8,128)(2,1)S(1)}, u32[]{:S(2)}, u32[]{:S(2)}) %collective-permute-start.7) | collective-permute-done | bytes 262176 | tf_op jit(solution)/shard_map/ppermute | solution.py:192
  24.5 1.7 %collective-permute-start.12 = (bf16[2,64,128]{2,1,0:T(8,128)(2,1)S(1)}, bf16[2,64,128]{2,1,0:T(8,128)(2,1)S(1)}, u32[]{:S(2)}, u32[]{:S(2)}) collective-permute-start(bf16[2,64,128]{2,1,0:T(8,128)(2,1)S(1)} %get-tuple-element.71), channel_id=1, source_target_pairs={{0,17},{1,16},{2,19},{3,18},{4,21},{5,20},{6,23},{7,22},{8,25},{9,... | collective-permute-start | bytes 98312 | tf_op jit(solution)/shard_map/ppermute | solution.py:215
  26.2 0.0 collective-permute-done.8.refs_8_
  26.2 0.0 copy-done
  26.2 4.6 %scores.1 = (bf16[4,2304,256]{2,1,0:T(8,128)(2,1)S(1)}, f32[4,1,256]{2,1,0:T(1,128)S(1)}, f32[4,64,256]{2,1,0:T(8,128)S(1)}, bf16[3072,128]{1,0:T(8,128)(2,1)S(1...) custom-call(s32[8]{0:T(128)S(1)} %copy-done, bf16[1024,128]{1,0:T(8,128)(2,1)S(1)} %keys.1.refs_1_, ...), custom_call_target="tpu_custom_call" | custom-call | flops 8999999488 | tf_op jit(solution)/shard_map/scores/pallas_call | solution.py:39
  30.8 0.0 collective-permute-done.10.refs_2_
  30.8 0.0 collective-permute-done.11.refs_3_
  30.9 0.0 collective-permute-done.12.refs_4_
  30.9 1.9 %far.1 = (bf16[1024,128]{1,0:T(8,128)(2,1)S(1)}, f32[4,1,256]{2,1,0:T(1,128)S(1)}, f32[4,64,256]{2,1,0:T(8,128)S(1)}, bf16[1024,128]{1,0:T(8,128)(2,1)S(1)}) custom-call(bf16[4,64,128]{2,1,0:T(8,128)(2,1)S(1)} %get-tuple-element.67.keep_ref.refs_0_, bf16[4,64,128]{2,1,0:T(8,128)(2,1)S(1)} %collective-permute-done.9.got_ref.refs_1_, ...), custom_call_target="tpu_custom_call" | custom-call | flops 2000000000 | tf_op jit(solution)/shard_map/far/pallas_call | solution.py:39
  32.8 1.7 %collective-permute-start.14 = (bf16[1024,128]{1,0:T(8,128)(2,1)S(1)}, bf16[1024,128]{1,0:T(8,128)(2,1)S(1)}, u32[]{:S(2)}, u32[]{:S(2)}) collective-permute-start(bf16[1024,128]{1,0:T(8,128)(2,1)S(1)} %get-tuple-element.84), channel_id=1, source_target_pairs={{0,2},{1,3},{2,0},{3,1},{4,6},{5,7},{6,4},{7,5},{8,10},{9,11},{10,... | collective-permute-start | bytes 786440 | tf_op jit(solution)/shard_map/ppermute | solution.py:192
  34.5 1.6 %far_next.1 = (f32[4,64,256]{2,1,0:T(8,128)S(1)}, bf16[1024,128]{1,0:T(8,128)(2,1)S(1)}) custom-call(bf16[4,2304,256]{2,1,0:T(8,128)(2,1)S(1)} %get-tuple-element.65.refs_5_.refs_0_, f32[4,1,256]{2,1,0:T(1,128)S(1)} %get-tuple-element.66.refs_6_.refs_1_, bf16[3072,128]{1,0:T(8,128)(2,1)S(1)} %get-tuple-element.73.refs_8_.refs_2_.refs_3_, ...), custom_call_target="tpu_custom_call" | custom-call | flops 2000000000 | tf_op jit(solution)/shard_map/far_next/pallas_call | solution.py:39
  36.1 0.1 collective-permute-start.15
  36.2 2.4 %near.1 = (f32[1024,128]{1,0:T(8,128)S(1)}, bf16[256,128]{1,0:T(8,128)(2,1)S(1)}, bf16[256,128]{1,0:T(8,128)(2,1)S(1)}) custom-call(bf16[4,2304,256]{2,1,0:T(8,128)(2,1)S(1)} %get-tuple-element.65.refs_5_.refs_0_, f32[4,1,256]{2,1,0:T(1,128)S(1)} %get-tuple-element.66.refs_6_.refs_1_, f32[4,1,256]{2,1,0:T(1,128)S(1)} %get-tuple-element.76.refs_6_.refs_2_, ...), custom_call_target="tpu_custom_call" | custom-call | flops 4000000000 | tf_op jit(solution)/shard_map/near/pallas_call | solution.py:39
  38.6 0.0 collective-permute-done.6.got_ref.refs_1_
  38.7 0.3 collective-permute-start.13
  38.9 1.0 %collective-permute-done.14.refs_0_ = bf16[1024,128]{1,0:T(8,128)(2,1)S(1)} collective-permute-done((bf16[1024,128]{1,0:T(8,128)(2,1)S(1)}, bf16[1024,128]{1,0:T(8,128)(2,1)S(1)}, u32[]{:S(2)}, u32[]{:S(2)}) %collective-permute-start.14) | collective-permute-done | bytes 262176 | tf_op jit(solution)/shard_map/ppermute | solution.py:192
  40.0 0.0 collective-permute-done.15.refs_1_
  40.0 0.2 sum.1
  40.2 0.7 %collective-permute-start.16 = (bf16[768,128]{1,0:T(8,128)(2,1)S(1)}, bf16[768,128]{1,0:T(8,128)(2,1)S(1)}, u32[]{:S(2)}, u32[]{:S(2)}) collective-permute-start(bf16[768,128]{1,0:T(8,128)(2,1)S(1)} %get-tuple-element.87), channel_id=1, source_target_pairs={{0,1},{1,0},{2,3},{3,2},{4,5},{5,4},{6,7},{7,6},{8,9},{9,8},{10,11... | collective-permute-start | bytes 589832 | tf_op jit(solution)/shard_map/ppermute | solution.py:613
  40.9 3.7 %collective-permute-done.13.refs_2_ = bf16[2,128,256]{2,1,0:T(8,128)(2,1)S(1)} collective-permute-done((bf16[2,128,256]{2,1,0:T(8,128)(2,1)S(1)}, bf16[2,128,256]{2,1,0:T(8,128)(2,1)S(1)}, u32[]{:S(2)}, u32[]{:S(2)}) %collective-permute-start.13) | collective-permute-done | bytes 131104 | tf_op jit(solution)/shard_map/ppermute | solution.py:215
  44.6 0.7 %resid.1 = bf16[1,512,256]{2,1,0:T(8,128)(2,1)} custom-call(bf16[2,128,256]{2,1,0:T(8,128)(2,1)S(1)} %get-tuple-element.81.keep_ref.refs_0_, bf16[2,128,256]{2,1,0:T(8,128)(2,1)S(1)} %collective-permute-done.6.got_ref.refs_1_, bf16[2,128,256]{2,1,0:T(8,128)(2,1)S(1)} %collective-permute-done.13.refs_2_), custom_call_target="tpu_custom_call" | custom-call | flops 1000000000 | tf_op jit(solution)/shard_map/resid/pallas_call | solution.py:39
  45.3 0.9 %collective-permute-done.16.refs_1_ = bf16[768,128]{1,0:T(8,128)(2,1)S(1)} collective-permute-done((bf16[768,128]{1,0:T(8,128)(2,1)S(1)}, bf16[768,128]{1,0:T(8,128)(2,1)S(1)}, u32[]{:S(2)}, u32[]{:S(2)}) %collective-permute-start.16) | collective-permute-done | bytes 196640 | tf_op jit(solution)/shard_map/ppermute | solution.py:613
  46.3 0.9 %last.1 = (bf16[1,512,128]{2,1,0:T(8,128)(2,1)}, bf16[1,512,128]{2,1,0:T(8,128)(2,1)}, bf16[1,512,128]{2,1,0:T(8,128)(2,1)}) custom-call(bf16[512,128]{1,0:T(8,128)(2,1)S(1)} %get-tuple-element.86.refs_0_, bf16[768,128]{1,0:T(8,128)(2,1)S(1)} %collective-permute-done.16.refs_1_, bf16[256,128]{1,0:T(8,128)(2,1)S(1)} %get-tuple-element.88.refs_2_), custom_call_target="tpu_custom_call" | custom-call | tf_op jit(solution)/shard_map/last/pallas_call | solution.py:39
  (4 shorter events, 0.1 us)
Async XLA Ops:
  2.1 3.2 %collective-permute-start = (bf16[1152,128]{1,0:T(8,128)(2,1)S(1)}, bf16[1152,128]{1,0:T(8,128)(2,1)S(1)}, u32[]{:S(2)}, u32[]{:S(2)}) collective-permute-start(bf16[1152,128]{1,0:T(8,128)(2,1)S(1)} %get-tuple-element.50), channel_id=1, source_target_pairs={{0,8},{1,9},{2,10},{3,11},{4,12},{5,13},{6,14},{7,15},{8,0},{9,1},... | collective-permute-start | bytes 884744 | tf_op jit(solution)/shard_map/ppermute | solution.py:185
  2.6 6.9 %collective-permute-start.1 = (bf16[48,1024]{1,0:T(8,128)(2,1)S(1)}, bf16[48,1024]{1,0:T(8,128)(2,1)S(1)}, u32[]{:S(2)}, u32[]{:S(2)}) collective-permute-start(bf16[48,1024]{1,0:T(8,128)(2,1)S(1)} %get-tuple-element.51), channel_id=1, source_target_pairs={{0,1},{1,0},{2,3},{3,2},{4,5},{5,4},{6,7},{7,6},{8,16},{9,17},{10,... | collective-permute-start | bytes 294920 | tf_op jit(solution)/shard_map/ppermute | solution.py:250
  5.2 4.3 %collective-permute-start.2 = (bf16[48,1024]{1,0:T(8,128)(2,1)S(1)}, bf16[48,1024]{1,0:T(8,128)(2,1)S(1)}, u32[]{:S(2)}, u32[]{:S(2)}) collective-permute-start(bf16[48,1024]{1,0:T(8,128)(2,1)S(1)} %get-tuple-element.51), channel_id=1, source_target_pairs={{0,8},{1,24},{2,25},{3,26},{4,27},{5,28},{6,29},{7,30},{8,0},{9,16... | collective-permute-start | bytes 294920 | tf_op jit(solution)/shard_map/ppermute | solution.py:251
  5.3 7.1 %collective-permute-start.3 = (bf16[2,192,128]{2,1,0:T(8,128)(2,1)S(1)}, bf16[2,192,128]{2,1,0:T(8,128)(2,1)S(1)}, u32[]{:S(2)}, u32[]{:S(2)}) collective-permute-start(bf16[2,192,128]{2,1,0:T(8,128)(2,1)S(1)} %get-tuple-element.54), channel_id=1, source_target_pairs={{0,16},{1,17},{2,18},{3,19},{4,20},{5,21},{6,22},{7,23},{8,24},{9,... | collective-permute-start | bytes 294920 | tf_op jit(solution)/shard_map/ppermute | solution.py:215
  8.0 6.2 %collective-permute-start.4 = (bf16[2,192,128]{2,1,0:T(8,128)(2,1)S(1)}, bf16[2,192,128]{2,1,0:T(8,128)(2,1)S(1)}, u32[]{:S(2)}, u32[]{:S(2)}) collective-permute-start(bf16[2,192,128]{2,1,0:T(8,128)(2,1)S(1)} %get-tuple-element.55), channel_id=1, source_target_pairs={{0,1},{1,0},{2,3},{3,2},{4,5},{5,4},{6,7},{7,6},{8,9},{9,8},{10,11... | collective-permute-start | bytes 294920 | tf_op jit(solution)/shard_map/ppermute | solution.py:215
  9.5 5.5 %collective-permute-start.5 = (bf16[2,192,128]{2,1,0:T(8,128)(2,1)S(1)}, bf16[2,192,128]{2,1,0:T(8,128)(2,1)S(1)}, u32[]{:S(2)}, u32[]{:S(2)}) collective-permute-start(bf16[2,192,128]{2,1,0:T(8,128)(2,1)S(1)} %get-tuple-element.56), channel_id=1, source_target_pairs={{0,17},{1,16},{2,19},{3,18},{4,21},{5,20},{6,23},{7,22},{8,25},{9,... | collective-permute-start | bytes 294920 | tf_op jit(solution)/shard_map/ppermute | solution.py:215
  15.1 11.1 %copy-start = (s32[8]{0:T(128)S(1)}, s32[8]{0:T(128)}, u32[]{:S(2)}) copy-start(s32[8]{0:T(128)} %refs_0_.1) | copy-start | bytes 100
  15.1 9.5 %collective-permute-start.7 = (bf16[1024,128]{1,0:T(8,128)(2,1)S(1)}, bf16[1024,128]{1,0:T(8,128)(2,1)S(1)}, u32[]{:S(2)}, u32[]{:S(2)}) collective-permute-start(bf16[1024,128]{1,0:T(8,128)(2,1)S(1)} %keys.1.refs_1_), channel_id=1, source_target_pairs={{0,2},{1,3},{2,0},{3,1},{4,6},{5,7},{6,4},{7,5},{8,10},{9,11},{10,... | collective-permute-start | bytes 786440 | tf_op jit(solution)/shard_map/ppermute | solution.py:192
  18.1 8.1 %collective-permute-start.8 = (bf16[1024,128]{1,0:T(8,128)(2,1)S(1)}, bf16[1024,128]{1,0:T(8,128)(2,1)S(1)}, u32[]{:S(2)}, u32[]{:S(2)}) collective-permute-start(bf16[1024,128]{1,0:T(8,128)(2,1)S(1)} %keys.1.refs_1_), channel_id=1, source_target_pairs={{0,8},{1,9},{2,4},{3,5},{4,2},{5,3},{6,14},{7,15},{8,0},{9,1},{10,... | collective-permute-start | bytes 786440 | tf_op jit(solution)/shard_map/ppermute | solution.py:192
  19.9 1.5 %collective-permute-start.9 = (bf16[4,64,128]{2,1,0:T(8,128)(2,1)S(1)}, bf16[4,64,128]{2,1,0:T(8,128)(2,1)S(1)}, u32[]{:S(2)}, u32[]{:S(2)}) collective-permute-start(bf16[4,64,128]{2,1,0:T(8,128)(2,1)S(1)} %get-tuple-element.68), channel_id=1, source_target_pairs={{0,8},{1,9},{2,10},{3,11},{4,12},{5,13},{6,14},{7,15},{8,0},{9,1},... | collective-permute-start | bytes 196616 | tf_op jit(solution)/shard_map/ppermute | solution.py:185
  20.5 18.2 %collective-permute-start.6 = (bf16[2,128,256]{2,1,0:T(8,128)(2,1)S(1)}, bf16[2,128,256]{2,1,0:T(8,128)(2,1)S(1)}, u32[]{:S(2)}, u32[]{:S(2)}) collective-permute-start(bf16[2,128,256]{2,1,0:T(8,128)(2,1)S(1)} %get-tuple-element.64), channel_id=1, source_target_pairs={{0,8},{1,9},{2,10},{3,11},{4,12},{5,13},{6,14},{7,15},{8,0},{9,1},... | collective-permute-start | bytes 393224 | tf_op jit(solution)/shard_map/ppermute | solution.py:185
  21.4 9.5 %collective-permute-start.10 = (bf16[2,64,128]{2,1,0:T(8,128)(2,1)S(1)}, bf16[2,64,128]{2,1,0:T(8,128)(2,1)S(1)}, u32[]{:S(2)}, u32[]{:S(2)}) collective-permute-start(bf16[2,64,128]{2,1,0:T(8,128)(2,1)S(1)} %get-tuple-element.69), channel_id=1, source_target_pairs={{0,16},{1,17},{2,18},{3,19},{4,20},{5,21},{6,22},{7,23},{8,24},{9,... | collective-permute-start | bytes 98312 | tf_op jit(solution)/shard_map/ppermute | solution.py:215
  21.5 9.3 %collective-permute-start.11 = (bf16[2,64,128]{2,1,0:T(8,128)(2,1)S(1)}, bf16[2,64,128]{2,1,0:T(8,128)(2,1)S(1)}, u32[]{:S(2)}, u32[]{:S(2)}) collective-permute-start(bf16[2,64,128]{2,1,0:T(8,128)(2,1)S(1)} %get-tuple-element.70), channel_id=1, source_target_pairs={{0,1},{1,0},{2,3},{3,2},{4,5},{5,4},{6,7},{7,6},{8,9},{9,8},{10,11... | collective-permute-start | bytes 98312 | tf_op jit(solution)/shard_map/ppermute | solution.py:215
  24.5 6.3 %collective-permute-start.12 = (bf16[2,64,128]{2,1,0:T(8,128)(2,1)S(1)}, bf16[2,64,128]{2,1,0:T(8,128)(2,1)S(1)}, u32[]{:S(2)}, u32[]{:S(2)}) collective-permute-start(bf16[2,64,128]{2,1,0:T(8,128)(2,1)S(1)} %get-tuple-element.71), channel_id=1, source_target_pairs={{0,17},{1,16},{2,19},{3,18},{4,21},{5,20},{6,23},{7,22},{8,25},{9,... | collective-permute-start | bytes 98312 | tf_op jit(solution)/shard_map/ppermute | solution.py:215
  32.8 7.2 %collective-permute-start.14 = (bf16[1024,128]{1,0:T(8,128)(2,1)S(1)}, bf16[1024,128]{1,0:T(8,128)(2,1)S(1)}, u32[]{:S(2)}, u32[]{:S(2)}) collective-permute-start(bf16[1024,128]{1,0:T(8,128)(2,1)S(1)} %get-tuple-element.84), channel_id=1, source_target_pairs={{0,2},{1,3},{2,0},{3,1},{4,6},{5,7},{6,4},{7,5},{8,10},{9,11},{10,... | collective-permute-start | bytes 786440 | tf_op jit(solution)/shard_map/ppermute | solution.py:192
  36.1 3.9 %collective-permute-start.15 = (bf16[1024,128]{1,0:T(8,128)(2,1)S(1)}, bf16[1024,128]{1,0:T(8,128)(2,1)S(1)}, u32[]{:S(2)}, u32[]{:S(2)}) collective-permute-start(bf16[1024,128]{1,0:T(8,128)(2,1)S(1)} %get-tuple-element.85), channel_id=1, source_target_pairs={{0,8},{1,9},{2,4},{3,5},{4,2},{5,3},{6,14},{7,15},{8,0},{9,1},{10,... | collective-permute-start | bytes 786440 | tf_op jit(solution)/shard_map/ppermute | solution.py:192
  38.7 6.0 %collective-permute-start.13 = (bf16[2,128,256]{2,1,0:T(8,128)(2,1)S(1)}, bf16[2,128,256]{2,1,0:T(8,128)(2,1)S(1)}, u32[]{:S(2)}, u32[]{:S(2)}) collective-permute-start(bf16[2,128,256]{2,1,0:T(8,128)(2,1)S(1)} %regroup_resid.1), channel_id=1, source_target_pairs={{0,16},{1,17},{2,18},{3,19},{4,20},{5,21},{6,22},{7,23},{8,24},{9,... | collective-permute-start | bytes 393224 | tf_op jit(solution)/shard_map/ppermute | solution.py:215
  40.2 6.1 %collective-permute-start.16 = (bf16[768,128]{1,0:T(8,128)(2,1)S(1)}, bf16[768,128]{1,0:T(8,128)(2,1)S(1)}, u32[]{:S(2)}, u32[]{:S(2)}) collective-permute-start(bf16[768,128]{1,0:T(8,128)(2,1)S(1)} %get-tuple-element.87), channel_id=1, source_target_pairs={{0,1},{1,0},{2,3},{3,2},{4,5},{5,4},{6,7},{7,6},{8,9},{9,8},{10,11... | collective-permute-start | bytes 589832 | tf_op jit(solution)/shard_map/ppermute | solution.py:613

commit v7 on v6

--- a/solution.py
+++ b/solution.py
@@ -239,8 +239,18 @@
                 outer[0, ctx + 1] = (h, ctx)
             elif 0 < h < last_head or (h, ctx) in ((0, 0), (last_head, ctx_count - 1)):
                 idle.append((h, ctx))
-    for one, two in zip(idle[::2], idle[1::2]):
+    def pair(one, two):
         outer[one], outer[two] = two, one
+
+    pair((0, 0), (1, 0))
+    pair((last_head, ctx_count - 1), (last_head - 1, ctx_count - 1))
+    for h, ctx in idle:
+        other = (h, ctx ^ group)
+        if (h, ctx) not in outer and other in idle and other not in outer:
+            pair((h, ctx), other)
+    rest = [place for place in idle if place not in outer]
+    for one, two in zip(rest[::2], rest[1::2]):
+        pair(one, two)
 
     def outside(h, z, y):
         head, ctx = outer[h, z * group + y]
@@ -297,7 +307,7 @@
             low_ref[:, lane] = out.astype(BF16)
             return carry
 
-        lax.fori_loop(start, stop, chunk, 0)
+        lax.fori_loop(start, stop, chunk, 0, unroll=2)
 
     def conv_first(*refs):
         conv_chunks(0, part_chunks, *refs)

time: 47.6 us -> 47.5 us (level)
  waiting for transfers between devices: 10.2 us -> 11.4 us
  starting transfers between devices: 17.6 us -> 16.5 us
    ppermute x7, starting transfers between devices: 8.29 us -> 6.35 us  [exchange(): lax.ppermute(part, mesh_axes, everyone(target(m)))]
    ppermute x4, waiting for transfers between devices: 2.06 us -> 3.26 us  [step(): return lax.ppermute(x, mesh_axes, everyone(target))]
    ppermute x7, waiting for transfers between devices: 6.37 us -> 5.57 us  [exchange(): lax.ppermute(part, mesh_axes, everyone(target(m)))]
    ppermute x1, waiting for transfers between devices: 0.95 us -> 1.72 us  [y_swap(): return lax.ppermute(x, mesh_axes, everyone(lambda h, z, y: (h, z, 1 - y)))]
    ppermute x1, starting transfers between devices: 0.71 us -> 1.26 us  [y_swap(): return lax.ppermute(x, mesh_axes, everyone(lambda h, z, y: (h, z, 1 - y)))]
where the time goes in v7:
time: 47.5 us; the launch traced here: 47.1 us
  Pallas kernels  18.5 us (39%)
  starting transfers between devices  16.5 us (35%)
  waiting for transfers between devices  11.4 us (24%)
  between operations  0.79 us (2%)
    pallas_call x13, Pallas kernels, run(): pl.pallas_call(body, out_shape=outs, in_specs=[pl.BlockSpec(memory_space=...  17 us
    ppermute x7, starting transfers between devices, exchange(): lax.ppermute(part, mesh_axes, everyone(target(m)))  6.35 us
    ppermute x7, waiting for transfers between devices, exchange(): lax.ppermute(part, mesh_axes, everyone(target(m)))  5.57 us
    ppermute x4, starting transfers between devices, step(): return lax.ppermute(x, mesh_axes, everyone(target))  5.01 us
    ppermute x4, waiting for transfers between devices, step(): return lax.ppermute(x, mesh_axes, everyone(target))  3.26 us
    ppermute x1, starting transfers between devices, on_device(): lax.ppermute(second, mesh_axes, everyone(inside))  2.59 us
    ppermute x1, waiting for transfers between devices, y_swap(): return lax.ppermute(x, mesh_axes, everyone(lambda h, z, y: (h, z, 1 - y)))  1.72 us
    pallas_call x1, Pallas kernels, on_device(): pl.pallas_call(pack_body, out_shape=pack_outs, in_specs=[raw] * 6, out_sp...  1.47 us
  transfers between devices with their start and end apart: 17, of which 7 were waited for; matrix products, arithmetic and copies ran while one was open for 0% of the time, Pallas kernels for 34%

profile of v7, /device:TPU:0, one launch (start us, length us, event | category | flops | bytes accessed | tf_op | source)
XLA Modules:
  0.0 47.1 jit_solution(6488005860339591524)
XLA Ops:
  0.6 1.5 %pack.1 = (bf16[4,192,128]{2,1,0:T(8,128)(2,1)S(1)}, bf16[1152,128]{1,0:T(8,128)(2,1)S(1)}, bf16[48,1024]{1,0:T(8,128)(2,1)S(1)}, bf16[1,128,1024]{2,1,0:T(8,128...) custom-call(bf16[1,128,512]{2,1,0:T(8,128)(2,1)} %q_hbm.1, bf16[1,128,512]{2,1,0:T(8,128)(2,1)} %k_hbm.1, ...), custom_call_target="tpu_custom_call" | custom-call | tf_op jit(solution)/shard_map/pack/pallas_call | solution.py:161
  2.1 0.5 %collective-permute-start = (bf16[1152,128]{1,0:T(8,128)(2,1)S(1)}, bf16[1152,128]{1,0:T(8,128)(2,1)S(1)}, u32[]{:S(2)}, u32[]{:S(2)}) collective-permute-start(bf16[1152,128]{1,0:T(8,128)(2,1)S(1)} %get-tuple-element.50), channel_id=1, source_target_pairs={{0,8},{1,9},{2,10},{3,11},{4,12},{5,13},{6,14},{7,15},{8,0},{9,1},... | collective-permute-start | bytes 884744 | tf_op jit(solution)/shard_map/ppermute | solution.py:185
  2.6 2.6 %collective-permute-start.1 = (bf16[48,1024]{1,0:T(8,128)(2,1)S(1)}, bf16[48,1024]{1,0:T(8,128)(2,1)S(1)}, u32[]{:S(2)}, u32[]{:S(2)}) collective-permute-start(bf16[48,1024]{1,0:T(8,128)(2,1)S(1)} %get-tuple-element.51), channel_id=1, source_target_pairs={{0,1},{1,0},{2,3},{3,2},{4,5},{5,4},{6,7},{7,6},{8,16},{9,17},{10,... | collective-permute-start | bytes 294920 | tf_op jit(solution)/shard_map/ppermute | solution.py:260
  5.2 0.1 collective-permute-start.2
  5.3 0.0 collective-permute-done.refs_2_.got_ref.refs_3_
  5.3 2.1 %collective-permute-start.3 = (bf16[2,192,128]{2,1,0:T(8,128)(2,1)S(1)}, bf16[2,192,128]{2,1,0:T(8,128)(2,1)S(1)}, u32[]{:S(2)}, u32[]{:S(2)}) collective-permute-start(bf16[2,192,128]{2,1,0:T(8,128)(2,1)S(1)} %get-tuple-element.54), channel_id=1, source_target_pairs={{0,16},{1,17},{2,18},{3,19},{4,20},{5,21},{6,22},{7,23},{8,24},{9,... | collective-permute-start | bytes 294920 | tf_op jit(solution)/shard_map/ppermute | solution.py:215
  7.4 1.5 %collective-permute-start.4 = (bf16[2,192,128]{2,1,0:T(8,128)(2,1)S(1)}, bf16[2,192,128]{2,1,0:T(8,128)(2,1)S(1)}, u32[]{:S(2)}, u32[]{:S(2)}) collective-permute-start(bf16[2,192,128]{2,1,0:T(8,128)(2,1)S(1)} %get-tuple-element.55), channel_id=1, source_target_pairs={{0,1},{1,0},{2,3},{3,2},{4,5},{5,4},{6,7},{7,6},{8,9},{9,8},{10,11... | collective-permute-start | bytes 294920 | tf_op jit(solution)/shard_map/ppermute | solution.py:215
  9.0 0.5 %collective-permute-start.5 = (bf16[2,192,128]{2,1,0:T(8,128)(2,1)S(1)}, bf16[2,192,128]{2,1,0:T(8,128)(2,1)S(1)}, u32[]{:S(2)}, u32[]{:S(2)}) collective-permute-start(bf16[2,192,128]{2,1,0:T(8,128)(2,1)S(1)} %get-tuple-element.56), channel_id=1, source_target_pairs={{0,17},{1,16},{2,19},{3,18},{4,21},{5,20},{6,23},{7,22},{8,25},{9,... | collective-permute-start | bytes 294920 | tf_op jit(solution)/shard_map/ppermute | solution.py:215
  9.5 0.0 collective-permute-done.1.refs_3_
  9.5 0.0 collective-permute-done.2.refs_4_
  9.5 2.7 %conv.1.refs_6_ = bf16[128,768]{1,0:T(8,128)(2,1)S(1)} custom-call(bf16[1,128,1024]{2,1,0:T(8,128)(2,1)S(1)} %get-tuple-element.48.refs_0_, bf16[1,128,1024]{2,1,0:T(8,128)(2,1)S(1)} %get-tuple-element.49.refs_1_, bf16[1152,128]{1,0:T(8,128)(2,1)S(1)} %collective-permute-done.refs_2_.got_ref.refs_3_, bf16[48,1024]{1,0:T(8,128)(2,1)S(1)} %collective-permute-done.1.refs_3_, ...), custom_call_target="tpu_custom_call" | custom-call | flops 3000000000 | tf_op jit(solution)/shard_map/conv/pallas_call | solution.py:39
  12.2 0.0 collective-permute-done.3.refs_0_.refs_4_
  12.3 1.7 %collective-permute-done.4.refs_1_.refs_5_ = bf16[2,192,128]{2,1,0:T(8,128)(2,1)S(1)} collective-permute-done((bf16[2,192,128]{2,1,0:T(8,128)(2,1)S(1)}, bf16[2,192,128]{2,1,0:T(8,128)(2,1)S(1)}, u32[]{:S(2)}, u32[]{:S(2)}) %collective-permute-start.4) | collective-permute-done | bytes 98336 | tf_op jit(solution)/shard_map/ppermute | solution.py:215
  14.0 1.0 %collective-permute-done.5.refs_2_.refs_6_ = bf16[2,192,128]{2,1,0:T(8,128)(2,1)S(1)} collective-permute-done((bf16[2,192,128]{2,1,0:T(8,128)(2,1)S(1)}, bf16[2,192,128]{2,1,0:T(8,128)(2,1)S(1)}, u32[]{:S(2)}, u32[]{:S(2)}) %collective-permute-start.5) | collective-permute-done | bytes 98336 | tf_op jit(solution)/shard_map/ppermute | solution.py:215
  15.0 0.0 copy-start
  15.0 3.2 %collective-permute-start.7 = (bf16[1024,128]{1,0:T(8,128)(2,1)S(1)}, bf16[1024,128]{1,0:T(8,128)(2,1)S(1)}, u32[]{:S(2)}, u32[]{:S(2)}) collective-permute-start(bf16[1024,128]{1,0:T(8,128)(2,1)S(1)} %keys.1.refs_1_), channel_id=1, source_target_pairs={{0,2},{1,3},{2,0},{3,1},{4,6},{5,7},{6,4},{7,5},{8,10},{9,11},{10,... | collective-permute-start | bytes 786440 | tf_op jit(solution)/shard_map/ppermute | solution.py:192
  18.2 0.0 collective-permute-start.8
  18.2 1.8 %conv_last.1 = (bf16[4,64,128]{2,1,0:T(8,128)(2,1)S(1)}, bf16[4,64,128]{2,1,0:T(8,128)(2,1)S(1)}, bf16[2,128,256]{2,1,0:T(8,128)(2,1)S(1)}, bf16[2,128,256]{2,1,0:T(8,128)(2,1)S(1)}) custom-call(bf16[1,128,1024]{2,1,0:T(8,128)(2,1)S(1)} %get-tuple-element.48.refs_0_, bf16[1,128,1024]{2,1,0:T(8,128)(2,1)S(1)} %get-tuple-element.49.refs_1_, ...), custom_call_target="tpu_custom_call" | custom-call | flops 3000000000 | tf_op jit(solution)/shard_map/conv_last/pallas_call | solution.py:39
  20.1 0.6 %collective-permute-start.9 = (bf16[4,64,128]{2,1,0:T(8,128)(2,1)S(1)}, bf16[4,64,128]{2,1,0:T(8,128)(2,1)S(1)}, u32[]{:S(2)}, u32[]{:S(2)}) collective-permute-start(bf16[4,64,128]{2,1,0:T(8,128)(2,1)S(1)} %get-tuple-element.68), channel_id=1, source_target_pairs={{0,8},{1,9},{2,10},{3,11},{4,12},{5,13},{6,14},{7,15},{8,0},{9,1},... | collective-permute-start | bytes 196616 | tf_op jit(solution)/shard_map/ppermute | solution.py:185
  20.6 0.1 collective-permute-start.6
  20.7 0.8 %collective-permute-done.9.got_ref.refs_1_ = bf16[4,64,128]{2,1,0:T(8,128)(2,1)S(1)} collective-permute-done((bf16[4,64,128]{2,1,0:T(8,128)(2,1)S(1)}, bf16[4,64,128]{2,1,0:T(8,128)(2,1)S(1)}, u32[]{:S(2)}, u32[]{:S(2)}) %collective-permute-start.9) | collective-permute-done | bytes 65568 | tf_op jit(solution)/shard_map/ppermute | solution.py:185
  21.5 0.0 collective-permute-start.10
  21.6 1.2 %collective-permute-start.11 = (bf16[2,64,128]{2,1,0:T(8,128)(2,1)S(1)}, bf16[2,64,128]{2,1,0:T(8,128)(2,1)S(1)}, u32[]{:S(2)}, u32[]{:S(2)}) collective-permute-start(bf16[2,64,128]{2,1,0:T(8,128)(2,1)S(1)} %get-tuple-element.70), channel_id=1, source_target_pairs={{0,1},{1,0},{2,3},{3,2},{4,5},{5,4},{6,7},{7,6},{8,9},{9,8},{10,11... | collective-permute-start | bytes 98312 | tf_op jit(solution)/shard_map/ppermute | solution.py:215
  22.7 1.9 %collective-permute-done.7.refs_7_ = bf16[1024,128]{1,0:T(8,128)(2,1)S(1)} collective-permute-done((bf16[1024,128]{1,0:T(8,128)(2,1)S(1)}, bf16[1024,128]{1,0:T(8,128)(2,1)S(1)}, u32[]{:S(2)}, u32[]{:S(2)}) %collective-permute-start.7) | collective-permute-done | bytes 262176 | tf_op jit(solution)/shard_map/ppermute | solution.py:192
  24.6 0.7 %collective-permute-start.12 = (bf16[2,64,128]{2,1,0:T(8,128)(2,1)S(1)}, bf16[2,64,128]{2,1,0:T(8,128)(2,1)S(1)}, u32[]{:S(2)}, u32[]{:S(2)}) collective-permute-start(bf16[2,64,128]{2,1,0:T(8,128)(2,1)S(1)} %get-tuple-element.71), channel_id=1, source_target_pairs={{0,17},{1,16},{2,19},{3,18},{4,21},{5,20},{6,23},{7,22},{8,25},{9,... | collective-permute-start | bytes 98312 | tf_op jit(solution)/shard_map/ppermute | solution.py:215
  25.3 0.0 collective-permute-done.8.refs_8_
  25.3 0.0 copy-done
  25.3 4.6 %scores.1 = (bf16[4,2304,256]{2,1,0:T(8,128)(2,1)S(1)}, f32[4,1,256]{2,1,0:T(1,128)S(1)}, f32[4,64,256]{2,1,0:T(8,128)S(1)}, bf16[3072,128]{1,0:T(8,128)(2,1)S(1...) custom-call(s32[8]{0:T(128)S(1)} %copy-done, bf16[1024,128]{1,0:T(8,128)(2,1)S(1)} %keys.1.refs_1_, ...), custom_call_target="tpu_custom_call" | custom-call | flops 8999999488 | tf_op jit(solution)/shard_map/scores/pallas_call | solution.py:39
  29.9 0.0 collective-permute-done.10.refs_2_
  30.0 0.0 collective-permute-done.11.refs_3_
  30.0 0.0 collective-permute-done.12.refs_4_
  30.0 1.9 %far.1 = (bf16[1024,128]{1,0:T(8,128)(2,1)S(1)}, f32[4,1,256]{2,1,0:T(1,128)S(1)}, f32[4,64,256]{2,1,0:T(8,128)S(1)}, bf16[1024,128]{1,0:T(8,128)(2,1)S(1)}) custom-call(bf16[4,64,128]{2,1,0:T(8,128)(2,1)S(1)} %get-tuple-element.67.keep_ref.refs_0_, bf16[4,64,128]{2,1,0:T(8,128)(2,1)S(1)} %collective-permute-done.9.got_ref.refs_1_, ...), custom_call_target="tpu_custom_call" | custom-call | flops 2000000000 | tf_op jit(solution)/shard_map/far/pallas_call | solution.py:39
  31.9 1.8 %collective-permute-start.14 = (bf16[1024,128]{1,0:T(8,128)(2,1)S(1)}, bf16[1024,128]{1,0:T(8,128)(2,1)S(1)}, u32[]{:S(2)}, u32[]{:S(2)}) collective-permute-start(bf16[1024,128]{1,0:T(8,128)(2,1)S(1)} %get-tuple-element.84), channel_id=1, source_target_pairs={{0,2},{1,3},{2,0},{3,1},{4,6},{5,7},{6,4},{7,5},{8,10},{9,11},{10,... | collective-permute-start | bytes 786440 | tf_op jit(solution)/shard_map/ppermute | solution.py:192
  33.7 1.6 %far_next.1 = (f32[4,64,256]{2,1,0:T(8,128)S(1)}, bf16[1024,128]{1,0:T(8,128)(2,1)S(1)}) custom-call(bf16[4,2304,256]{2,1,0:T(8,128)(2,1)S(1)} %get-tuple-element.65.refs_5_.refs_0_, f32[4,1,256]{2,1,0:T(1,128)S(1)} %get-tuple-element.66.refs_6_.refs_1_, bf16[3072,128]{1,0:T(8,128)(2,1)S(1)} %get-tuple-element.73.refs_8_.refs_2_.refs_3_, ...), custom_call_target="tpu_custom_call" | custom-call | flops 2000000000 | tf_op jit(solution)/shard_map/far_next/pallas_call | solution.py:39
  35.3 0.1 collective-permute-start.15
  35.4 2.4 %near.1 = (f32[1024,128]{1,0:T(8,128)S(1)}, bf16[256,128]{1,0:T(8,128)(2,1)S(1)}, bf16[256,128]{1,0:T(8,128)(2,1)S(1)}) custom-call(bf16[4,2304,256]{2,1,0:T(8,128)(2,1)S(1)} %get-tuple-element.65.refs_5_.refs_0_, f32[4,1,256]{2,1,0:T(1,128)S(1)} %get-tuple-element.66.refs_6_.refs_1_, f32[4,1,256]{2,1,0:T(1,128)S(1)} %get-tuple-element.76.refs_6_.refs_2_, ...), custom_call_target="tpu_custom_call" | custom-call | flops 4000000000 | tf_op jit(solution)/shard_map/near/pallas_call | solution.py:39
  37.8 0.0 collective-permute-done.6.got_ref.refs_1_
  37.8 0.3 collective-permute-start.13
  38.2 1.4 %collective-permute-done.14.refs_0_ = bf16[1024,128]{1,0:T(8,128)(2,1)S(1)} collective-permute-done((bf16[1024,128]{1,0:T(8,128)(2,1)S(1)}, bf16[1024,128]{1,0:T(8,128)(2,1)S(1)}, u32[]{:S(2)}, u32[]{:S(2)}) %collective-permute-start.14) | collective-permute-done | bytes 262176 | tf_op jit(solution)/shard_map/ppermute | solution.py:192
  39.5 0.0 collective-permute-done.15.refs_1_
  39.5 0.2 sum.1
  39.7 1.3 %collective-permute-start.16 = (bf16[768,128]{1,0:T(8,128)(2,1)S(1)}, bf16[768,128]{1,0:T(8,128)(2,1)S(1)}, u32[]{:S(2)}, u32[]{:S(2)}) collective-permute-start(bf16[768,128]{1,0:T(8,128)(2,1)S(1)} %get-tuple-element.87), channel_id=1, source_target_pairs={{0,1},{1,0},{2,3},{3,2},{4,5},{5,4},{6,7},{7,6},{8,9},{9,8},{10,11... | collective-permute-start | bytes 589832 | tf_op jit(solution)/shard_map/ppermute | solution.py:623
  41.0 2.8 %collective-permute-done.13.refs_2_ = bf16[2,128,256]{2,1,0:T(8,128)(2,1)S(1)} collective-permute-done((bf16[2,128,256]{2,1,0:T(8,128)(2,1)S(1)}, bf16[2,128,256]{2,1,0:T(8,128)(2,1)S(1)}, u32[]{:S(2)}, u32[]{:S(2)}) %collective-permute-start.13) | collective-permute-done | bytes 131104 | tf_op jit(solution)/shard_map/ppermute | solution.py:215
  43.8 0.7 %resid.1 = bf16[1,512,256]{2,1,0:T(8,128)(2,1)} custom-call(bf16[2,128,256]{2,1,0:T(8,128)(2,1)S(1)} %get-tuple-element.81.keep_ref.refs_0_, bf16[2,128,256]{2,1,0:T(8,128)(2,1)S(1)} %collective-permute-done.6.got_ref.refs_1_, bf16[2,128,256]{2,1,0:T(8,128)(2,1)S(1)} %collective-permute-done.13.refs_2_), custom_call_target="tpu_custom_call" | custom-call | flops 1000000000 | tf_op jit(solution)/shard_map/resid/pallas_call | solution.py:39
  44.5 1.7 %collective-permute-done.16.refs_1_ = bf16[768,128]{1,0:T(8,128)(2,1)S(1)} collective-permute-done((bf16[768,128]{1,0:T(8,128)(2,1)S(1)}, bf16[768,128]{1,0:T(8,128)(2,1)S(1)}, u32[]{:S(2)}, u32[]{:S(2)}) %collective-permute-start.16) | collective-permute-done | bytes 196640 | tf_op jit(solution)/shard_map/ppermute | solution.py:623
  46.2 0.9 %last.1 = (bf16[1,512,128]{2,1,0:T(8,128)(2,1)}, bf16[1,512,128]{2,1,0:T(8,128)(2,1)}, bf16[1,512,128]{2,1,0:T(8,128)(2,1)}) custom-call(bf16[512,128]{1,0:T(8,128)(2,1)S(1)} %get-tuple-element.86.refs_0_, bf16[768,128]{1,0:T(8,128)(2,1)S(1)} %collective-permute-done.16.refs_1_, bf16[256,128]{1,0:T(8,128)(2,1)S(1)} %get-tuple-element.88.refs_2_), custom_call_target="tpu_custom_call" | custom-call | tf_op jit(solution)/shard_map/last/pallas_call | solution.py:39
  (4 shorter events, 0.1 us)
Async XLA Ops:
  2.1 3.2 %collective-permute-start = (bf16[1152,128]{1,0:T(8,128)(2,1)S(1)}, bf16[1152,128]{1,0:T(8,128)(2,1)S(1)}, u32[]{:S(2)}, u32[]{:S(2)}) collective-permute-start(bf16[1152,128]{1,0:T(8,128)(2,1)S(1)} %get-tuple-element.50), channel_id=1, source_target_pairs={{0,8},{1,9},{2,10},{3,11},{4,12},{5,13},{6,14},{7,15},{8,0},{9,1},... | collective-permute-start | bytes 884744 | tf_op jit(solution)/shard_map/ppermute | solution.py:185
  2.6 6.9 %collective-permute-start.1 = (bf16[48,1024]{1,0:T(8,128)(2,1)S(1)}, bf16[48,1024]{1,0:T(8,128)(2,1)S(1)}, u32[]{:S(2)}, u32[]{:S(2)}) collective-permute-start(bf16[48,1024]{1,0:T(8,128)(2,1)S(1)} %get-tuple-element.51), channel_id=1, source_target_pairs={{0,1},{1,0},{2,3},{3,2},{4,5},{5,4},{6,7},{7,6},{8,16},{9,17},{10,... | collective-permute-start | bytes 294920 | tf_op jit(solution)/shard_map/ppermute | solution.py:260
  5.2 4.3 %collective-permute-start.2 = (bf16[48,1024]{1,0:T(8,128)(2,1)S(1)}, bf16[48,1024]{1,0:T(8,128)(2,1)S(1)}, u32[]{:S(2)}, u32[]{:S(2)}) collective-permute-start(bf16[48,1024]{1,0:T(8,128)(2,1)S(1)} %get-tuple-element.51), channel_id=1, source_target_pairs={{0,8},{1,24},{2,25},{3,26},{4,27},{5,28},{6,29},{7,30},{8,0},{9,11... | collective-permute-start | bytes 294920 | tf_op jit(solution)/shard_map/ppermute | solution.py:261
  5.3 6.9 %collective-permute-start.3 = (bf16[2,192,128]{2,1,0:T(8,128)(2,1)S(1)}, bf16[2,192,128]{2,1,0:T(8,128)(2,1)S(1)}, u32[]{:S(2)}, u32[]{:S(2)}) collective-permute-start(bf16[2,192,128]{2,1,0:T(8,128)(2,1)S(1)} %get-tuple-element.54), channel_id=1, source_target_pairs={{0,16},{1,17},{2,18},{3,19},{4,20},{5,21},{6,22},{7,23},{8,24},{9,... | collective-permute-start | bytes 294920 | tf_op jit(solution)/shard_map/ppermute | solution.py:215
  7.4 6.5 %collective-permute-start.4 = (bf16[2,192,128]{2,1,0:T(8,128)(2,1)S(1)}, bf16[2,192,128]{2,1,0:T(8,128)(2,1)S(1)}, u32[]{:S(2)}, u32[]{:S(2)}) collective-permute-start(bf16[2,192,128]{2,1,0:T(8,128)(2,1)S(1)} %get-tuple-element.55), channel_id=1, source_target_pairs={{0,1},{1,0},{2,3},{3,2},{4,5},{5,4},{6,7},{7,6},{8,9},{9,8},{10,11... | collective-permute-start | bytes 294920 | tf_op jit(solution)/shard_map/ppermute | solution.py:215
  9.0 6.0 %collective-permute-start.5 = (bf16[2,192,128]{2,1,0:T(8,128)(2,1)S(1)}, bf16[2,192,128]{2,1,0:T(8,128)(2,1)S(1)}, u32[]{:S(2)}, u32[]{:S(2)}) collective-permute-start(bf16[2,192,128]{2,1,0:T(8,128)(2,1)S(1)} %get-tuple-element.56), channel_id=1, source_target_pairs={{0,17},{1,16},{2,19},{3,18},{4,21},{5,20},{6,23},{7,22},{8,25},{9,... | collective-permute-start | bytes 294920 | tf_op jit(solution)/shard_map/ppermute | solution.py:215
  15.0 10.3 %copy-start = (s32[8]{0:T(128)S(1)}, s32[8]{0:T(128)}, u32[]{:S(2)}) copy-start(s32[8]{0:T(128)} %refs_0_.1) | copy-start | bytes 100
  15.0 9.6 %collective-permute-start.7 = (bf16[1024,128]{1,0:T(8,128)(2,1)S(1)}, bf16[1024,128]{1,0:T(8,128)(2,1)S(1)}, u32[]{:S(2)}, u32[]{:S(2)}) collective-permute-start(bf16[1024,128]{1,0:T(8,128)(2,1)S(1)} %keys.1.refs_1_), channel_id=1, source_target_pairs={{0,2},{1,3},{2,0},{3,1},{4,6},{5,7},{6,4},{7,5},{8,10},{9,11},{10,... | collective-permute-start | bytes 786440 | tf_op jit(solution)/shard_map/ppermute | solution.py:192
  18.2 7.1 %collective-permute-start.8 = (bf16[1024,128]{1,0:T(8,128)(2,1)S(1)}, bf16[1024,128]{1,0:T(8,128)(2,1)S(1)}, u32[]{:S(2)}, u32[]{:S(2)}) collective-permute-start(bf16[1024,128]{1,0:T(8,128)(2,1)S(1)} %keys.1.refs_1_), channel_id=1, source_target_pairs={{0,8},{1,9},{2,4},{3,5},{4,2},{5,3},{6,14},{7,15},{8,0},{9,1},{10,... | collective-permute-start | bytes 786440 | tf_op jit(solution)/shard_map/ppermute | solution.py:192
  20.1 1.5 %collective-permute-start.9 = (bf16[4,64,128]{2,1,0:T(8,128)(2,1)S(1)}, bf16[4,64,128]{2,1,0:T(8,128)(2,1)S(1)}, u32[]{:S(2)}, u32[]{:S(2)}) collective-permute-start(bf16[4,64,128]{2,1,0:T(8,128)(2,1)S(1)} %get-tuple-element.68), channel_id=1, source_target_pairs={{0,8},{1,9},{2,10},{3,11},{4,12},{5,13},{6,14},{7,15},{8,0},{9,1},... | collective-permute-start | bytes 196616 | tf_op jit(solution)/shard_map/ppermute | solution.py:185
  20.6 17.2 %collective-permute-start.6 = (bf16[2,128,256]{2,1,0:T(8,128)(2,1)S(1)}, bf16[2,128,256]{2,1,0:T(8,128)(2,1)S(1)}, u32[]{:S(2)}, u32[]{:S(2)}) collective-permute-start(bf16[2,128,256]{2,1,0:T(8,128)(2,1)S(1)} %get-tuple-element.64), channel_id=1, source_target_pairs={{0,8},{1,9},{2,10},{3,11},{4,12},{5,13},{6,14},{7,15},{8,0},{9,1},... | collective-permute-start | bytes 393224 | tf_op jit(solution)/shard_map/ppermute | solution.py:185
  21.5 8.4 %collective-permute-start.10 = (bf16[2,64,128]{2,1,0:T(8,128)(2,1)S(1)}, bf16[2,64,128]{2,1,0:T(8,128)(2,1)S(1)}, u32[]{:S(2)}, u32[]{:S(2)}) collective-permute-start(bf16[2,64,128]{2,1,0:T(8,128)(2,1)S(1)} %get-tuple-element.69), channel_id=1, source_target_pairs={{0,16},{1,17},{2,18},{3,19},{4,20},{5,21},{6,22},{7,23},{8,24},{9,... | collective-permute-start | bytes 98312 | tf_op jit(solution)/shard_map/ppermute | solution.py:215
  21.6 8.4 %collective-permute-start.11 = (bf16[2,64,128]{2,1,0:T(8,128)(2,1)S(1)}, bf16[2,64,128]{2,1,0:T(8,128)(2,1)S(1)}, u32[]{:S(2)}, u32[]{:S(2)}) collective-permute-start(bf16[2,64,128]{2,1,0:T(8,128)(2,1)S(1)} %get-tuple-element.70), channel_id=1, source_target_pairs={{0,1},{1,0},{2,3},{3,2},{4,5},{5,4},{6,7},{7,6},{8,9},{9,8},{10,11... | collective-permute-start | bytes 98312 | tf_op jit(solution)/shard_map/ppermute | solution.py:215
  24.6 5.3 %collective-permute-start.12 = (bf16[2,64,128]{2,1,0:T(8,128)(2,1)S(1)}, bf16[2,64,128]{2,1,0:T(8,128)(2,1)S(1)}, u32[]{:S(2)}, u32[]{:S(2)}) collective-permute-start(bf16[2,64,128]{2,1,0:T(8,128)(2,1)S(1)} %get-tuple-element.71), channel_id=1, source_target_pairs={{0,17},{1,16},{2,19},{3,18},{4,21},{5,20},{6,23},{7,22},{8,25},{9,... | collective-permute-start | bytes 98312 | tf_op jit(solution)/shard_map/ppermute | solution.py:215
  31.9 7.6 %collective-permute-start.14 = (bf16[1024,128]{1,0:T(8,128)(2,1)S(1)}, bf16[1024,128]{1,0:T(8,128)(2,1)S(1)}, u32[]{:S(2)}, u32[]{:S(2)}) collective-permute-start(bf16[1024,128]{1,0:T(8,128)(2,1)S(1)} %get-tuple-element.84), channel_id=1, source_target_pairs={{0,2},{1,3},{2,0},{3,1},{4,6},{5,7},{6,4},{7,5},{8,10},{9,11},{10,... | collective-permute-start | bytes 786440 | tf_op jit(solution)/shard_map/ppermute | solution.py:192
  35.3 4.3 %collective-permute-start.15 = (bf16[1024,128]{1,0:T(8,128)(2,1)S(1)}, bf16[1024,128]{1,0:T(8,128)(2,1)S(1)}, u32[]{:S(2)}, u32[]{:S(2)}) collective-permute-start(bf16[1024,128]{1,0:T(8,128)(2,1)S(1)} %get-tuple-element.85), channel_id=1, source_target_pairs={{0,8},{1,9},{2,4},{3,5},{4,2},{5,3},{6,14},{7,15},{8,0},{9,1},{10,... | collective-permute-start | bytes 786440 | tf_op jit(solution)/shard_map/ppermute | solution.py:192
  37.8 6.0 %collective-permute-start.13 = (bf16[2,128,256]{2,1,0:T(8,128)(2,1)S(1)}, bf16[2,128,256]{2,1,0:T(8,128)(2,1)S(1)}, u32[]{:S(2)}, u32[]{:S(2)}) collective-permute-start(bf16[2,128,256]{2,1,0:T(8,128)(2,1)S(1)} %regroup_resid.1), channel_id=1, source_target_pairs={{0,16},{1,17},{2,18},{3,19},{4,20},{5,21},{6,22},{7,23},{8,24},{9,... | collective-permute-start | bytes 393224 | tf_op jit(solution)/shard_map/ppermute | solution.py:215
  39.7 6.5 %collective-permute-start.16 = (bf16[768,128]{1,0:T(8,128)(2,1)S(1)}, bf16[768,128]{1,0:T(8,128)(2,1)S(1)}, u32[]{:S(2)}, u32[]{:S(2)}) collective-permute-start(bf16[768,128]{1,0:T(8,128)(2,1)S(1)} %get-tuple-element.87), channel_id=1, source_target_pairs={{0,1},{1,0},{2,3},{3,2},{4,5},{5,4},{6,7},{7,6},{8,9},{9,8},{10,11... | collective-permute-start | bytes 589832 | tf_op jit(solution)/shard_map/ppermute | solution.py:623

commit v8 on v7

--- a/solution.py
+++ b/solution.py
@@ -530,13 +530,22 @@
             def tiles_at(distance):
                 return range((near + distance) * q_tiles, (near + distance + 1) * q_tiles)
 
-            @pl.when(right)
+            z = lax.axis_index("z")
+            partner = jnp.where(right, z + d, z - d)
+            real = jnp.logical_and(partner >= 0, partner < z_count)
+
+            @pl.when(jnp.logical_and(real, right))
             def _():
                 side(tiles_at(d))
 
-            @pl.when(jnp.logical_not(right))
+            @pl.when(jnp.logical_and(real, jnp.logical_not(right)))
             def _():
                 side(tiles_at(-d))
+
+            @pl.when(jnp.logical_not(real))
+            def _():
+                acc[...] = jnp.zeros_like(acc)
+                dq[...] = jnp.zeros_like(dq) if first else dq_in[...]
 
             back_ref[...] = acc[...].astype(BF16)
 

time: 47.5 us -> 47.5 us (level)
  the two profiles are of different devices: /device:TPU:0 before, /device:TPU:16 now
where the time goes in v8:
time: 47.5 us; the launch traced here: 47.4 us
  Pallas kernels  18.5 us (39%)
  waiting for transfers between devices  14.1 us (30%)
  starting transfers between devices  13.9 us (29%)
  between operations  0.81 us (2%)
    pallas_call x13, Pallas kernels, run(): pl.pallas_call(body, out_shape=outs, in_specs=[pl.BlockSpec(memory_space=...  17 us
    ppermute x7, starting transfers between devices, exchange(): lax.ppermute(part, mesh_axes, everyone(target(m)))  8.4 us
    ppermute x4, waiting for transfers between devices, step(): return lax.ppermute(x, mesh_axes, everyone(target))  5.76 us
    ppermute x1, waiting for transfers between devices, y_swap(): return lax.ppermute(x, mesh_axes, everyone(lambda h, z, y: (h, z, 1 - y)))  4.8 us
    ppermute x4, starting transfers between devices, step(): return lax.ppermute(x, mesh_axes, everyone(target))  2.18 us
    ppermute x1, starting transfers between devices, on_device(): lax.ppermute(second, mesh_axes, everyone(inside))  1.58 us
    ppermute x7, waiting for transfers between devices, exchange(): lax.ppermute(part, mesh_axes, everyone(target(m)))  1.52 us
    pallas_call x1, Pallas kernels, on_device(): pl.pallas_call(pack_body, out_shape=pack_outs, in_specs=[raw] * 6, out_sp...  1.47 us
  transfers between devices with their start and end apart: 17, of which 8 were waited for; matrix products, arithmetic and copies ran while one was open for 0% of the time, Pallas kernels for 34%

profile of v8, /device:TPU:16, one launch (start us, length us, event | category | flops | bytes accessed | tf_op | source)
XLA Modules:
  0.0 47.4 jit_solution(4687159588554276168)
XLA Ops:
  0.6 1.5 %pack.1 = (bf16[4,192,128]{2,1,0:T(8,128)(2,1)S(1)}, bf16[1152,128]{1,0:T(8,128)(2,1)S(1)}, bf16[48,1024]{1,0:T(8,128)(2,1)S(1)}, bf16[1,128,1024]{2,1,0:T(8,128...) custom-call(bf16[1,128,512]{2,1,0:T(8,128)(2,1)} %q_hbm.1, bf16[1,128,512]{2,1,0:T(8,128)(2,1)} %k_hbm.1, ...), custom_call_target="tpu_custom_call" | custom-call | tf_op jit(solution)/shard_map/pack/pallas_call | solution.py:161
  2.1 0.1 collective-permute-start
  2.2 1.6 %collective-permute-start.1 = (bf16[48,1024]{1,0:T(8,128)(2,1)S(1)}, bf16[48,1024]{1,0:T(8,128)(2,1)S(1)}, u32[]{:S(2)}, u32[]{:S(2)}) collective-permute-start(bf16[48,1024]{1,0:T(8,128)(2,1)S(1)} %get-tuple-element.51), channel_id=1, source_target_pairs={{0,1},{1,0},{2,3},{3,2},{4,5},{5,4},{6,7},{7,6},{8,16},{9,17},{10,... | collective-permute-start | bytes 294920 | tf_op jit(solution)/shard_map/ppermute | solution.py:260
  3.8 1.1 %collective-permute-start.2 = (bf16[48,1024]{1,0:T(8,128)(2,1)S(1)}, bf16[48,1024]{1,0:T(8,128)(2,1)S(1)}, u32[]{:S(2)}, u32[]{:S(2)}) collective-permute-start(bf16[48,1024]{1,0:T(8,128)(2,1)S(1)} %get-tuple-element.51), channel_id=1, source_target_pairs={{0,8},{1,24},{2,25},{3,26},{4,27},{5,28},{6,29},{7,30},{8,0},{9,11... | collective-permute-start | bytes 294920 | tf_op jit(solution)/shard_map/ppermute | solution.py:261
  4.8 0.0 collective-permute-done.refs_2_.got_ref.refs_3_
  4.9 1.1 %collective-permute-start.3 = (bf16[2,192,128]{2,1,0:T(8,128)(2,1)S(1)}, bf16[2,192,128]{2,1,0:T(8,128)(2,1)S(1)}, u32[]{:S(2)}, u32[]{:S(2)}) collective-permute-start(bf16[2,192,128]{2,1,0:T(8,128)(2,1)S(1)} %get-tuple-element.54), channel_id=1, source_target_pairs={{0,16},{1,17},{2,18},{3,19},{4,20},{5,21},{6,22},{7,23},{8,24},{9,... | collective-permute-start | bytes 294920 | tf_op jit(solution)/shard_map/ppermute | solution.py:215
  6.0 0.9 %collective-permute-start.4 = (bf16[2,192,128]{2,1,0:T(8,128)(2,1)S(1)}, bf16[2,192,128]{2,1,0:T(8,128)(2,1)S(1)}, u32[]{:S(2)}, u32[]{:S(2)}) collective-permute-start(bf16[2,192,128]{2,1,0:T(8,128)(2,1)S(1)} %get-tuple-element.55), channel_id=1, source_target_pairs={{0,1},{1,0},{2,3},{3,2},{4,5},{5,4},{6,7},{7,6},{8,9},{9,8},{10,11... | collective-permute-start | bytes 294920 | tf_op jit(solution)/shard_map/ppermute | solution.py:215
  6.9 1.5 %collective-permute-start.5 = (bf16[2,192,128]{2,1,0:T(8,128)(2,1)S(1)}, bf16[2,192,128]{2,1,0:T(8,128)(2,1)S(1)}, u32[]{:S(2)}, u32[]{:S(2)}) collective-permute-start(bf16[2,192,128]{2,1,0:T(8,128)(2,1)S(1)} %get-tuple-element.56), channel_id=1, source_target_pairs={{0,17},{1,16},{2,19},{3,18},{4,21},{5,20},{6,23},{7,22},{8,25},{9,... | collective-permute-start | bytes 294920 | tf_op jit(solution)/shard_map/ppermute | solution.py:215
  8.4 0.0 collective-permute-done.1.refs_3_
  8.4 1.3 %collective-permute-done.2.refs_4_ = bf16[48,1024]{1,0:T(8,128)(2,1)S(1)} collective-permute-done((bf16[48,1024]{1,0:T(8,128)(2,1)S(1)}, bf16[48,1024]{1,0:T(8,128)(2,1)S(1)}, u32[]{:S(2)}, u32[]{:S(2)}) %collective-permute-start.2) | collective-permute-done | bytes 98336 | tf_op jit(solution)/shard_map/ppermute | solution.py:261
  9.7 2.7 %conv.1.refs_6_ = bf16[128,768]{1,0:T(8,128)(2,1)S(1)} custom-call(bf16[1,128,1024]{2,1,0:T(8,128)(2,1)S(1)} %get-tuple-element.48.refs_0_, bf16[1,128,1024]{2,1,0:T(8,128)(2,1)S(1)} %get-tuple-element.49.refs_1_, bf16[1152,128]{1,0:T(8,128)(2,1)S(1)} %collective-permute-done.refs_2_.got_ref.refs_3_, bf16[48,1024]{1,0:T(8,128)(2,1)S(1)} %collective-permute-done.1.refs_3_, ...), custom_call_target="tpu_custom_call" | custom-call | flops 3000000000 | tf_op jit(solution)/shard_map/conv/pallas_call | solution.py:39
  12.4 0.0 collective-permute-done.3.refs_0_.refs_4_
  12.5 0.0 collective-permute-done.4.refs_1_.refs_5_
  12.5 1.4 %collective-permute-done.5.refs_2_.refs_6_ = bf16[2,192,128]{2,1,0:T(8,128)(2,1)S(1)} collective-permute-done((bf16[2,192,128]{2,1,0:T(8,128)(2,1)S(1)}, bf16[2,192,128]{2,1,0:T(8,128)(2,1)S(1)}, u32[]{:S(2)}, u32[]{:S(2)}) %collective-permute-start.5) | collective-permute-done | bytes 98336 | tf_op jit(solution)/shard_map/ppermute | solution.py:215
  13.9 0.0 copy-start
  13.9 1.3 %collective-permute-start.7 = (bf16[1024,128]{1,0:T(8,128)(2,1)S(1)}, bf16[1024,128]{1,0:T(8,128)(2,1)S(1)}, u32[]{:S(2)}, u32[]{:S(2)}) collective-permute-start(bf16[1024,128]{1,0:T(8,128)(2,1)S(1)} %keys.1.refs_1_), channel_id=1, source_target_pairs={{0,2},{1,3},{2,0},{3,1},{4,6},{5,7},{6,4},{7,5},{8,10},{9,11},{10,... | collective-permute-start | bytes 786440 | tf_op jit(solution)/shard_map/ppermute | solution.py:192
  15.2 0.5 %collective-permute-start.8 = (bf16[1024,128]{1,0:T(8,128)(2,1)S(1)}, bf16[1024,128]{1,0:T(8,128)(2,1)S(1)}, u32[]{:S(2)}, u32[]{:S(2)}) collective-permute-start(bf16[1024,128]{1,0:T(8,128)(2,1)S(1)} %keys.1.refs_1_), channel_id=1, source_target_pairs={{0,8},{1,9},{2,4},{3,5},{4,2},{5,3},{6,14},{7,15},{8,0},{9,1},{10,... | collective-permute-start | bytes 786440 | tf_op jit(solution)/shard_map/ppermute | solution.py:192
  15.7 1.8 %conv_last.1 = (bf16[4,64,128]{2,1,0:T(8,128)(2,1)S(1)}, bf16[4,64,128]{2,1,0:T(8,128)(2,1)S(1)}, bf16[2,128,256]{2,1,0:T(8,128)(2,1)S(1)}, bf16[2,128,256]{2,1,0:T(8,128)(2,1)S(1)}) custom-call(bf16[1,128,1024]{2,1,0:T(8,128)(2,1)S(1)} %get-tuple-element.48.refs_0_, bf16[1,128,1024]{2,1,0:T(8,128)(2,1)S(1)} %get-tuple-element.49.refs_1_, ...), custom_call_target="tpu_custom_call" | custom-call | flops 3000000000 | tf_op jit(solution)/shard_map/conv_last/pallas_call | solution.py:39
  17.6 0.1 collective-permute-start.9
  17.6 0.5 %collective-permute-start.6 = (bf16[2,128,256]{2,1,0:T(8,128)(2,1)S(1)}, bf16[2,128,256]{2,1,0:T(8,128)(2,1)S(1)}, u32[]{:S(2)}, u32[]{:S(2)}) collective-permute-start(bf16[2,128,256]{2,1,0:T(8,128)(2,1)S(1)} %get-tuple-element.64), channel_id=1, source_target_pairs={{0,8},{1,9},{2,10},{3,11},{4,12},{5,13},{6,14},{7,15},{8,0},{9,1},... | collective-permute-start | bytes 393224 | tf_op jit(solution)/shard_map/ppermute | solution.py:185
  18.1 0.7 %collective-permute-done.9.got_ref.refs_1_ = bf16[4,64,128]{2,1,0:T(8,128)(2,1)S(1)} collective-permute-done((bf16[4,64,128]{2,1,0:T(8,128)(2,1)S(1)}, bf16[4,64,128]{2,1,0:T(8,128)(2,1)S(1)}, u32[]{:S(2)}, u32[]{:S(2)}) %collective-permute-start.9) | collective-permute-done | bytes 65568 | tf_op jit(solution)/shard_map/ppermute | solution.py:185
  18.9 0.3 collective-permute-start.10
  19.2 1.3 %collective-permute-start.11 = (bf16[2,64,128]{2,1,0:T(8,128)(2,1)S(1)}, bf16[2,64,128]{2,1,0:T(8,128)(2,1)S(1)}, u32[]{:S(2)}, u32[]{:S(2)}) collective-permute-start(bf16[2,64,128]{2,1,0:T(8,128)(2,1)S(1)} %get-tuple-element.70), channel_id=1, source_target_pairs={{0,1},{1,0},{2,3},{3,2},{4,5},{5,4},{6,7},{7,6},{8,9},{9,8},{10,11... | collective-permute-start | bytes 98312 | tf_op jit(solution)/shard_map/ppermute | solution.py:215
  20.5 1.7 %collective-permute-done.7.refs_7_ = bf16[1024,128]{1,0:T(8,128)(2,1)S(1)} collective-permute-done((bf16[1024,128]{1,0:T(8,128)(2,1)S(1)}, bf16[1024,128]{1,0:T(8,128)(2,1)S(1)}, u32[]{:S(2)}, u32[]{:S(2)}) %collective-permute-start.7) | collective-permute-done | bytes 262176 | tf_op jit(solution)/shard_map/ppermute | solution.py:192
  22.2 2.6 %collective-permute-start.12 = (bf16[2,64,128]{2,1,0:T(8,128)(2,1)S(1)}, bf16[2,64,128]{2,1,0:T(8,128)(2,1)S(1)}, u32[]{:S(2)}, u32[]{:S(2)}) collective-permute-start(bf16[2,64,128]{2,1,0:T(8,128)(2,1)S(1)} %get-tuple-element.71), channel_id=1, source_target_pairs={{0,17},{1,16},{2,19},{3,18},{4,21},{5,20},{6,23},{7,22},{8,25},{9,... | collective-permute-start | bytes 98312 | tf_op jit(solution)/shard_map/ppermute | solution.py:215
  24.8 0.0 collective-permute-done.8.refs_8_
  24.8 0.0 copy-done
  24.8 4.6 %scores.1 = (bf16[4,2304,256]{2,1,0:T(8,128)(2,1)S(1)}, f32[4,1,256]{2,1,0:T(1,128)S(1)}, f32[4,64,256]{2,1,0:T(8,128)S(1)}, bf16[3072,128]{1,0:T(8,128)(2,1)S(1...) custom-call(s32[8]{0:T(128)S(1)} %copy-done, bf16[1024,128]{1,0:T(8,128)(2,1)S(1)} %keys.1.refs_1_, ...), custom_call_target="tpu_custom_call" | custom-call | flops 8999999488 | tf_op jit(solution)/shard_map/scores/pallas_call | solution.py:39
  29.5 0.0 collective-permute-done.10.refs_2_
  29.5 0.0 collective-permute-done.11.refs_3_
  29.5 0.0 collective-permute-done.12.refs_4_
  29.5 1.9 %far.1 = (bf16[1024,128]{1,0:T(8,128)(2,1)S(1)}, f32[4,1,256]{2,1,0:T(1,128)S(1)}, f32[4,64,256]{2,1,0:T(8,128)S(1)}, bf16[1024,128]{1,0:T(8,128)(2,1)S(1)}) custom-call(bf16[4,64,128]{2,1,0:T(8,128)(2,1)S(1)} %get-tuple-element.67.keep_ref.refs_0_, bf16[4,64,128]{2,1,0:T(8,128)(2,1)S(1)} %collective-permute-done.9.got_ref.refs_1_, ...), custom_call_target="tpu_custom_call" | custom-call | flops 2000000000 | tf_op jit(solution)/shard_map/far/pallas_call | solution.py:39
  31.5 0.3 collective-permute-start.14
  31.8 1.6 %far_next.1 = (f32[4,64,256]{2,1,0:T(8,128)S(1)}, bf16[1024,128]{1,0:T(8,128)(2,1)S(1)}) custom-call(bf16[4,2304,256]{2,1,0:T(8,128)(2,1)S(1)} %get-tuple-element.65.refs_5_.refs_0_, f32[4,1,256]{2,1,0:T(1,128)S(1)} %get-tuple-element.66.refs_6_.refs_1_, bf16[3072,128]{1,0:T(8,128)(2,1)S(1)} %get-tuple-element.73.refs_8_.refs_2_.refs_3_, ...), custom_call_target="tpu_custom_call" | custom-call | flops 2000000000 | tf_op jit(solution)/shard_map/far_next/pallas_call | solution.py:39
  33.4 0.1 collective-permute-start.15
  33.4 2.4 %near.1 = (f32[1024,128]{1,0:T(8,128)S(1)}, bf16[256,128]{1,0:T(8,128)(2,1)S(1)}, bf16[256,128]{1,0:T(8,128)(2,1)S(1)}) custom-call(bf16[4,2304,256]{2,1,0:T(8,128)(2,1)S(1)} %get-tuple-element.65.refs_5_.refs_0_, f32[4,1,256]{2,1,0:T(1,128)S(1)} %get-tuple-element.66.refs_6_.refs_1_, f32[4,1,256]{2,1,0:T(1,128)S(1)} %get-tuple-element.76.refs_6_.refs_2_, ...), custom_call_target="tpu_custom_call" | custom-call | flops 4000000000 | tf_op jit(solution)/shard_map/near/pallas_call | solution.py:39
  35.9 0.0 collective-permute-done.6.got_ref.refs_1_
  35.9 0.6 %collective-permute-start.13 = (bf16[2,128,256]{2,1,0:T(8,128)(2,1)S(1)}, bf16[2,128,256]{2,1,0:T(8,128)(2,1)S(1)}, u32[]{:S(2)}, u32[]{:S(2)}) collective-permute-start(bf16[2,128,256]{2,1,0:T(8,128)(2,1)S(1)} %regroup_resid.1), channel_id=1, source_target_pairs={{0,16},{1,17},{2,18},{3,19},{4,20},{5,21},{6,22},{7,23},{8,24},{9,... | collective-permute-start | bytes 393224 | tf_op jit(solution)/shard_map/ppermute | solution.py:215
  36.5 2.1 %collective-permute-done.14.refs_0_ = bf16[1024,128]{1,0:T(8,128)(2,1)S(1)} collective-permute-done((bf16[1024,128]{1,0:T(8,128)(2,1)S(1)}, bf16[1024,128]{1,0:T(8,128)(2,1)S(1)}, u32[]{:S(2)}, u32[]{:S(2)}) %collective-permute-start.14) | collective-permute-done | bytes 262176 | tf_op jit(solution)/shard_map/ppermute | solution.py:192
  38.6 1.9 %collective-permute-done.15.refs_1_ = bf16[1024,128]{1,0:T(8,128)(2,1)S(1)} collective-permute-done((bf16[1024,128]{1,0:T(8,128)(2,1)S(1)}, bf16[1024,128]{1,0:T(8,128)(2,1)S(1)}, u32[]{:S(2)}, u32[]{:S(2)}) %collective-permute-start.15) | collective-permute-done | bytes 262176 | tf_op jit(solution)/shard_map/ppermute | solution.py:192
  40.6 0.2 sum.1
  40.7 0.1 collective-permute-start.16
  40.8 0.1 collective-permute-done.13.refs_2_
  40.9 0.7 %resid.1 = bf16[1,512,256]{2,1,0:T(8,128)(2,1)} custom-call(bf16[2,128,256]{2,1,0:T(8,128)(2,1)S(1)} %get-tuple-element.81.keep_ref.refs_0_, bf16[2,128,256]{2,1,0:T(8,128)(2,1)S(1)} %collective-permute-done.6.got_ref.refs_1_, bf16[2,128,256]{2,1,0:T(8,128)(2,1)S(1)} %collective-permute-done.13.refs_2_), custom_call_target="tpu_custom_call" | custom-call | flops 1000000000 | tf_op jit(solution)/shard_map/resid/pallas_call | solution.py:39
  41.7 4.8 %collective-permute-done.16.refs_1_ = bf16[768,128]{1,0:T(8,128)(2,1)S(1)} collective-permute-done((bf16[768,128]{1,0:T(8,128)(2,1)S(1)}, bf16[768,128]{1,0:T(8,128)(2,1)S(1)}, u32[]{:S(2)}, u32[]{:S(2)}) %collective-permute-start.16) | collective-permute-done | bytes 196640 | tf_op jit(solution)/shard_map/ppermute | solution.py:632
  46.5 0.9 %last.1 = (bf16[1,512,128]{2,1,0:T(8,128)(2,1)}, bf16[1,512,128]{2,1,0:T(8,128)(2,1)}, bf16[1,512,128]{2,1,0:T(8,128)(2,1)}) custom-call(bf16[512,128]{1,0:T(8,128)(2,1)S(1)} %get-tuple-element.86.refs_0_, bf16[768,128]{1,0:T(8,128)(2,1)S(1)} %collective-permute-done.16.refs_1_, bf16[256,128]{1,0:T(8,128)(2,1)S(1)} %get-tuple-element.88.refs_2_), custom_call_target="tpu_custom_call" | custom-call | tf_op jit(solution)/shard_map/last/pallas_call | solution.py:39
  (4 shorter events, 0.1 us)
Async XLA Ops:
  2.1 2.7 %collective-permute-start = (bf16[1152,128]{1,0:T(8,128)(2,1)S(1)}, bf16[1152,128]{1,0:T(8,128)(2,1)S(1)}, u32[]{:S(2)}, u32[]{:S(2)}) collective-permute-start(bf16[1152,128]{1,0:T(8,128)(2,1)S(1)} %get-tuple-element.50), channel_id=1, source_target_pairs={{0,8},{1,9},{2,10},{3,11},{4,12},{5,13},{6,14},{7,15},{8,0},{9,1},... | collective-permute-start | bytes 884744 | tf_op jit(solution)/shard_map/ppermute | solution.py:185
  2.2 6.2 %collective-permute-start.1 = (bf16[48,1024]{1,0:T(8,128)(2,1)S(1)}, bf16[48,1024]{1,0:T(8,128)(2,1)S(1)}, u32[]{:S(2)}, u32[]{:S(2)}) collective-permute-start(bf16[48,1024]{1,0:T(8,128)(2,1)S(1)} %get-tuple-element.51), channel_id=1, source_target_pairs={{0,1},{1,0},{2,3},{3,2},{4,5},{5,4},{6,7},{7,6},{8,16},{9,17},{10,... | collective-permute-start | bytes 294920 | tf_op jit(solution)/shard_map/ppermute | solution.py:260
  3.8 5.9 %collective-permute-start.2 = (bf16[48,1024]{1,0:T(8,128)(2,1)S(1)}, bf16[48,1024]{1,0:T(8,128)(2,1)S(1)}, u32[]{:S(2)}, u32[]{:S(2)}) collective-permute-start(bf16[48,1024]{1,0:T(8,128)(2,1)S(1)} %get-tuple-element.51), channel_id=1, source_target_pairs={{0,8},{1,24},{2,25},{3,26},{4,27},{5,28},{6,29},{7,30},{8,0},{9,11... | collective-permute-start | bytes 294920 | tf_op jit(solution)/shard_map/ppermute | solution.py:261
  4.9 7.6 %collective-permute-start.3 = (bf16[2,192,128]{2,1,0:T(8,128)(2,1)S(1)}, bf16[2,192,128]{2,1,0:T(8,128)(2,1)S(1)}, u32[]{:S(2)}, u32[]{:S(2)}) collective-permute-start(bf16[2,192,128]{2,1,0:T(8,128)(2,1)S(1)} %get-tuple-element.54), channel_id=1, source_target_pairs={{0,16},{1,17},{2,18},{3,19},{4,20},{5,21},{6,22},{7,23},{8,24},{9,... | collective-permute-start | bytes 294920 | tf_op jit(solution)/shard_map/ppermute | solution.py:215
  6.0 6.5 %collective-permute-start.4 = (bf16[2,192,128]{2,1,0:T(8,128)(2,1)S(1)}, bf16[2,192,128]{2,1,0:T(8,128)(2,1)S(1)}, u32[]{:S(2)}, u32[]{:S(2)}) collective-permute-start(bf16[2,192,128]{2,1,0:T(8,128)(2,1)S(1)} %get-tuple-element.55), channel_id=1, source_target_pairs={{0,1},{1,0},{2,3},{3,2},{4,5},{5,4},{6,7},{7,6},{8,9},{9,8},{10,11... | collective-permute-start | bytes 294920 | tf_op jit(solution)/shard_map/ppermute | solution.py:215
  6.9 6.9 %collective-permute-start.5 = (bf16[2,192,128]{2,1,0:T(8,128)(2,1)S(1)}, bf16[2,192,128]{2,1,0:T(8,128)(2,1)S(1)}, u32[]{:S(2)}, u32[]{:S(2)}) collective-permute-start(bf16[2,192,128]{2,1,0:T(8,128)(2,1)S(1)} %get-tuple-element.56), channel_id=1, source_target_pairs={{0,17},{1,16},{2,19},{3,18},{4,21},{5,20},{6,23},{7,22},{8,25},{9,... | collective-permute-start | bytes 294920 | tf_op jit(solution)/shard_map/ppermute | solution.py:215
  13.9 10.9 %copy-start = (s32[8]{0:T(128)S(1)}, s32[8]{0:T(128)}, u32[]{:S(2)}) copy-start(s32[8]{0:T(128)} %refs_0_.1) | copy-start | bytes 100
  13.9 8.3 %collective-permute-start.7 = (bf16[1024,128]{1,0:T(8,128)(2,1)S(1)}, bf16[1024,128]{1,0:T(8,128)(2,1)S(1)}, u32[]{:S(2)}, u32[]{:S(2)}) collective-permute-start(bf16[1024,128]{1,0:T(8,128)(2,1)S(1)} %keys.1.refs_1_), channel_id=1, source_target_pairs={{0,2},{1,3},{2,0},{3,1},{4,6},{5,7},{6,4},{7,5},{8,10},{9,11},{10,... | collective-permute-start | bytes 786440 | tf_op jit(solution)/shard_map/ppermute | solution.py:192
  15.2 9.6 %collective-permute-start.8 = (bf16[1024,128]{1,0:T(8,128)(2,1)S(1)}, bf16[1024,128]{1,0:T(8,128)(2,1)S(1)}, u32[]{:S(2)}, u32[]{:S(2)}) collective-permute-start(bf16[1024,128]{1,0:T(8,128)(2,1)S(1)} %keys.1.refs_1_), channel_id=1, source_target_pairs={{0,8},{1,9},{2,4},{3,5},{4,2},{5,3},{6,14},{7,15},{8,0},{9,1},{10,... | collective-permute-start | bytes 786440 | tf_op jit(solution)/shard_map/ppermute | solution.py:192
  17.6 1.3 %collective-permute-start.9 = (bf16[4,64,128]{2,1,0:T(8,128)(2,1)S(1)}, bf16[4,64,128]{2,1,0:T(8,128)(2,1)S(1)}, u32[]{:S(2)}, u32[]{:S(2)}) collective-permute-start(bf16[4,64,128]{2,1,0:T(8,128)(2,1)S(1)} %get-tuple-element.68), channel_id=1, source_target_pairs={{0,8},{1,9},{2,10},{3,11},{4,12},{5,13},{6,14},{7,15},{8,0},{9,1},... | collective-permute-start | bytes 196616 | tf_op jit(solution)/shard_map/ppermute | solution.py:185
  17.6 18.2 %collective-permute-start.6 = (bf16[2,128,256]{2,1,0:T(8,128)(2,1)S(1)}, bf16[2,128,256]{2,1,0:T(8,128)(2,1)S(1)}, u32[]{:S(2)}, u32[]{:S(2)}) collective-permute-start(bf16[2,128,256]{2,1,0:T(8,128)(2,1)S(1)} %get-tuple-element.64), channel_id=1, source_target_pairs={{0,8},{1,9},{2,10},{3,11},{4,12},{5,13},{6,14},{7,15},{8,0},{9,1},... | collective-permute-start | bytes 393224 | tf_op jit(solution)/shard_map/ppermute | solution.py:185
  18.9 10.6 %collective-permute-start.10 = (bf16[2,64,128]{2,1,0:T(8,128)(2,1)S(1)}, bf16[2,64,128]{2,1,0:T(8,128)(2,1)S(1)}, u32[]{:S(2)}, u32[]{:S(2)}) collective-permute-start(bf16[2,64,128]{2,1,0:T(8,128)(2,1)S(1)} %get-tuple-element.69), channel_id=1, source_target_pairs={{0,16},{1,17},{2,18},{3,19},{4,20},{5,21},{6,22},{7,23},{8,24},{9,... | collective-permute-start | bytes 98312 | tf_op jit(solution)/shard_map/ppermute | solution.py:215
  19.2 10.3 %collective-permute-start.11 = (bf16[2,64,128]{2,1,0:T(8,128)(2,1)S(1)}, bf16[2,64,128]{2,1,0:T(8,128)(2,1)S(1)}, u32[]{:S(2)}, u32[]{:S(2)}) collective-permute-start(bf16[2,64,128]{2,1,0:T(8,128)(2,1)S(1)} %get-tuple-element.70), channel_id=1, source_target_pairs={{0,1},{1,0},{2,3},{3,2},{4,5},{5,4},{6,7},{7,6},{8,9},{9,8},{10,11... | collective-permute-start | bytes 98312 | tf_op jit(solution)/shard_map/ppermute | solution.py:215
  22.2 7.3 %collective-permute-start.12 = (bf16[2,64,128]{2,1,0:T(8,128)(2,1)S(1)}, bf16[2,64,128]{2,1,0:T(8,128)(2,1)S(1)}, u32[]{:S(2)}, u32[]{:S(2)}) collective-permute-start(bf16[2,64,128]{2,1,0:T(8,128)(2,1)S(1)} %get-tuple-element.71), channel_id=1, source_target_pairs={{0,17},{1,16},{2,19},{3,18},{4,21},{5,20},{6,23},{7,22},{8,25},{9,... | collective-permute-start | bytes 98312 | tf_op jit(solution)/shard_map/ppermute | solution.py:215
  31.5 7.2 %collective-permute-start.14 = (bf16[1024,128]{1,0:T(8,128)(2,1)S(1)}, bf16[1024,128]{1,0:T(8,128)(2,1)S(1)}, u32[]{:S(2)}, u32[]{:S(2)}) collective-permute-start(bf16[1024,128]{1,0:T(8,128)(2,1)S(1)} %get-tuple-element.84), channel_id=1, source_target_pairs={{0,2},{1,3},{2,0},{3,1},{4,6},{5,7},{6,4},{7,5},{8,10},{9,11},{10,... | collective-permute-start | bytes 786440 | tf_op jit(solution)/shard_map/ppermute | solution.py:192
  33.4 7.2 %collective-permute-start.15 = (bf16[1024,128]{1,0:T(8,128)(2,1)S(1)}, bf16[1024,128]{1,0:T(8,128)(2,1)S(1)}, u32[]{:S(2)}, u32[]{:S(2)}) collective-permute-start(bf16[1024,128]{1,0:T(8,128)(2,1)S(1)} %get-tuple-element.85), channel_id=1, source_target_pairs={{0,8},{1,9},{2,4},{3,5},{4,2},{5,3},{6,14},{7,15},{8,0},{9,1},{10,... | collective-permute-start | bytes 786440 | tf_op jit(solution)/shard_map/ppermute | solution.py:192
  35.9 5.0 %collective-permute-start.13 = (bf16[2,128,256]{2,1,0:T(8,128)(2,1)S(1)}, bf16[2,128,256]{2,1,0:T(8,128)(2,1)S(1)}, u32[]{:S(2)}, u32[]{:S(2)}) collective-permute-start(bf16[2,128,256]{2,1,0:T(8,128)(2,1)S(1)} %regroup_resid.1), channel_id=1, source_target_pairs={{0,16},{1,17},{2,18},{3,19},{4,20},{5,21},{6,22},{7,23},{8,24},{9,... | collective-permute-start | bytes 393224 | tf_op jit(solution)/shard_map/ppermute | solution.py:215
  40.7 5.7 %collective-permute-start.16 = (bf16[768,128]{1,0:T(8,128)(2,1)S(1)}, bf16[768,128]{1,0:T(8,128)(2,1)S(1)}, u32[]{:S(2)}, u32[]{:S(2)}) collective-permute-start(bf16[768,128]{1,0:T(8,128)(2,1)S(1)} %get-tuple-element.87), channel_id=1, source_target_pairs={{0,1},{1,0},{2,3},{3,2},{4,5},{5,4},{6,7},{7,6},{8,9},{9,8},{10,11... | collective-permute-start | bytes 589832 | tf_op jit(solution)/shard_map/ppermute | solution.py:632
